TPU v7x, 512 devices: a whole 4x8x8 slice. The times are simulated.
512 devices in a mesh: tp: 8 (over z), ep: 64 (over y, x, core).
Axes of the slice: x: 4, y: 8, z: 8, core: 2. Of those that a mesh axis runs over, the one named last changes fastest.
Arguments:
- attn: bfloat16 [32768, 1536], P('ep', 'tp'), may hold values from -6 to 6
- resid: bfloat16 [32768, 1536], P('ep', 'tp'), may hold values from -6 to 6
- w_out: bfloat16 [1536, 1536], P('tp', 'ep'), may hold values from -0.15625 to 0.15625
- gain_mix: float32 [1536], replicated, may hold values from 0.1 to 1.9
- gain_out: float32 [1536], replicated, may hold values from 0.1 to 1.9
- routes: int32 [32768, 8], P('ep'), may hold values from 0 to 39, all different within a row; in each aligned block of 64 rows (0 to 63, 64 to 127, ...) at most 16 rows name the same one
- gates: float32 [32768, 8], P('ep'), may hold values from 0.05 to 1
- w_gate: bfloat16 [64, 1536, 512], P('ep'), as said below
- w_up: bfloat16 [64, 1536, 512], P('ep'), as said below
- w_down: bfloat16 [64, 512, 1536], P('ep'), as said below
Outputs:
- layer_out: bfloat16 [32768, 1536], P('ep', 'tp')
Inputs may be any that keep to these rules, and one draw needn't show every extreme that they name: `routes`: in each aligned block of 64 rows no expert is named more than 16 times; each row names 8 different experts. `w_gate`: copy s holds the weights of expert s % 40. `w_up`: copy s holds the weights of expert s % 40. `w_down`: copy s holds the weights of expert s % 40.
All inputs are finite; a program needn't handle non-finite values.
Results may differ from a plain program's by a relative error of at most 0.0053.
Values may be sent and summed in bfloat16 or wider, within the bound.
No kernel may reach another device: no remote copies, remote signals or barrier semaphores. Data moves between devices by JAX's collectives and lax.ppermute only.
A program may use at most 64 MiB of HBM per device.

v0:
```python
import jax
import jax.numpy as jnp
from jax import lax
from jax.experimental import pallas as pl
from jax.experimental.pallas import tpu as pltpu
from jax.sharding import Mesh, PartitionSpec as P

EXPERTS = 40
CAP = 16
EPS = 1e-05
BF = jnp.bfloat16
F32 = jnp.float32
EP = ("h", "y", "x", "c")
VMEM = 56 * 1024 * 1024


def params():
    return pltpu.CompilerParams(vmem_limit_bytes=VMEM)


def dot(a, b, ca, cb):
    return lax.dot_general(a, b, (((ca,), (cb,)), ((), ())), preferred_element_type=F32)


def project_kernel(place_ref, attn_ref, resid_ref, w_ref, out_ref):
    tp = place_ref[4]
    weights = w_ref[...].reshape(1536, 192)
    at = lax.broadcasted_iota(jnp.int32, (1536, 192), 0)
    of = lax.broadcasted_iota(jnp.int32, (1536, 192), 1)
    choose = jnp.where(at == of + tp * 192, 1.0, 0.0).astype(BF)
    part = dot(attn_ref[...].T, weights, 1, 1) + dot(resid_ref[...].T, choose, 1, 1)
    out_ref[...] = part.astype(BF).reshape(8, 64, 1536)


def piece_kernel(place_ref, wg_ref, wu_ref, wd_ref, out_ref):
    out_ref[0:192, :] = wg_ref[0]
    out_ref[192:384, :] = wu_ref[0]
    for i in range(3):
        out_ref[384 + i * 64 : 448 + i * 64, :] = wd_ref[0, :, i * 512 : (i + 1) * 512]


def one_hot_rows(routed, expert, rank_of):
    hits = jnp.zeros((routed.shape[0], expert.shape[1]), F32)
    for k in range(8):
        hits = hits + jnp.where(routed[:, k : k + 1] == expert, 1.0, 0.0)
    ranks = dot(rank_of, hits.astype(BF), 1, 0)
    return hits, ranks


def before_matrix(rows):
    a = lax.broadcasted_iota(jnp.int32, (rows, rows), 0)
    b = lax.broadcasted_iota(jnp.int32, (rows, rows), 1)
    keep = (b < a) & (a // 64 == b // 64)
    return jnp.where(keep, 1.0, 0.0).astype(BF)


def lane_experts(place_ref, lane):
    half, me = place_ref[3], place_ref[5]
    slot = lane // CAP
    near = (32 * half + slot) % EXPERTS
    far = 32 - 8 * half + (me + slot) % 8
    return jnp.where(slot < 32, near, far).astype(F32)


def mix_kernel(place_ref, part_ref, routes_ref, gain_ref, send_ref, hid_ref, *far_refs):
    hidden = part_ref[0].astype(F32)
    for z in range(1, 8):
        hidden = hidden + part_ref[z].astype(F32)
    hid_ref[...] = hidden
    mean = jnp.sum(hidden * hidden, axis=1, keepdims=True) / 1536
    normed = (hidden * lax.rsqrt(mean + EPS) * gain_ref[...]).astype(BF)
    lane = lax.broadcasted_iota(jnp.int32, (1, 640), 1)
    hits, ranks = one_hot_rows(routes_ref[...].astype(F32), lane_experts(place_ref, lane), before_matrix(64))
    pick = jnp.where(ranks == (lane % CAP).astype(F32), hits, 0.0).astype(BF)
    far = dot(pick[:, 512:640], normed, 0, 0).astype(BF)
    for k in range(8):
        far_refs[k][...] = far[k * CAP : (k + 1) * CAP]
    send_ref[...] = dot(pick[:, 0:512], normed, 0, 0).astype(BF).reshape(32, CAP, 1536)


def expert(x, w_gate, w_up, w_down):
    gate = dot(x, w_gate, 1, 0)
    up = dot(x, w_up, 1, 0)
    act = (gate / (1.0 + jnp.exp(-gate)) * up).astype(BF)
    return dot(act, w_down, 1, 0).astype(BF)


def near_kernel(x_ref, wg_ref, wu_ref, wd_ref, out_ref):
    y = expert(x_ref[...].reshape(256, 1536), wg_ref[0], wu_ref[0], wd_ref[0])
    out_ref[...] = y.reshape(16, CAP, 1536)


def far_kernel(*refs):
    x_refs, w_ref, out_refs, (wg_scr, wu_scr, wd_scr) = refs[0:8], refs[8], refs[9:17], refs[17:]
    for z in range(8):
        wg_scr[z * 192 : (z + 1) * 192, :] = w_ref[z, 0:192, :]
        wu_scr[z * 192 : (z + 1) * 192, :] = w_ref[z, 192:384, :]
        for i in range(3):
            wd_scr[z * 64 : (z + 1) * 64, i * 512 : (i + 1) * 512] = w_ref[z, 384 + i * 64 : 448 + i * 64, :]
    x = jnp.concatenate([ref[...] for ref in x_refs], axis=0)
    y = expert(x, wg_scr[...], wu_scr[...], wd_scr[...])
    for k in range(8):
        out_refs[k][...] = y[k * CAP : (k + 1) * CAP]


def close_kernel(place_ref, routes_ref, gates_ref, hid_ref, gain_ref, near_ref, *refs):
    far_refs, out_ref = refs[0:8], refs[8]
    lane = lax.broadcasted_iota(jnp.int32, (1, 640), 1)
    expert_of = lane_experts(place_ref, lane)
    routed = routes_ref[...].astype(F32)
    hits, ranks = one_hot_rows(routed, expert_of, before_matrix(64))
    gate = jnp.zeros((64, 640), F32)
    for k in range(8):
        gate = gate + jnp.where(routed[:, k : k + 1] == expert_of, gates_ref[:, k : k + 1], 0.0)
    gate = jnp.where((ranks == (lane % CAP).astype(F32)) & (hits > 0.5), gate, 0.0)
    high = gate.astype(BF)
    low = (gate - high.astype(F32)).astype(BF)
    both = jnp.concatenate([high, low], axis=0)
    far = jnp.concatenate([ref[...] for ref in far_refs], axis=0)
    total = dot(both[:, 0:512], near_ref[...].reshape(512, 1536), 1, 0) + dot(both[:, 512:640], far, 1, 0)
    combined = hid_ref[...] + (total[0:64] + total[64:128])
    mean = jnp.sum(combined * combined, axis=1, keepdims=True) / 1536
    out = (combined * lax.rsqrt(mean + EPS) * gain_ref[...]).astype(BF)
    for z in range(8):
        out_ref[z] = out[:, z * 192 : (z + 1) * 192]


def smem():
    return pl.BlockSpec(memory_space=pltpu.SMEM)


def vmem():
    return pl.BlockSpec(memory_space=pltpu.VMEM)


def per_device(attn, resid, w_out, gain_mix, gain_out, routes, gates, w_gate, w_up, w_down):
    tp, h, y = lax.axis_index("tp"), lax.axis_index("h"), lax.axis_index("y")
    core, me = lax.axis_index("c"), lax.axis_index(("x", "c"))
    place = jnp.stack([core, h * 4 + y, y, h, tp, me])
    shape = jax.ShapeDtypeStruct
    my_routes = lax.dynamic_slice_in_dim(routes, tp * 64, 64, 0)
    my_gates = lax.dynamic_slice_in_dim(gates, tp * 64, 64, 0)

    piece = pl.pallas_call(
        piece_kernel,
        grid_spec=pltpu.PrefetchScalarGridSpec(
            num_scalar_prefetch=1,
            grid=(1,),
            in_specs=[
                pl.BlockSpec((1, 192, 512), lambda i, p: (0, p[4], 0)),
                pl.BlockSpec((1, 192, 512), lambda i, p: (0, p[4], 0)),
                pl.BlockSpec((1, 64, 1536), lambda i, p: (0, p[4], 0)),
            ],
            out_specs=pl.BlockSpec((576, 512), lambda i, p: (0, 0)),
        ),
        out_shape=shape((576, 512), BF),
        compiler_params=params(),
        name="piece",
    )(place, w_gate, w_up, w_down)
    crossed = lax.ppermute(piece, ("h", "y"), [(4, 3), (3, 4)])
    columns = lax.all_to_all(jnp.broadcast_to(w_out.T[None], (64, 24, 192)), EP, 0, 0, tiled=True)
    crossed, _ = lax.optimization_barrier((crossed, columns))
    pieces = lax.all_gather(crossed, "y", axis=0, tiled=False)

    parts = pl.pallas_call(
        project_kernel,
        out_shape=shape((8, 64, 1536), BF),
        in_specs=[smem()] + [vmem()] * 3,
        out_specs=vmem(),
        compiler_params=params(),
        name="project",
    )(place, attn.T, resid.T, columns)
    parts = lax.all_to_all(parts, "tp", 0, 0, tiled=True)
    rows = shape((CAP, 1536), BF)
    send, hidden, *far = pl.pallas_call(
        mix_kernel,
        out_shape=(shape((32, CAP, 1536), BF), shape((64, 1536), F32)) + (rows,) * 8,
        in_specs=[smem()] + [vmem()] * 3,
        out_specs=(vmem(),) * 10,
        compiler_params=params(),
        name="mix",
    )(place, parts, my_routes, gain_mix.reshape(1, 1536))

    pieces, _ = lax.optimization_barrier((pieces, send))
    far_piece = lax.dynamic_index_in_dim(pieces, 3 - 3 * h, 0, keepdims=False)
    far_weights = lax.all_gather(far_piece, "tp", axis=0, tiled=False)

    shift = lambda v, k: lax.ppermute(v, ("x", "c"), [(i, (i + k) % 8) for i in range(8)])
    far = far[0:1] + [shift(far[k], k) for k in range(1, 8)]
    received = lax.all_to_all(send, ("y", "x", "c"), 0, 0, tiled=True)
    received, far = lax.optimization_barrier((received, far))

    whole = lambda *dims: pl.BlockSpec(dims, lambda i: (0,) * len(dims))
    near = pl.pallas_call(
        near_kernel,
        grid=(2,),
        out_shape=shape((32, CAP, 1536), BF),
        in_specs=[
            pl.BlockSpec((16, CAP, 1536), lambda i: (i, 0, 0)),
            whole(1, 1536, 512),
            whole(1, 1536, 512),
            whole(1, 512, 1536),
        ],
        out_specs=pl.BlockSpec((16, CAP, 1536), lambda i: (i, 0, 0)),
        compiler_params=params(),
        name="near",
    )(received, w_gate, w_up, w_down)
    far = pl.pallas_call(
        far_kernel,
        out_shape=(rows,) * 8,
        in_specs=[vmem()] * 9,
        out_specs=(vmem(),) * 8,
        scratch_shapes=[pltpu.VMEM((1536, 512), BF), pltpu.VMEM((1536, 512), BF), pltpu.VMEM((512, 1536), BF)],
        compiler_params=params(),
        name="far",
    )(*far, far_weights)
    near = lax.all_to_all(near, ("y", "x", "c"), 0, 0, tiled=True)
    far = [far[0]] + [shift(far[k], 8 - k) for k in range(1, 8)]

    finished = pl.pallas_call(
        close_kernel,
        out_shape=shape((8, 64, 192), BF),
        in_specs=[smem()] + [vmem()] * 13,
        out_specs=vmem(),
        compiler_params=params(),
        name="close",
    )(place, my_routes, my_gates, hidden, gain_out.reshape(1, 1536), near, *far)
    return lax.all_to_all(finished, "tp", 0, 0, tiled=True).reshape(512, 192)


def solution(mesh):
    fine = Mesh(mesh.devices.reshape(8, 2, 4, 4, 2), ("tp",) + EP)
    return jax.shard_map(
        per_device,
        mesh=fine,
        in_specs=(
            P(EP, "tp"),
            P(EP, "tp"),
            P("tp", EP),
            P(),
            P(),
            P(EP, None),
            P(EP, None),
            P(EP, None, None),
            P(EP, None, None),
            P(EP, None, None),
        ),
        out_specs=P(EP, "tp"),
        check_vma=False,
    )
```

profile of v0, /device:TPU:57, one launch (start us, length us, event | category | flops | bytes accessed | tf_op | source)
XLA Modules:
  0.0 241.1 jit_solution(8567739073413389499)
XLA Ops:
  8.2 10.5 %all-to-all-start = ((bf16[64,24,192]{2,1,0:T(8,128)(2,1)}), bf16[64,24,192]{2,1,0:T(8,128)(2,1)S(1)}, u32[]{:S(2)}, u32[]{:S(2)}) async-start(bf16[64,24,192]{2,1,0:T(8,128)(2,1)} %broadcast_in_dim.2), calls=%async_computation | async-start | bytes 1572864 | tf_op jit(solution)/shard_map/all_to_all | solution.py:161
  19.4 2.6 %piece.1 = bf16[576,512]{1,0:T(8,128)(2,1)} custom-call(s32[6]{0:T(128)} %stack.27.place_ref, bf16[1,1536,512]{2,1,0:T(8,128)(2,1)} %wg_ref.3, bf16[1,1536,512]{2,1,0:T(8,128)(2,1)} %wu_ref.3, bf16[1,512,1536]{2,1,0:T(8,128)(2,1)} %wd_ref.3), custom_call_target="tpu_custom_call" | custom-call | tf_op jit(solution)/shard_map/piece/pallas_call | solution.py:144
  22.8 17.6 %all-to-all-done.w_ref = bf16[64,24,192]{2,1,0:T(8,128)(2,1)S(1)} async-done(((bf16[64,24,192]{2,1,0:T(8,128)(2,1)}), bf16[64,24,192]{2,1,0:T(8,128)(2,1)S(1)}, u32[]{:S(2)}, u32[]{:S(2)}) %all-to-all-start) | async-done | bytes 589856 | tf_op jit(solution)/shard_map/all_to_all | solution.py:161
  41.3 3.5 %project.1 = bf16[8,64,1536]{2,1,0:T(8,128)(2,1)} custom-call(s32[6]{0:T(128)} %stack.27.place_ref, bf16[192,512]{1,0:T(8,128)(2,1)} %bitcast.12, bf16[192,512]{1,0:T(8,128)(2,1)} %bitcast.13, bf16[64,24,192]{2,1,0:T(8,128)(2,1)} %copy-done.4), custom_call_target="tpu_custom_call" | custom-call | tf_op jit(solution)/shard_map/project/pallas_call | solution.py:165
  44.8 10.2 %all-to-all-start.1 = ((bf16[8,64,1536]{2,1,0:T(8,128)(2,1)}), bf16[8,64,1536]{2,1,0:T(8,128)(2,1)S(1)}, u32[]{:S(2)}, u32[]{:S(2)}) async-start(bf16[8,64,1536]{2,1,0:T(8,128)(2,1)} %project.1), calls=%async_computation.1 | async-start | bytes 3145728 | tf_op jit(solution)/shard_map/all_to_all | solution.py:173
  56.4 36.8 %all-to-all-done.1.part_ref = bf16[8,64,1536]{2,1,0:T(8,128)(2,1)S(1)} async-done(((bf16[8,64,1536]{2,1,0:T(8,128)(2,1)}), bf16[8,64,1536]{2,1,0:T(8,128)(2,1)S(1)}, u32[]{:S(2)}, u32[]{:S(2)}) %all-to-all-start.1) | async-done | bytes 1572896 | tf_op jit(solution)/shard_map/all_to_all | solution.py:173
  94.4 3.8 %mix.1 = (bf16[32,16,1536]{2,1,0:T(8,128)(2,1)}, f32[64,1536]{1,0:T(8,128)}, bf16[16,1536]{1,0:T(8,128)(2,1)}, bf16[16,1536]{1,0:T(8,128)(2,1)}, bf16[16,1536]{1...) custom-call(s32[6]{0:T(128)} %stack.27.place_ref, ...), custom_call_target="tpu_custom_call" | custom-call | tf_op jit(solution)/shard_map/mix/pallas_call | solution.py:175
  98.2 14.5 %all-gather.6.cloned.1.call-done = bf16[2304,512]{1,0:T(8,128)(2,1)} async-done(((bf16[576,512]{1,0:T(8,128)(2,1)}), bf16[2304,512]{1,0:T(8,128)(2,1)}) %all-gather.6.cloned.1.call-update) | async-done | bytes 2359312 | tf_op jit(solution)/shard_map/all_gather | solution.py:163
  114.8 8.2 %all-to-all-start.2 = ((bf16[32,16,1536]{2,1,0:T(8,128)(2,1)}), bf16[32,16,1536]{2,1,0:T(8,128)(2,1)S(1)}, u32[]{:S(2)}, u32[]{:S(2)}) async-start(bf16[32,16,1536]{2,1,0:T(8,128)(2,1)} %get-tuple-element.35), calls=%async_computation.2 | async-start | bytes 3145728 | tf_op jit(solution)/shard_map/all_to_all | solution.py:190
  124.4 3.1 %collective-permute-start.1 = (bf16[16,1536]{1,0:T(8,128)(2,1)S(1)}, bf16[16,1536]{1,0:T(8,128)(2,1)S(1)}, u32[]{:S(2)}, u32[]{:S(2)}) collective-permute-start(bf16[16,1536]{1,0:T(8,128)(2,1)S(1)} %copy-done.27), channel_id=1, source_target_pairs={{0,2},{1,3},{2,4},{3,5},{4,6},{5,7},{6,0},{7,1},{8,10},{9,11},{10,... | collective-permute-start | bytes 147464 | tf_op jit(solution)/shard_map/ppermute | solution.py:188
  127.5 3.6 %collective-permute-start.2 = (bf16[16,1536]{1,0:T(8,128)(2,1)S(1)}, bf16[16,1536]{1,0:T(8,128)(2,1)S(1)}, u32[]{:S(2)}, u32[]{:S(2)}) collective-permute-start(bf16[16,1536]{1,0:T(8,128)(2,1)S(1)} %copy-done.26), channel_id=1, source_target_pairs={{0,3},{1,4},{2,5},{3,6},{4,7},{5,0},{6,1},{7,2},{8,11},{9,12},{10,... | collective-permute-start | bytes 147464 | tf_op jit(solution)/shard_map/ppermute | solution.py:188
  133.6 3.8 %collective-permute-start.4 = (bf16[16,1536]{1,0:T(8,128)(2,1)S(1)}, bf16[16,1536]{1,0:T(8,128)(2,1)S(1)}, u32[]{:S(2)}, u32[]{:S(2)}) collective-permute-start(bf16[16,1536]{1,0:T(8,128)(2,1)S(1)} %copy-done.24), channel_id=1, source_target_pairs={{0,5},{1,6},{2,7},{3,0},{4,1},{5,2},{6,3},{7,4},{8,13},{9,14},{10,... | collective-permute-start | bytes 147464 | tf_op jit(solution)/shard_map/ppermute | solution.py:188
  145.0 13.4 %all-to-all-done.2.x_ref = bf16[32,16,1536]{2,1,0:T(8,128)(2,1)S(1)} async-done(((bf16[32,16,1536]{2,1,0:T(8,128)(2,1)}), bf16[32,16,1536]{2,1,0:T(8,128)(2,1)S(1)}, u32[]{:S(2)}, u32[]{:S(2)}) %all-to-all-start.2) | async-done | bytes 1572896 | tf_op jit(solution)/shard_map/all_to_all | solution.py:190
  159.6 6.5 %near.1 = bf16[32,16,1536]{2,1,0:T(8,128)(2,1)} custom-call(bf16[32,16,1536]{2,1,0:T(8,128)(2,1)} %copy-done.3, bf16[1,1536,512]{2,1,0:T(8,128)(2,1)} %wg_ref.3, bf16[1,1536,512]{2,1,0:T(8,128)(2,1)} %wu_ref.3, bf16[1,512,1536]{2,1,0:T(8,128)(2,1)} %wd_ref.3), custom_call_target="tpu_custom_call" | custom-call | tf_op jit(solution)/shard_map/near/pallas_call | solution.py:194
  166.2 7.7 %all-to-all-start.3 = ((bf16[32,16,1536]{2,1,0:T(8,128)(2,1)}), bf16[32,16,1536]{2,1,0:T(8,128)(2,1)S(1)}, u32[]{:S(2)}, u32[]{:S(2)}) async-start(bf16[32,16,1536]{2,1,0:T(8,128)(2,1)} %near.1), calls=%async_computation.3 | async-start | bytes 3145728 | tf_op jit(solution)/shard_map/all_to_all | solution.py:217
  174.0 2.8 %all-gather.4.cloned.1.call-done.refs_8_ = bf16[8,576,512]{2,1,0:T(8,128)(2,1)} async-done(((bf16[1,576,512]{2,1,0:T(8,128)(2,1)}), bf16[8,576,512]{2,1,0:T(8,128)(2,1)}) %all-gather.4.cloned.1.call-update) | async-done | bytes 4718608 | tf_op jit(solution)/shard_map/all_gather | solution.py:186
  176.7 4.2 %far.1 = (bf16[16,1536]{1,0:T(8,128)(2,1)}, bf16[16,1536]{1,0:T(8,128)(2,1)}, bf16[16,1536]{1,0:T(8,128)(2,1)}, bf16[16,1536]{1,0:T(8,128)(2,1)}, bf16[16,1536]{...) custom-call(bf16[16,1536]{1,0:T(8,128)(2,1)} %get-tuple-element.45.refs_0_, ...), custom_call_target="tpu_custom_call" | custom-call | tf_op jit(solution)/shard_map/far/pallas_call | solution.py:208
  181.6 4.3 %collective-permute-start.9 = (bf16[16,1536]{1,0:T(8,128)(2,1)}, bf16[16,1536]{1,0:T(8,128)(2,1)S(1)}, u32[]{:S(2)}, u32[]{:S(2)}) collective-permute-start(bf16[16,1536]{1,0:T(8,128)(2,1)} %get-tuple-element.57), channel_id=1, source_target_pairs={{0,6},{1,7},{2,0},{3,1},{4,2},{5,3},{6,4},{7,5},{8,14},{9,15},{10,... | collective-permute-start | bytes 147464 | tf_op jit(solution)/shard_map/ppermute | solution.py:188
  185.9 2.7 %collective-permute-start.10 = (bf16[16,1536]{1,0:T(8,128)(2,1)}, bf16[16,1536]{1,0:T(8,128)(2,1)S(1)}, u32[]{:S(2)}, u32[]{:S(2)}) collective-permute-start(bf16[16,1536]{1,0:T(8,128)(2,1)} %get-tuple-element.58), channel_id=1, source_target_pairs={{0,5},{1,6},{2,7},{3,0},{4,1},{5,2},{6,3},{7,4},{8,13},{9,14},{10,... | collective-permute-start | bytes 147464 | tf_op jit(solution)/shard_map/ppermute | solution.py:188
  188.6 4.3 %collective-permute-start.11 = (bf16[16,1536]{1,0:T(8,128)(2,1)}, bf16[16,1536]{1,0:T(8,128)(2,1)S(1)}, u32[]{:S(2)}, u32[]{:S(2)}) collective-permute-start(bf16[16,1536]{1,0:T(8,128)(2,1)} %get-tuple-element.59), channel_id=1, source_target_pairs={{0,4},{1,5},{2,6},{3,7},{4,0},{5,1},{6,2},{7,3},{8,12},{9,13},{10,... | collective-permute-start | bytes 147464 | tf_op jit(solution)/shard_map/ppermute | solution.py:188
  192.9 2.9 %collective-permute-start.12 = (bf16[16,1536]{1,0:T(8,128)(2,1)}, bf16[16,1536]{1,0:T(8,128)(2,1)S(1)}, u32[]{:S(2)}, u32[]{:S(2)}) collective-permute-start(bf16[16,1536]{1,0:T(8,128)(2,1)} %get-tuple-element.60), channel_id=1, source_target_pairs={{0,3},{1,4},{2,5},{3,6},{4,7},{5,0},{6,1},{7,2},{8,11},{9,12},{10,... | collective-permute-start | bytes 147464 | tf_op jit(solution)/shard_map/ppermute | solution.py:188
  201.4 7.9 %all-to-all-done.3.near_ref = bf16[32,16,1536]{2,1,0:T(8,128)(2,1)S(1)} async-done(((bf16[32,16,1536]{2,1,0:T(8,128)(2,1)}), bf16[32,16,1536]{2,1,0:T(8,128)(2,1)S(1)}, u32[]{:S(2)}, u32[]{:S(2)}) %all-to-all-start.3) | async-done | bytes 1572896 | tf_op jit(solution)/shard_map/all_to_all | solution.py:217
  210.6 3.4 %close.1 = bf16[8,64,192]{2,1,0:T(8,128)(2,1)} custom-call(s32[6]{0:T(128)} %stack.27.place_ref, s32[64,8]{1,0:T(8,128)} %copy.17.routes_ref, f32[64,8]{1,0:T(8,128)} %copy.18.gates_ref, f32[64,1536]{1,0:T(8,128)} %get-tuple-element.34.hid_ref, f32[1,1536]{1,0:T(1,128)} %reshape.11.gain_ref, bf16[32,16,1536]{2,1,0:T(8,128)(2,1)} %copy-done.1, ...), custom_call_target="tpu_custom_call" | custom-call | tf_op jit(solution)/shard_map/close/pallas_call | solution.py:220
  214.0 19.5 %all_to_all.25 = bf16[8,64,192]{2,1,0:T(8,128)(2,1)S(1)} all-to-all(bf16[8,64,192]{2,1,0:T(8,128)(2,1)} %close.1), channel_id=1, replica_groups=mesh['tp'=8,'h'=2,'y'=4,'x'=4,'c'=2] {'tp'}, dimensions={0} | all-to-all | bytes 393216 | tf_op jit(solution)/shard_map/all_to_all | solution.py:228
  (95 shorter events, 29.6 us)
Async XLA Ops:
  6.5 48.5 %copy-start = (s32[512,8]{0,1:T(8,128)S(1)}, s32[512,8]{0,1:T(8,128)}, u32[]{:S(2)}) copy-start(s32[512,8]{0,1:T(8,128)} %param.15) | copy-start | bytes 49156
  8.2 32.1 %all-to-all-start = ((bf16[64,24,192]{2,1,0:T(8,128)(2,1)}), bf16[64,24,192]{2,1,0:T(8,128)(2,1)S(1)}, u32[]{:S(2)}, u32[]{:S(2)}) async-start(bf16[64,24,192]{2,1,0:T(8,128)(2,1)} %broadcast_in_dim.2), calls=%async_computation | async-start | bytes 1572864 | tf_op jit(solution)/shard_map/all_to_all | solution.py:161
  18.7 94.0 %all-gather.6.cloned.1.call-start = ((), (), s32[]{:S(2)}) async-start(), calls=%async_computation.6 | async-start | bytes 2949120 | tf_op jit(solution)/shard_map/all_gather | solution.py:163
  22.1 0.7 collective-permute-start.7
  44.8 48.4 %all-to-all-start.1 = ((bf16[8,64,1536]{2,1,0:T(8,128)(2,1)}), bf16[8,64,1536]{2,1,0:T(8,128)(2,1)S(1)}, u32[]{:S(2)}, u32[]{:S(2)}) async-start(bf16[8,64,1536]{2,1,0:T(8,128)(2,1)} %project.1), calls=%async_computation.1 | async-start | bytes 3145728 | tf_op jit(solution)/shard_map/all_to_all | solution.py:173
  55.0 121.8 %all-gather.4.cloned.1.call-start = ((), (), s32[]{:S(2)}) async-start(), calls=%async_computation.5 | async-start | bytes 5308416 | tf_op jit(solution)/shard_map/all_gather | solution.py:186
  114.8 43.6 %all-to-all-start.2 = ((bf16[32,16,1536]{2,1,0:T(8,128)(2,1)}), bf16[32,16,1536]{2,1,0:T(8,128)(2,1)S(1)}, u32[]{:S(2)}, u32[]{:S(2)}) async-start(bf16[32,16,1536]{2,1,0:T(8,128)(2,1)} %get-tuple-element.35), calls=%async_computation.2 | async-start | bytes 3145728 | tf_op jit(solution)/shard_map/all_to_all | solution.py:190
  123.0 14.4 %collective-permute-start = (bf16[16,1536]{1,0:T(8,128)(2,1)S(1)}, bf16[16,1536]{1,0:T(8,128)(2,1)S(1)}, u32[]{:S(2)}, u32[]{:S(2)}) collective-permute-start(bf16[16,1536]{1,0:T(8,128)(2,1)S(1)} %copy-done.28), channel_id=1, source_target_pairs={{0,1},{1,2},{2,3},{3,4},{4,5},{5,6},{6,7},{7,0},{8,9},{9,10},{10,1... | collective-permute-start | bytes 147464 | tf_op jit(solution)/shard_map/ppermute | solution.py:188
  124.4 15.5 %collective-permute-start.1 = (bf16[16,1536]{1,0:T(8,128)(2,1)S(1)}, bf16[16,1536]{1,0:T(8,128)(2,1)S(1)}, u32[]{:S(2)}, u32[]{:S(2)}) collective-permute-start(bf16[16,1536]{1,0:T(8,128)(2,1)S(1)} %copy-done.27), channel_id=1, source_target_pairs={{0,2},{1,3},{2,4},{3,5},{4,6},{5,7},{6,0},{7,1},{8,10},{9,11},{10,... | collective-permute-start | bytes 147464 | tf_op jit(solution)/shard_map/ppermute | solution.py:188
  127.5 14.2 %collective-permute-start.2 = (bf16[16,1536]{1,0:T(8,128)(2,1)S(1)}, bf16[16,1536]{1,0:T(8,128)(2,1)S(1)}, u32[]{:S(2)}, u32[]{:S(2)}) collective-permute-start(bf16[16,1536]{1,0:T(8,128)(2,1)S(1)} %copy-done.26), channel_id=1, source_target_pairs={{0,3},{1,4},{2,5},{3,6},{4,7},{5,0},{6,1},{7,2},{8,11},{9,12},{10,... | collective-permute-start | bytes 147464 | tf_op jit(solution)/shard_map/ppermute | solution.py:188
  131.1 12.4 %collective-permute-start.3 = (bf16[16,1536]{1,0:T(8,128)(2,1)S(1)}, bf16[16,1536]{1,0:T(8,128)(2,1)S(1)}, u32[]{:S(2)}, u32[]{:S(2)}) collective-permute-start(bf16[16,1536]{1,0:T(8,128)(2,1)S(1)} %copy-done.25), channel_id=1, source_target_pairs={{0,4},{1,5},{2,6},{3,7},{4,0},{5,1},{6,2},{7,3},{8,12},{9,13},{10,... | collective-permute-start | bytes 147464 | tf_op jit(solution)/shard_map/ppermute | solution.py:188
  133.6 10.3 %collective-permute-start.4 = (bf16[16,1536]{1,0:T(8,128)(2,1)S(1)}, bf16[16,1536]{1,0:T(8,128)(2,1)S(1)}, u32[]{:S(2)}, u32[]{:S(2)}) collective-permute-start(bf16[16,1536]{1,0:T(8,128)(2,1)S(1)} %copy-done.24), channel_id=1, source_target_pairs={{0,5},{1,6},{2,7},{3,0},{4,1},{5,2},{6,3},{7,4},{8,13},{9,14},{10,... | collective-permute-start | bytes 147464 | tf_op jit(solution)/shard_map/ppermute | solution.py:188
  137.4 28.8 %copy-start.6 = (bf16[16,1536]{1,0:T(8,128)(2,1)}, bf16[16,1536]{1,0:T(8,128)(2,1)S(1)}, u32[]{:S(2)}) copy-start(bf16[16,1536]{1,0:T(8,128)(2,1)S(1)} %collective-permute-done.refs_1_) | copy-start | bytes 147460
  137.4 6.5 %collective-permute-start.5 = (bf16[16,1536]{1,0:T(8,128)(2,1)S(1)}, bf16[16,1536]{1,0:T(8,128)(2,1)S(1)}, u32[]{:S(2)}, u32[]{:S(2)}) collective-permute-start(bf16[16,1536]{1,0:T(8,128)(2,1)S(1)} %copy-done.23), channel_id=1, source_target_pairs={{0,6},{1,7},{2,0},{3,1},{4,2},{5,3},{6,4},{7,5},{8,14},{9,15},{10,... | collective-permute-start | bytes 147464 | tf_op jit(solution)/shard_map/ppermute | solution.py:188
  140.0 5.0 %collective-permute-start.6 = (bf16[16,1536]{1,0:T(8,128)(2,1)S(1)}, bf16[16,1536]{1,0:T(8,128)(2,1)S(1)}, u32[]{:S(2)}, u32[]{:S(2)}) collective-permute-start(bf16[16,1536]{1,0:T(8,128)(2,1)S(1)} %copy-done.22), channel_id=1, source_target_pairs={{0,7},{1,0},{2,1},{3,2},{4,3},{5,4},{6,5},{7,6},{8,15},{9,8},{10,9... | collective-permute-start | bytes 147464 | tf_op jit(solution)/shard_map/ppermute | solution.py:188
  166.2 43.1 %all-to-all-start.3 = ((bf16[32,16,1536]{2,1,0:T(8,128)(2,1)}), bf16[32,16,1536]{2,1,0:T(8,128)(2,1)S(1)}, u32[]{:S(2)}, u32[]{:S(2)}) async-start(bf16[32,16,1536]{2,1,0:T(8,128)(2,1)} %near.1), calls=%async_computation.3 | async-start | bytes 3145728 | tf_op jit(solution)/shard_map/all_to_all | solution.py:217
  173.9 26.9 %copy-start.21 = (f32[1536]{0:T(1024)S(1)}, f32[1536]{0:T(1024)}, u32[]{:S(2)}) copy-start(f32[1536]{0:T(1024)} %param.14) | copy-start | bytes 18436
  180.9 14.8 %collective-permute-start.8 = (bf16[16,1536]{1,0:T(8,128)(2,1)}, bf16[16,1536]{1,0:T(8,128)(2,1)S(1)}, u32[]{:S(2)}, u32[]{:S(2)}) collective-permute-start(bf16[16,1536]{1,0:T(8,128)(2,1)} %get-tuple-element.56), channel_id=1, source_target_pairs={{0,7},{1,0},{2,1},{3,2},{4,3},{5,4},{6,5},{7,6},{8,15},{9,8},{10,9... | collective-permute-start | bytes 147464 | tf_op jit(solution)/shard_map/ppermute | solution.py:188
  181.6 16.7 %collective-permute-start.9 = (bf16[16,1536]{1,0:T(8,128)(2,1)}, bf16[16,1536]{1,0:T(8,128)(2,1)S(1)}, u32[]{:S(2)}, u32[]{:S(2)}) collective-permute-start(bf16[16,1536]{1,0:T(8,128)(2,1)} %get-tuple-element.57), channel_id=1, source_target_pairs={{0,6},{1,7},{2,0},{3,1},{4,2},{5,3},{6,4},{7,5},{8,14},{9,15},{10,... | collective-permute-start | bytes 147464 | tf_op jit(solution)/shard_map/ppermute | solution.py:188
  185.9 23.5 %collective-permute-start.10 = (bf16[16,1536]{1,0:T(8,128)(2,1)}, bf16[16,1536]{1,0:T(8,128)(2,1)S(1)}, u32[]{:S(2)}, u32[]{:S(2)}) collective-permute-start(bf16[16,1536]{1,0:T(8,128)(2,1)} %get-tuple-element.58), channel_id=1, source_target_pairs={{0,5},{1,6},{2,7},{3,0},{4,1},{5,2},{6,3},{7,4},{8,13},{9,14},{10,... | collective-permute-start | bytes 147464 | tf_op jit(solution)/shard_map/ppermute | solution.py:188
  188.6 20.8 %collective-permute-start.11 = (bf16[16,1536]{1,0:T(8,128)(2,1)}, bf16[16,1536]{1,0:T(8,128)(2,1)S(1)}, u32[]{:S(2)}, u32[]{:S(2)}) collective-permute-start(bf16[16,1536]{1,0:T(8,128)(2,1)} %get-tuple-element.59), channel_id=1, source_target_pairs={{0,4},{1,5},{2,6},{3,7},{4,0},{5,1},{6,2},{7,3},{8,12},{9,13},{10,... | collective-permute-start | bytes 147464 | tf_op jit(solution)/shard_map/ppermute | solution.py:188
  192.9 16.5 %collective-permute-start.12 = (bf16[16,1536]{1,0:T(8,128)(2,1)}, bf16[16,1536]{1,0:T(8,128)(2,1)S(1)}, u32[]{:S(2)}, u32[]{:S(2)}) collective-permute-start(bf16[16,1536]{1,0:T(8,128)(2,1)} %get-tuple-element.60), channel_id=1, source_target_pairs={{0,3},{1,4},{2,5},{3,6},{4,7},{5,0},{6,1},{7,2},{8,11},{9,12},{10,... | collective-permute-start | bytes 147464 | tf_op jit(solution)/shard_map/ppermute | solution.py:188
  195.8 13.6 %collective-permute-start.13 = (bf16[16,1536]{1,0:T(8,128)(2,1)}, bf16[16,1536]{1,0:T(8,128)(2,1)S(1)}, u32[]{:S(2)}, u32[]{:S(2)}) collective-permute-start(bf16[16,1536]{1,0:T(8,128)(2,1)} %get-tuple-element.61), channel_id=1, source_target_pairs={{0,2},{1,3},{2,4},{3,5},{4,6},{5,7},{6,0},{7,1},{8,10},{9,11},{10,... | collective-permute-start | bytes 147464 | tf_op jit(solution)/shard_map/ppermute | solution.py:188
  198.3 11.1 %collective-permute-start.14 = (bf16[16,1536]{1,0:T(8,128)(2,1)}, bf16[16,1536]{1,0:T(8,128)(2,1)S(1)}, u32[]{:S(2)}, u32[]{:S(2)}) collective-permute-start(bf16[16,1536]{1,0:T(8,128)(2,1)} %get-tuple-element.62), channel_id=1, source_target_pairs={{0,1},{1,2},{2,3},{3,4},{4,5},{5,6},{6,7},{7,0},{8,9},{9,10},{10,1... | collective-permute-start | bytes 147464 | tf_op jit(solution)/shard_map/ppermute | solution.py:188
  (26 other events, 316.7 us)
Sparse Core Ops, SparseCore 0:
  40.5 72.1 all-gather.5
  114.8 61.8 all-gather.3
where the time goes:
time: 242 us; the launch traced here: 241 us
  waiting for transfers between devices  96.3 us (40%)
  starting transfers between devices  74.3 us (31%)
  Pallas kernels  24.1 us (10%)
  blocking collectives  19.5 us (8%)
  between operations  13.9 us (6%)
  local copies, waits for them, and re-layouts  13.1 us (5%)
    ppermute x14, starting transfers between devices, per_device(): lax.ppermute(v, ('x', 'c'), [(i, (i + k) % 8) for i in range(8)])  37 us
    all_to_all x1, waiting for transfers between devices, per_device(): parts = lax.all_to_all(parts, 'tp', 0, 0, tiled=True)  36.8 us
    all_to_all x1, blocking collectives, per_device(): return lax.all_to_all(finished, 'tp', 0, 0, tiled=True).reshape(512, 192)  19.5 us
    all_to_all x1, waiting for transfers between devices, per_device(): lax.all_to_all(jnp.broadcast_to(w_out.T[None], (64, 24, 192)), EP, 0, 0,...  17.6 us
    all_gather x1, waiting for transfers between devices, per_device(): pieces = lax.all_gather(crossed, 'y', axis=0, tiled=False)  14.5 us
    all_to_all x1, waiting for transfers between devices, per_device(): received = lax.all_to_all(send, ('y', 'x', 'c'), 0, 0, tiled=True)  13.4 us
    all_to_all x1, starting transfers between devices, per_device(): lax.all_to_all(jnp.broadcast_to(w_out.T[None], (64, 24, 192)), EP, 0, 0,...  10.5 us
    all_to_all x1, starting transfers between devices, per_device(): parts = lax.all_to_all(parts, 'tp', 0, 0, tiled=True)  10.2 us
  transfers between devices with their start and end apart: 21, of which 9 were waited for; matrix products, arithmetic and copies ran while one was open for 2% of the time, Pallas kernels for 9%

commit v1 on v0

v1 whole, which is shorter than its diff:
```python
import jax
import jax.numpy as jnp
from jax import lax
from jax.experimental import pallas as pl
from jax.experimental.pallas import tpu as pltpu
from jax.sharding import Mesh, PartitionSpec as P

EXPERTS = 40
CAP = 16
EPS = 1e-05
BF = jnp.bfloat16
F32 = jnp.float32
EP = ("h", "y", "x", "c")
VMEM = 56 * 1024 * 1024


def params():
    return pltpu.CompilerParams(vmem_limit_bytes=VMEM)


def dot(a, b, ca, cb):
    return lax.dot_general(a, b, (((ca,), (cb,)), ((), ())), preferred_element_type=F32)


def project_kernel(place_ref, attn_ref, resid_ref, w_ref, out_ref, w_scr):
    tp = place_ref[1]
    for i in range(8):
        for y in range(8):
            w_scr[(y * 8 + i) * 24 : (y * 8 + i + 1) * 24, :] = w_ref[i, y * 24 : (y + 1) * 24, :]
    at = lax.broadcasted_iota(jnp.int32, (1536, 192), 0)
    of = lax.broadcasted_iota(jnp.int32, (1536, 192), 1)
    choose = jnp.where(at == of + tp * 192, 1.0, 0.0).astype(BF)
    part = dot(attn_ref[...].T, w_scr[...], 1, 1) + dot(resid_ref[...].T, choose, 1, 1)
    out_ref[...] = part.astype(BF).reshape(8, 64, 1536)


def piece_kernel(place_ref, wg_ref, wu_ref, wd_ref, out_ref):
    out_ref[0:192, :] = wg_ref[0]
    out_ref[192:384, :] = wu_ref[0]
    for i in range(3):
        out_ref[384 + i * 64 : 448 + i * 64, :] = wd_ref[0, :, i * 512 : (i + 1) * 512]


def one_hot_rows(routed, expert, rank_of):
    hits = jnp.zeros((routed.shape[0], expert.shape[1]), F32)
    for k in range(8):
        hits = hits + jnp.where(routed[:, k : k + 1] == expert, 1.0, 0.0)
    ranks = dot(rank_of, hits.astype(BF), 1, 0)
    return hits, ranks


def before_matrix(rows):
    a = lax.broadcasted_iota(jnp.int32, (rows, rows), 0)
    b = lax.broadcasted_iota(jnp.int32, (rows, rows), 1)
    keep = (b < a) & (a // 64 == b // 64)
    return jnp.where(keep, 1.0, 0.0).astype(BF)


def lanes_of(half):
    lane = lax.broadcasted_iota(jnp.int32, (1, 768), 1)
    near = lane < 512
    far_lane = lane - 512
    expert_of = jnp.where(near, (32 * half + lane // CAP) % EXPERTS, 32 - 8 * half + (far_lane // 8) % 8)
    want = jnp.where(near, lane % CAP, 4 * (far_lane // 64) + lane % 4)
    copy = jnp.where(near, 2, (lane % 8) // 4)
    return expert_of.astype(F32), want.astype(F32), copy


def upper_copy(rows, columns):
    return lax.broadcasted_iota(jnp.int32, (rows, columns), 0) % 8 < 4


def near_to_wire(values, ref, slots):
    for k in range(12):
        ref[:, k * CAP : (k + 1) * CAP, :] = values[:, k * 128 : (k + 1) * 128].reshape(slots, CAP, 128)


def near_from_wire(ref, slots):
    parts = [ref[:, k * CAP : (k + 1) * CAP, :].reshape(slots * CAP, 128) for k in range(12)]
    return jnp.concatenate(parts, axis=1)


def far_to_wire(values, ref, start):
    upper = upper_copy(256, 128)
    for m in range(6):
        even, odd = values[:, m * 256 : m * 256 + 128], values[:, m * 256 + 128 : m * 256 + 256]
        ref[:, start + m * 8 : start + m * 8 + 8, :] = jnp.where(upper, even, odd).astype(BF).reshape(32, 8, 128)


def mix_kernel(place_ref, part_ref, routes_ref, gain_ref, send_ref, hid_ref):
    hidden = part_ref[0].astype(F32)
    for z in range(1, 8):
        hidden = hidden + part_ref[z].astype(F32)
    hid_ref[...] = hidden
    mean = jnp.sum(hidden * hidden, axis=1, keepdims=True) / 1536
    normed = (hidden * lax.rsqrt(mean + EPS) * gain_ref[...]).astype(BF)
    expert_of, want, _ = lanes_of(place_ref[0])
    hits, ranks = one_hot_rows(routes_ref[...].astype(F32), expert_of, before_matrix(64))
    pick = jnp.where(ranks == want, hits, 0.0).astype(BF)
    near_to_wire(dot(pick[:, 0:512], normed, 0, 0).astype(BF), send_ref, 32)
    far_to_wire(dot(pick[:, 512:768], normed, 0, 0), send_ref, 192)


def act(gate, up):
    return (gate / (1.0 + jnp.exp(-gate)) * up).astype(BF)


def near_kernel(x_ref, wg_ref, wu_ref, wd_ref, out_ref):
    x = near_from_wire(x_ref, 16)
    y = dot(act(dot(x, wg_ref[0], 1, 0), dot(x, wu_ref[0], 1, 0)), wd_ref[0], 1, 0)
    near_to_wire(y.astype(BF), out_ref, 16)


def far_kernel(place_ref, x_ref, *refs):
    w_refs, out_ref, (wg_scr, wu_scr, wd_scr) = refs[0:8], refs[9], refs[10:]
    tp = place_ref[1]
    for ref, away in zip(w_refs, (0, -1, 1, -2, 2, -3, 3, -4)):
        z = (tp + away + 8) % 8
        wide, thin = pl.ds(pl.multiple_of(z * 192, 64), 192), pl.ds(pl.multiple_of(z * 64, 64), 64)
        wg_scr[wide, :] = ref[0:192, :]
        wu_scr[wide, :] = ref[192:384, :]
        for i in range(3):
            wd_scr[thin, i * 512 : (i + 1) * 512] = ref[384 + i * 64 : 448 + i * 64, :]
    x = jnp.concatenate([x_ref[:, m * 8 : m * 8 + 8, :].reshape(256, 128) for m in range(6)], axis=1)
    upper = upper_copy(256, 512)

    def whole(scr):
        even = jnp.concatenate([scr[m * 256 : m * 256 + 128, :] for m in range(6)], axis=0)
        odd = jnp.concatenate([scr[m * 256 + 128 : m * 256 + 256, :] for m in range(6)], axis=0)
        a, b = dot(x, even, 1, 0), dot(x, odd, 1, 0)
        return jnp.where(upper, a + pltpu.roll(b, 252, 0), b + pltpu.roll(a, 4, 0))

    far_to_wire(dot(act(whole(wg_scr), whole(wu_scr)), wd_scr[...], 1, 0), out_ref, 0)


def close_kernel(place_ref, routes_ref, gates_ref, hid_ref, gain_ref, got_ref, out_ref):
    expert_of, want, copy = lanes_of(place_ref[0])
    routed = routes_ref[...].astype(F32)
    hits, ranks = one_hot_rows(routed, expert_of, before_matrix(64))
    gate = jnp.zeros((64, 768), F32)
    for k in range(8):
        gate = gate + jnp.where(routed[:, k : k + 1] == expert_of, gates_ref[:, k : k + 1], 0.0)
    gate = jnp.where((ranks == want) & (hits > 0.5), gate, 0.0)
    high = gate.astype(BF).astype(F32)
    both = jnp.concatenate([high, gate - high], axis=0)
    total = dot(both[:, 0:512].astype(BF), near_from_wire(got_ref, 32), 1, 0)
    far = both[:, 512:768]
    copies = [jnp.where(copy[:, 512:768] == u, far, 0.0) for u in range(2)]
    far = jnp.concatenate(copies, axis=0).astype(BF)
    chunks = []
    for m in range(6):
        part = dot(far, got_ref[:, 192 + m * 8 : 200 + m * 8, :].reshape(256, 128), 1, 0)
        chunks += [part[0:128], part[128:256]]
    total = total + jnp.concatenate(chunks, axis=1)
    combined = hid_ref[...] + (total[0:64] + total[64:128])
    mean = jnp.sum(combined * combined, axis=1, keepdims=True) / 1536
    out = (combined * lax.rsqrt(mean + EPS) * gain_ref[...]).astype(BF)
    for z in range(8):
        out_ref[z] = out[:, z * 192 : (z + 1) * 192]


def smem():
    return pl.BlockSpec(memory_space=pltpu.SMEM)


def vmem():
    return pl.BlockSpec(memory_space=pltpu.VMEM)


def per_device(attn, resid, w_out, gain_mix, gain_out, routes, gates, w_gate, w_up, w_down):
    tp, h = lax.axis_index("tp"), lax.axis_index("h")
    place = jnp.stack([h, tp])
    shape = jax.ShapeDtypeStruct
    my_routes = lax.dynamic_slice_in_dim(routes, tp * 64, 64, 0)
    my_gates = lax.dynamic_slice_in_dim(gates, tp * 64, 64, 0)

    piece = pl.pallas_call(
        piece_kernel,
        grid_spec=pltpu.PrefetchScalarGridSpec(
            num_scalar_prefetch=1,
            grid=(1,),
            in_specs=[
                pl.BlockSpec((1, 192, 512), lambda i, p: (0, p[1], 0)),
                pl.BlockSpec((1, 192, 512), lambda i, p: (0, p[1], 0)),
                pl.BlockSpec((1, 64, 1536), lambda i, p: (0, p[1], 0)),
            ],
            out_specs=pl.BlockSpec((576, 512), lambda i, p: (0, 0)),
        ),
        out_shape=shape((576, 512), BF),
        compiler_params=params(),
        name="piece",
    )(place, w_gate, w_up, w_down)
    across = lambda v, a, b, c, d: lax.ppermute(v, ("h", "y"), [(a, b), (c, d)])
    step_1 = across(piece, 4, 3, 3, 4)
    columns = lax.all_to_all(jnp.broadcast_to(w_out.T[None], (8, 24, 192)), ("h", "y"), 0, 0, tiled=True)
    columns = jnp.broadcast_to(columns.reshape(1, 192, 192), (8, 192, 192))
    columns = lax.all_to_all(columns, ("x", "c"), 0, 0, tiled=True)
    columns, step_1, piece = lax.optimization_barrier((columns, step_1, piece))
    step_2 = across(step_1, 3, 2, 4, 5)
    step_3 = across(piece, 4, 1, 3, 6)
    step_4 = across(step_3, 1, 0, 6, 7)

    parts = pl.pallas_call(
        project_kernel,
        out_shape=shape((8, 64, 1536), BF),
        in_specs=[smem()] + [vmem()] * 3,
        out_specs=vmem(),
        scratch_shapes=[pltpu.VMEM((1536, 192), BF)],
        compiler_params=params(),
        name="project",
    )(place, attn.T, resid.T, columns)
    parts = lax.all_to_all(parts, "tp", 0, 0, tiled=True)
    far_piece = (step_1 + step_2) + (step_3 + step_4)
    parts, far_piece = lax.optimization_barrier((parts, far_piece))

    turn = lambda v, d: lax.ppermute(v, "tp", [(i, (i + d) % 8) for i in range(8)])
    ring = [far_piece]
    up = down = far_piece
    for _ in range(3):
        up, down = turn(up, 1), turn(down, -1)
        ring += [up, down]
    ring.append(turn(up, 1))

    send, hidden = pl.pallas_call(
        mix_kernel,
        out_shape=(shape((32, 240, 128), BF), shape((64, 1536), F32)),
        in_specs=[smem()] + [vmem()] * 3,
        out_specs=(vmem(), vmem()),
        compiler_params=params(),
        name="mix",
    )(place, parts, my_routes, gain_mix.reshape(1, 1536))
    received = lax.all_to_all(send, ("y", "x", "c"), 0, 0, tiled=True)

    whole = lambda *dims: pl.BlockSpec(dims, lambda i: (0,) * len(dims))
    near = pl.pallas_call(
        near_kernel,
        grid=(2,),
        out_shape=shape((32, 240, 128), BF),
        in_specs=[
            pl.BlockSpec((16, 192, 128), lambda i: (i, 0, 0)),
            whole(1, 1536, 512),
            whole(1, 1536, 512),
            whole(1, 512, 1536),
        ],
        out_specs=pl.BlockSpec((16, 192, 128), lambda i: (i, 0, 0)),
        compiler_params=params(),
        name="near",
    )(received, w_gate, w_up, w_down)
    done = pl.pallas_call(
        far_kernel,
        grid=(1,),
        out_shape=shape((32, 240, 128), BF),
        in_specs=[smem(), pl.BlockSpec((32, 48, 128), lambda i: (0, 4, 0))]
        + [whole(576, 512)] * 8
        + [pl.BlockSpec(memory_space=pl.ANY)],
        out_specs=pl.BlockSpec((32, 48, 128), lambda i: (0, 4, 0)),
        scratch_shapes=[pltpu.VMEM((1536, 512), BF), pltpu.VMEM((1536, 512), BF), pltpu.VMEM((512, 1536), BF)],
        input_output_aliases={10: 0},
        compiler_params=params(),
        name="far",
    )(place, received, *ring, near)
    done = lax.all_to_all(done, ("y", "x", "c"), 0, 0, tiled=True)

    finished = pl.pallas_call(
        close_kernel,
        out_shape=shape((8, 64, 192), BF),
        in_specs=[smem()] + [vmem()] * 5,
        out_specs=vmem(),
        compiler_params=params(),
        name="close",
    )(place, my_routes, my_gates, hidden, gain_out.reshape(1, 1536), done)
    return lax.all_to_all(finished, "tp", 0, 0, tiled=True).reshape(512, 192)


def solution(mesh):
    fine = Mesh(mesh.devices.reshape(8, 2, 4, 4, 2), ("tp",) + EP)
    return jax.shard_map(
        per_device,
        mesh=fine,
        in_specs=(
            P(EP, "tp"),
            P(EP, "tp"),
            P("tp", EP),
            P(),
            P(),
            P(EP, None),
            P(EP, None),
            P(EP, None, None),
            P(EP, None, None),
            P(EP, None, None),
        ),
        out_specs=P(EP, "tp"),
        check_vma=False,
    )
```

time: 242 us -> 251 us (1.037); the launches traced: 241 us -> 247 us
  waiting for transfers between devices: 96.3 us -> 125 us
  between operations: 13.9 us -> 0.19 us
  starting transfers between devices: 74.3 us -> 67.2 us
  blocking collectives: 19.5 us -> 15.6 us
    ppermute x15 -> x11, waiting for transfers between devices: 3.27 us -> 63.4 us  [the longest x7 36.2 us: per_device(): lax.ppermute(v, 'tp', [(i, (i + d) % 8) for i in range(8)])]
    all_to_all x1, waiting for transfers between devices: 36.8 us -> 7.02 us  [per_device(): parts = lax.all_to_all(parts, 'tp', 0, 0, tiled=True)]
    all_to_all x2 -> x3, waiting for transfers between devices: 25.5 us -> 55 us  [the longest x1 42 us: per_device(): done = lax.all_to_all(done, ('y', 'x', 'c'), 0, 0, tiled=True)]
    all_gather x2 -> x0, waiting for transfers between devices: 17.3 us -> none  [the longest x1 14.5 us: per_device(): pieces = lax.all_gather(crossed, 'y', axis=0, tiled=False)]
    all_to_all x1, waiting for transfers between devices: 13.4 us -> 0.01 us  [per_device(): received = lax.all_to_all(send, ('y', 'x', 'c'), 0, 0, tiled=True)]
    ppermute x15 -> x11, starting transfers between devices: 37.7 us -> 25.5 us  [the longest x7 21.4 us: per_device(): lax.ppermute(v, 'tp', [(i, (i + d) % 8) for i in range(8)])]
    all_to_all x2 -> x3, starting transfers between devices: 18.2 us -> 24.9 us  [the longest x1 11.5 us: per_device(): done = lax.all_to_all(done, ('y', 'x', 'c'), 0, 0, tiled=True)]
    all_to_all x1, blocking collectives: 19.5 us -> 15.6 us  [per_device(): return lax.all_to_all(finished, 'tp', 0, 0, tiled=True).reshape(512, 192)]
  transfers between devices with their start and end apart: 21 -> 16, of which waited for: 9 -> 9; matrix products, arithmetic and copies ran while one was open for 2% -> 3% of each run, Pallas kernels for 9% -> 4%
where the time goes in v1:
time: 251 us; the launch traced here: 247 us
  waiting for transfers between devices  125 us (50%)
  starting transfers between devices  67.2 us (27%)
  Pallas kernels  25.4 us (10%)
  blocking collectives  15.6 us (6%)
  local copies, waits for them, and re-layouts  11.2 us (4%)
    all_to_all x1, waiting for transfers between devices, per_device(): done = lax.all_to_all(done, ('y', 'x', 'c'), 0, 0, tiled=True)  42 us
    ppermute x7, waiting for transfers between devices, per_device(): lax.ppermute(v, 'tp', [(i, (i + d) % 8) for i in range(8)])  36.2 us
    ppermute x4, waiting for transfers between devices, per_device(): across = lambda v, a, b, c, d: lax.ppermute(v, ('h', 'y'), [(a, b), (c, d)])  27.2 us
    ppermute x7, starting transfers between devices, per_device(): lax.ppermute(v, 'tp', [(i, (i + d) % 8) for i in range(8)])  21.4 us
    all_to_all x1, blocking collectives, per_device(): return lax.all_to_all(finished, 'tp', 0, 0, tiled=True).reshape(512, 192)  15.6 us
    all_to_all x1, waiting for transfers between devices, per_device(): columns = lax.all_to_all(columns, ('x', 'c'), 0, 0, tiled=True)  12.3 us
    all_to_all x1, starting transfers between devices, per_device(): done = lax.all_to_all(done, ('y', 'x', 'c'), 0, 0, tiled=True)  11.5 us
    all_to_all x1, starting transfers between devices, per_device(): parts = lax.all_to_all(parts, 'tp', 0, 0, tiled=True)  9.38 us
  transfers between devices with their start and end apart: 16, of which 9 were waited for; matrix products, arithmetic and copies ran while one was open for 3% of the time, Pallas kernels for 4%

profile of v1, /device:TPU:57, one launch (start us, length us, event | category | flops | bytes accessed | tf_op | source)
XLA Modules:
  0.0 247.0 jit_solution(1894390371402167757)
XLA Ops:
  1.4 6.3 %all-to-all-start = ((bf16[8,24,192]{2,1,0:T(8,128)(2,1)}), bf16[8,24,192]{2,1,0:T(8,128)(2,1)S(1)}, u32[]{:S(2)}, u32[]{:S(2)}) async-start(bf16[8,24,192]{2,1,0:T(8,128)(2,1)} %broadcast_in_dim.6), calls=%async_computation | async-start | bytes 196608 | tf_op jit(solution)/shard_map/all_to_all | solution.py:195
  8.3 2.6 %piece.1 = bf16[576,512]{1,0:T(8,128)(2,1)} custom-call(s32[2]{0:T(128)} %pad_add_fusion.place_ref, bf16[1,1536,512]{2,1,0:T(8,128)(2,1)} %wg_ref.3, bf16[1,1536,512]{2,1,0:T(8,128)(2,1)} %wu_ref.3, bf16[1,512,1536]{2,1,0:T(8,128)(2,1)} %wd_ref.3), custom_call_target="tpu_custom_call" | custom-call | tf_op jit(solution)/shard_map/piece/pallas_call | solution.py:177
  13.3 7.2 %all-to-all-start.1 = ((bf16[8,192,192]{2,1,0:T(8,128)(2,1)}), bf16[8,192,192]{2,1,0:T(8,128)(2,1)S(1)}, u32[]{:S(2)}, u32[]{:S(2)}) async-start(bf16[8,192,192]{2,1,0:T(8,128)(2,1)} %broadcast_in_dim.15), calls=%async_computation.1 | async-start | bytes 1572864 | tf_op jit(solution)/shard_map/all_to_all | solution.py:197
  20.5 12.3 %all-to-all-done.1.w_ref = bf16[8,192,192]{2,1,0:T(8,128)(2,1)S(1)} async-done(((bf16[8,192,192]{2,1,0:T(8,128)(2,1)}), bf16[8,192,192]{2,1,0:T(8,128)(2,1)S(1)}, u32[]{:S(2)}, u32[]{:S(2)}) %all-to-all-start.1) | async-done | bytes 589856 | tf_op jit(solution)/shard_map/all_to_all | solution.py:197
  33.7 3.6 %project.1 = bf16[8,64,1536]{2,1,0:T(8,128)(2,1)} custom-call(s32[2]{0:T(128)} %pad_add_fusion.place_ref, bf16[192,512]{1,0:T(8,128)(2,1)} %bitcast.9, bf16[192,512]{1,0:T(8,128)(2,1)} %bitcast.10, bf16[8,192,192]{2,1,0:T(8,128)(2,1)} %copy-done.4), custom_call_target="tpu_custom_call" | custom-call | tf_op jit(solution)/shard_map/project/pallas_call | solution.py:203
  37.3 9.4 %all-to-all-start.2 = ((bf16[8,64,1536]{2,1,0:T(8,128)(2,1)}), bf16[8,64,1536]{2,1,0:T(8,128)(2,1)S(1)}, u32[]{:S(2)}, u32[]{:S(2)}) async-start(bf16[8,64,1536]{2,1,0:T(8,128)(2,1)} %project.1), calls=%async_computation.2 | async-start | bytes 3145728 | tf_op jit(solution)/shard_map/all_to_all | solution.py:212
  51.6 27.2 %collective-permute-done.3 = bf16[576,512]{1,0:T(8,128)(2,1)} collective-permute-done((bf16[576,512]{1,0:T(8,128)(2,1)S(1)}, bf16[576,512]{1,0:T(8,128)(2,1)}, u32[]{:S(2)}, u32[]{:S(2)}) %collective-permute-start.3) | collective-permute-done | bytes 589856 | tf_op jit(solution)/shard_map/ppermute | solution.py:193
  80.1 7.0 %all-to-all-done.2.part_ref = bf16[8,64,1536]{2,1,0:T(8,128)(2,1)S(1)} async-done(((bf16[8,64,1536]{2,1,0:T(8,128)(2,1)}), bf16[8,64,1536]{2,1,0:T(8,128)(2,1)S(1)}, u32[]{:S(2)}, u32[]{:S(2)}) %all-to-all-start.2) | async-done | bytes 1572896 | tf_op jit(solution)/shard_map/all_to_all | solution.py:212
  88.3 4.0 %mix.1 = (bf16[32,240,128]{2,1,0:T(8,128)(2,1)}, f32[64,1536]{1,0:T(8,128)}) custom-call(s32[2]{0:T(128)} %pad_add_fusion.place_ref, bf16[8,64,1536]{2,1,0:T(8,128)(2,1)} %copy-done.3, s32[64,8]{1,0:T(8,128)} %copy.15.routes_ref, f32[1,1536]{1,0:T(1,128)} %reshape.12.gain_ref), custom_call_target="tpu_custom_call" | custom-call | tf_op jit(solution)/shard_map/mix/pallas_call | solution.py:224
  92.3 7.4 %all-to-all-start.3 = ((bf16[32,240,128]{2,1,0:T(8,128)(2,1)}), bf16[32,240,128]{2,1,0:T(8,128)(2,1)S(1)}, u32[]{:S(2)}, u32[]{:S(2)}) async-start(bf16[32,240,128]{2,1,0:T(8,128)(2,1)} %get-tuple-element.17), calls=%async_computation.3 | async-start | bytes 3932160 | tf_op jit(solution)/shard_map/all_to_all | solution.py:232
  99.7 2.2 collective-permute-start.4
  101.9 4.3 %collective-permute-start.5 = (bf16[576,512]{1,0:T(8,128)(2,1)S(1)}, bf16[576,512]{1,0:T(8,128)(2,1)S(1)}, u32[]{:S(2)}, u32[]{:S(2)}) collective-permute-start(bf16[576,512]{1,0:T(8,128)(2,1)S(1)} %add_add_fusion.refs_0_), channel_id=1, source_target_pairs={{0,448},{64,0},{128,64},{192,128},{256,192},{320,256},{384,320},{4... | collective-permute-start | bytes 1769480 | tf_op jit(solution)/shard_map/ppermute | solution.py:216
  106.2 11.1 %collective-permute-done.4.refs_1_ = bf16[576,512]{1,0:T(8,128)(2,1)S(1)} collective-permute-done((bf16[576,512]{1,0:T(8,128)(2,1)S(1)}, bf16[576,512]{1,0:T(8,128)(2,1)S(1)}, u32[]{:S(2)}, u32[]{:S(2)}) %collective-permute-start.4) | collective-permute-done | bytes 589856 | tf_op jit(solution)/shard_map/ppermute | solution.py:216
  119.3 4.6 %collective-permute-start.7 = (bf16[576,512]{1,0:T(8,128)(2,1)S(1)}, bf16[576,512]{1,0:T(8,128)(2,1)}, u32[]{:S(2)}, u32[]{:S(2)}) collective-permute-start(bf16[576,512]{1,0:T(8,128)(2,1)S(1)} %collective-permute-done.5.refs_2_), channel_id=1, source_target_pairs={{0,448},{64,0},{128,64},{192,128},{256,192},{320,256},{384,320},{4... | collective-permute-start | bytes 1769480 | tf_op jit(solution)/shard_map/ppermute | solution.py:216
  123.9 10.2 %collective-permute-done.6.refs_3_ = bf16[576,512]{1,0:T(8,128)(2,1)S(1)} collective-permute-done((bf16[576,512]{1,0:T(8,128)(2,1)S(1)}, bf16[576,512]{1,0:T(8,128)(2,1)S(1)}, u32[]{:S(2)}, u32[]{:S(2)}) %collective-permute-start.6) | collective-permute-done | bytes 589856 | tf_op jit(solution)/shard_map/ppermute | solution.py:216
  136.0 4.6 %collective-permute-start.9 = (bf16[576,512]{1,0:T(8,128)(2,1)}, bf16[576,512]{1,0:T(8,128)(2,1)}, u32[]{:S(2)}, u32[]{:S(2)}) collective-permute-start(bf16[576,512]{1,0:T(8,128)(2,1)} %collective-permute-done.7.refs_4_), channel_id=1, source_target_pairs={{0,448},{64,0},{128,64},{192,128},{256,192},{320,256},{384,320},{4... | collective-permute-start | bytes 1769480 | tf_op jit(solution)/shard_map/ppermute | solution.py:216
  140.6 9.4 %collective-permute-done.8.refs_5_ = bf16[576,512]{1,0:T(8,128)(2,1)} collective-permute-done((bf16[576,512]{1,0:T(8,128)(2,1)S(1)}, bf16[576,512]{1,0:T(8,128)(2,1)}, u32[]{:S(2)}, u32[]{:S(2)}) %collective-permute-start.8) | collective-permute-done | bytes 589856 | tf_op jit(solution)/shard_map/ppermute | solution.py:216
  153.2 6.5 %near.1.refs_8_ = bf16[32,240,128]{2,1,0:T(8,128)(2,1)} custom-call(bf16[32,240,128]{2,1,0:T(8,128)(2,1)} %copy-done.1, bf16[1,1536,512]{2,1,0:T(8,128)(2,1)} %wg_ref.3, bf16[1,1536,512]{2,1,0:T(8,128)(2,1)} %wu_ref.3, bf16[1,512,1536]{2,1,0:T(8,128)(2,1)} %wd_ref.3), custom_call_target="tpu_custom_call" | custom-call | tf_op jit(solution)/shard_map/near/pallas_call | solution.py:235
  159.7 5.5 %collective-permute-done.10.refs_7_ = bf16[576,512]{1,0:T(8,128)(2,1)} collective-permute-done((bf16[576,512]{1,0:T(8,128)(2,1)}, bf16[576,512]{1,0:T(8,128)(2,1)}, u32[]{:S(2)}, u32[]{:S(2)}) %collective-permute-start.10) | collective-permute-done | bytes 589856 | tf_op jit(solution)/shard_map/ppermute | solution.py:216
  165.2 5.0 %far.1 = bf16[32,240,128]{2,1,0:T(8,128)(2,1)} custom-call(s32[2]{0:T(128)} %pad_add_fusion.place_ref, bf16[32,240,128]{2,1,0:T(8,128)(2,1)} %copy-done.1, bf16[576,512]{1,0:T(8,128)(2,1)} %copy-done.5, bf16[576,512]{1,0:T(8,128)(2,1)} %copy-done.7, bf16[576,512]{1,0:T(8,128)(2,1)} %copy-done.8, ...), custom_call_target="tpu_custom_call", output_to_operand_aliasing={{}: (10, {})} | custom-call | tf_op jit(solution)/shard_map/far/pallas_call | solution.py:249
  170.2 11.5 %all-to-all-start.4 = ((bf16[32,240,128]{2,1,0:T(8,128)(2,1)}), bf16[32,240,128]{2,1,0:T(8,128)(2,1)S(1)}, u32[]{:S(2)}, u32[]{:S(2)}) async-start(bf16[32,240,128]{2,1,0:T(8,128)(2,1)} %far.1), calls=%async_computation.4 | async-start | bytes 3932160 | tf_op jit(solution)/shard_map/all_to_all | solution.py:262
  183.7 42.0 %all-to-all-done.4.got_ref = bf16[32,240,128]{2,1,0:T(8,128)(2,1)S(1)} async-done(((bf16[32,240,128]{2,1,0:T(8,128)(2,1)}), bf16[32,240,128]{2,1,0:T(8,128)(2,1)S(1)}, u32[]{:S(2)}, u32[]{:S(2)}) %all-to-all-start.4) | async-done | bytes 1966112 | tf_op jit(solution)/shard_map/all_to_all | solution.py:262
  227.0 3.6 %close.1 = bf16[8,64,192]{2,1,0:T(8,128)(2,1)} custom-call(s32[2]{0:T(128)} %pad_add_fusion.place_ref, s32[64,8]{1,0:T(8,128)} %copy.15.routes_ref, f32[64,8]{1,0:T(8,128)} %copy.16.gates_ref, f32[64,1536]{1,0:T(8,128)} %get-tuple-element.16.hid_ref, f32[1,1536]{1,0:T(1,128)} %reshape.13.gain_ref, bf16[32,240,128]{2,1,0:T(8,128)(2,1)} %copy-done.2), custom_call_target="tpu_custom_call" | custom-call | tf_op jit(solution)/shard_map/close/pallas_call | solution.py:264
  230.6 15.6 %all_to_all.30 = bf16[8,64,192]{2,1,0:T(8,128)(2,1)S(1)} all-to-all(bf16[8,64,192]{2,1,0:T(8,128)(2,1)} %close.1), channel_id=1, replica_groups=mesh['tp'=8,'h'=2,'y'=4,'x'=4,'c'=2] {'tp'}, dimensions={0} | all-to-all | bytes 393216 | tf_op jit(solution)/shard_map/all_to_all | solution.py:272
  (50 shorter events, 23.8 us)
Async XLA Ops:
  0.0 50.2 %copy-start = (s32[512,8]{0,1:T(8,128)S(1)}, s32[512,8]{0,1:T(8,128)}, u32[]{:S(2)}) copy-start(s32[512,8]{0,1:T(8,128)} %param.15) | copy-start | bytes 49156
  1.4 11.0 %all-to-all-start = ((bf16[8,24,192]{2,1,0:T(8,128)(2,1)}), bf16[8,24,192]{2,1,0:T(8,128)(2,1)S(1)}, u32[]{:S(2)}, u32[]{:S(2)}) async-start(bf16[8,24,192]{2,1,0:T(8,128)(2,1)} %broadcast_in_dim.6), calls=%async_computation | async-start | bytes 196608 | tf_op jit(solution)/shard_map/all_to_all | solution.py:195
  10.9 9.6 %collective-permute-start = (bf16[576,512]{1,0:T(8,128)(2,1)}, bf16[576,512]{1,0:T(8,128)(2,1)S(1)}, u32[]{:S(2)}, u32[]{:S(2)}) collective-permute-start(bf16[576,512]{1,0:T(8,128)(2,1)} %piece.1), channel_id=1, source_target_pairs={{32,24},{24,32},{33,25},{25,33},{34,26},{26,34},{35,27},{27,35},{3... | collective-permute-start | bytes 1769480 | tf_op jit(solution)/shard_map/ppermute | solution.py:193
  13.3 19.5 %all-to-all-start.1 = ((bf16[8,192,192]{2,1,0:T(8,128)(2,1)}), bf16[8,192,192]{2,1,0:T(8,128)(2,1)S(1)}, u32[]{:S(2)}, u32[]{:S(2)}) async-start(bf16[8,192,192]{2,1,0:T(8,128)(2,1)} %broadcast_in_dim.15), calls=%async_computation.1 | async-start | bytes 1572864 | tf_op jit(solution)/shard_map/all_to_all | solution.py:197
  37.3 9.4 %copy-start.6 = (bf16[576,512]{1,0:T(8,128)(2,1)S(1)}, bf16[576,512]{1,0:T(8,128)(2,1)}, u32[]{:S(2)}) copy-start(bf16[576,512]{1,0:T(8,128)(2,1)} %piece.1) | copy-start | bytes 1769476
  37.3 13.7 %copy-start.10 = (f32[1536]{0:T(1024)S(1)}, f32[1536]{0:T(1024)}, u32[]{:S(2)}) copy-start(f32[1536]{0:T(1024)} %param.13) | copy-start | bytes 18436
  37.3 49.8 %all-to-all-start.2 = ((bf16[8,64,1536]{2,1,0:T(8,128)(2,1)}), bf16[8,64,1536]{2,1,0:T(8,128)(2,1)S(1)}, u32[]{:S(2)}, u32[]{:S(2)}) async-start(bf16[8,64,1536]{2,1,0:T(8,128)(2,1)} %project.1), calls=%async_computation.2 | async-start | bytes 3145728 | tf_op jit(solution)/shard_map/all_to_all | solution.py:212
  46.7 2.2 collective-permute-start.2
  47.4 4.2 %collective-permute-start.1 = (bf16[576,512]{1,0:T(8,128)(2,1)S(1)}, bf16[576,512]{1,0:T(8,128)(2,1)}, u32[]{:S(2)}, u32[]{:S(2)}) collective-permute-start(bf16[576,512]{1,0:T(8,128)(2,1)S(1)} %collective-permute-done), channel_id=1, source_target_pairs={{24,16},{32,40},{25,17},{33,41},{26,18},{34,42},{27,19},{35,43},{2... | collective-permute-start | bytes 1769480 | tf_op jit(solution)/shard_map/ppermute | solution.py:193
  48.9 29.9 %collective-permute-start.3 = (bf16[576,512]{1,0:T(8,128)(2,1)S(1)}, bf16[576,512]{1,0:T(8,128)(2,1)}, u32[]{:S(2)}, u32[]{:S(2)}) collective-permute-start(bf16[576,512]{1,0:T(8,128)(2,1)S(1)} %collective-permute-done.2), channel_id=1, source_target_pairs={{8,0},{48,56},{9,1},{49,57},{10,2},{50,58},{11,3},{51,59},{12,4},{... | collective-permute-start | bytes 1769480 | tf_op jit(solution)/shard_map/ppermute | solution.py:193
  80.1 79.6 %copy-start.5 = (bf16[576,512]{1,0:T(8,128)(2,1)}, bf16[576,512]{1,0:T(8,128)(2,1)S(1)}, u32[]{:S(2)}) copy-start(bf16[576,512]{1,0:T(8,128)(2,1)S(1)} %add_add_fusion.refs_0_) | copy-start | bytes 1769476
  92.3 59.6 %all-to-all-start.3 = ((bf16[32,240,128]{2,1,0:T(8,128)(2,1)}), bf16[32,240,128]{2,1,0:T(8,128)(2,1)S(1)}, u32[]{:S(2)}, u32[]{:S(2)}) async-start(bf16[32,240,128]{2,1,0:T(8,128)(2,1)} %get-tuple-element.17), calls=%async_computation.3 | async-start | bytes 3932160 | tf_op jit(solution)/shard_map/all_to_all | solution.py:232
  99.7 17.7 %collective-permute-start.4 = (bf16[576,512]{1,0:T(8,128)(2,1)S(1)}, bf16[576,512]{1,0:T(8,128)(2,1)S(1)}, u32[]{:S(2)}, u32[]{:S(2)}) collective-permute-start(bf16[576,512]{1,0:T(8,128)(2,1)S(1)} %add_add_fusion.refs_0_), channel_id=1, source_target_pairs={{0,64},{64,128},{128,192},{192,256},{256,320},{320,384},{384,448},... | collective-permute-start | bytes 1769480 | tf_op jit(solution)/shard_map/ppermute | solution.py:216
  101.9 17.4 %collective-permute-start.5 = (bf16[576,512]{1,0:T(8,128)(2,1)S(1)}, bf16[576,512]{1,0:T(8,128)(2,1)S(1)}, u32[]{:S(2)}, u32[]{:S(2)}) collective-permute-start(bf16[576,512]{1,0:T(8,128)(2,1)S(1)} %add_add_fusion.refs_0_), channel_id=1, source_target_pairs={{0,448},{64,0},{128,64},{192,128},{256,192},{320,256},{384,320},{4... | collective-permute-start | bytes 1769480 | tf_op jit(solution)/shard_map/ppermute | solution.py:216
  117.3 47.8 %copy-start.7 = (bf16[576,512]{1,0:T(8,128)(2,1)}, bf16[576,512]{1,0:T(8,128)(2,1)S(1)}, u32[]{:S(2)}) copy-start(bf16[576,512]{1,0:T(8,128)(2,1)S(1)} %collective-permute-done.4.refs_1_) | copy-start | bytes 1769476
  117.3 16.7 %collective-permute-start.6 = (bf16[576,512]{1,0:T(8,128)(2,1)S(1)}, bf16[576,512]{1,0:T(8,128)(2,1)S(1)}, u32[]{:S(2)}, u32[]{:S(2)}) collective-permute-start(bf16[576,512]{1,0:T(8,128)(2,1)S(1)} %collective-permute-done.4.refs_1_), channel_id=1, source_target_pairs={{0,64},{64,128},{128,192},{192,256},{256,320},{320,384},{384,448},... | collective-permute-start | bytes 1769480 | tf_op jit(solution)/shard_map/ppermute | solution.py:216
  119.3 30.7 %copy-start.8 = (bf16[576,512]{1,0:T(8,128)(2,1)}, bf16[576,512]{1,0:T(8,128)(2,1)S(1)}, u32[]{:S(2)}) copy-start(bf16[576,512]{1,0:T(8,128)(2,1)S(1)} %collective-permute-done.5.refs_2_) | copy-start | bytes 1769476
  119.3 16.7 %collective-permute-start.7 = (bf16[576,512]{1,0:T(8,128)(2,1)S(1)}, bf16[576,512]{1,0:T(8,128)(2,1)}, u32[]{:S(2)}, u32[]{:S(2)}) collective-permute-start(bf16[576,512]{1,0:T(8,128)(2,1)S(1)} %collective-permute-done.5.refs_2_), channel_id=1, source_target_pairs={{0,448},{64,0},{128,64},{192,128},{256,192},{320,256},{384,320},{4... | collective-permute-start | bytes 1769480 | tf_op jit(solution)/shard_map/ppermute | solution.py:216
  134.1 15.9 %copy-start.9 = (bf16[576,512]{1,0:T(8,128)(2,1)}, bf16[576,512]{1,0:T(8,128)(2,1)S(1)}, u32[]{:S(2)}) copy-start(bf16[576,512]{1,0:T(8,128)(2,1)S(1)} %collective-permute-done.6.refs_3_) | copy-start | bytes 1769476
  134.1 15.9 %collective-permute-start.8 = (bf16[576,512]{1,0:T(8,128)(2,1)S(1)}, bf16[576,512]{1,0:T(8,128)(2,1)}, u32[]{:S(2)}, u32[]{:S(2)}) collective-permute-start(bf16[576,512]{1,0:T(8,128)(2,1)S(1)} %collective-permute-done.6.refs_3_), channel_id=1, source_target_pairs={{0,64},{64,128},{128,192},{192,256},{256,320},{320,384},{384,448},... | collective-permute-start | bytes 1769480 | tf_op jit(solution)/shard_map/ppermute | solution.py:216
  136.0 23.7 %collective-permute-start.9 = (bf16[576,512]{1,0:T(8,128)(2,1)}, bf16[576,512]{1,0:T(8,128)(2,1)}, u32[]{:S(2)}, u32[]{:S(2)}) collective-permute-start(bf16[576,512]{1,0:T(8,128)(2,1)} %collective-permute-done.7.refs_4_), channel_id=1, source_target_pairs={{0,448},{64,0},{128,64},{192,128},{256,192},{320,256},{384,320},{4... | collective-permute-start | bytes 1769480 | tf_op jit(solution)/shard_map/ppermute | solution.py:216
  150.0 15.2 %collective-permute-start.10 = (bf16[576,512]{1,0:T(8,128)(2,1)}, bf16[576,512]{1,0:T(8,128)(2,1)}, u32[]{:S(2)}, u32[]{:S(2)}) collective-permute-start(bf16[576,512]{1,0:T(8,128)(2,1)} %collective-permute-done.8.refs_5_), channel_id=1, source_target_pairs={{0,64},{64,128},{128,192},{192,256},{256,320},{320,384},{384,448},... | collective-permute-start | bytes 1769480 | tf_op jit(solution)/shard_map/ppermute | solution.py:216
  170.2 12.9 %copy-start.11 = (f32[1536]{0:T(1024)S(1)}, f32[1536]{0:T(1024)}, u32[]{:S(2)}) copy-start(f32[1536]{0:T(1024)} %param.14) | copy-start | bytes 18436
  170.2 55.5 %all-to-all-start.4 = ((bf16[32,240,128]{2,1,0:T(8,128)(2,1)}), bf16[32,240,128]{2,1,0:T(8,128)(2,1)S(1)}, u32[]{:S(2)}, u32[]{:S(2)}) async-start(bf16[32,240,128]{2,1,0:T(8,128)(2,1)} %far.1), calls=%async_computation.4 | async-start | bytes 3932160 | tf_op jit(solution)/shard_map/all_to_all | solution.py:262
  (4 other events, 4.6 us)

commit v2 on v0

--- a/solution.py
+++ b/solution.py
@@ -90,13 +90,16 @@
     out_ref[...] = y.reshape(16, CAP, 1536)
 
 
-def far_kernel(*refs):
-    x_refs, w_ref, out_refs, (wg_scr, wu_scr, wd_scr) = refs[0:8], refs[8], refs[9:17], refs[17:]
-    for z in range(8):
-        wg_scr[z * 192 : (z + 1) * 192, :] = w_ref[z, 0:192, :]
-        wu_scr[z * 192 : (z + 1) * 192, :] = w_ref[z, 192:384, :]
+def far_kernel(place_ref, *refs):
+    x_refs, w_refs, out_refs, (wg_scr, wu_scr, wd_scr) = refs[0:8], refs[8:16], refs[16:24], refs[24:]
+    tp = place_ref[4]
+    for ref, away in zip(w_refs, (0, -1, 1, -2, 2, -3, 3, -4)):
+        z = (tp + away + 8) % 8
+        wide, thin = pl.ds(pl.multiple_of(z * 192, 64), 192), pl.ds(pl.multiple_of(z * 64, 64), 64)
+        wg_scr[wide, :] = ref[0:192, :]
+        wu_scr[wide, :] = ref[192:384, :]
         for i in range(3):
-            wd_scr[z * 64 : (z + 1) * 64, i * 512 : (i + 1) * 512] = w_ref[z, 384 + i * 64 : 448 + i * 64, :]
+            wd_scr[thin, i * 512 : (i + 1) * 512] = ref[384 + i * 64 : 448 + i * 64, :]
     x = jnp.concatenate([ref[...] for ref in x_refs], axis=0)
     y = expert(x, wg_scr[...], wu_scr[...], wd_scr[...])
     for k in range(8):
@@ -131,6 +134,10 @@
 
 def vmem():
     return pl.BlockSpec(memory_space=pltpu.VMEM)
+
+
+def keep(value):
+    return pltpu.with_memory_space_constraint(value, pltpu.VMEM)
 
 
 def per_device(attn, resid, w_out, gain_mix, gain_out, routes, gates, w_gate, w_up, w_down):
@@ -157,10 +164,13 @@
         compiler_params=params(),
         name="piece",
     )(place, w_gate, w_up, w_down)
-    crossed = lax.ppermute(piece, ("h", "y"), [(4, 3), (3, 4)])
+    across = lambda v, a, b, c, d: lax.ppermute(v, ("h", "y"), [(a, b), (c, d)])
+    step_1 = across(piece, 4, 3, 3, 4)
+    step_3 = across(piece, 4, 1, 3, 6)
     columns = lax.all_to_all(jnp.broadcast_to(w_out.T[None], (64, 24, 192)), EP, 0, 0, tiled=True)
-    crossed, _ = lax.optimization_barrier((crossed, columns))
-    pieces = lax.all_gather(crossed, "y", axis=0, tiled=False)
+    columns, step_1, step_3 = lax.optimization_barrier((columns, step_1, step_3))
+    step_2 = across(step_1, 3, 2, 4, 5)
+    step_4 = across(step_3, 1, 0, 6, 7)
 
     parts = pl.pallas_call(
         project_kernel,
@@ -169,8 +179,14 @@
         out_specs=vmem(),
         compiler_params=params(),
         name="project",
-    )(place, attn.T, resid.T, columns)
+    )(place, attn.T, resid.T, keep(columns))
     parts = lax.all_to_all(parts, "tp", 0, 0, tiled=True)
+    far_piece = (step_1 + step_2) + (step_3 + step_4)
+    turn = lambda v, d: lax.ppermute(v, "tp", [(i, (i + d) % 8) for i in range(8)])
+    up, down = turn(far_piece, 1), turn(far_piece, -1)
+    parts, up, down = lax.optimization_barrier((parts, up, down))
+    ring = [far_piece, up, down]
+
     rows = shape((CAP, 1536), BF)
     send, hidden, *far = pl.pallas_call(
         mix_kernel,
@@ -179,16 +195,16 @@
         out_specs=(vmem(),) * 10,
         compiler_params=params(),
         name="mix",
-    )(place, parts, my_routes, gain_mix.reshape(1, 1536))
-
-    pieces, _ = lax.optimization_barrier((pieces, send))
-    far_piece = lax.dynamic_index_in_dim(pieces, 3 - 3 * h, 0, keepdims=False)
-    far_weights = lax.all_gather(far_piece, "tp", axis=0, tiled=False)
+    )(place, keep(parts), my_routes, gain_mix.reshape(1, 1536))
 
     shift = lambda v, k: lax.ppermute(v, ("x", "c"), [(i, (i + k) % 8) for i in range(8)])
     far = far[0:1] + [shift(far[k], k) for k in range(1, 8)]
     received = lax.all_to_all(send, ("y", "x", "c"), 0, 0, tiled=True)
-    received, far = lax.optimization_barrier((received, far))
+    for _ in range(2):
+        up, down = turn(up, 1), turn(down, -1)
+        ring += [up, down]
+    received, far, ring = lax.optimization_barrier((received, far, ring))
+    ring.append(turn(ring[5], 1))
 
     whole = lambda *dims: pl.BlockSpec(dims, lambda i: (0,) * len(dims))
     near = pl.pallas_call(
@@ -208,12 +224,12 @@
     far = pl.pallas_call(
         far_kernel,
         out_shape=(rows,) * 8,
-        in_specs=[vmem()] * 9,
+        in_specs=[smem()] + [vmem()] * 16,
         out_specs=(vmem(),) * 8,
         scratch_shapes=[pltpu.VMEM((1536, 512), BF), pltpu.VMEM((1536, 512), BF), pltpu.VMEM((512, 1536), BF)],
         compiler_params=params(),
         name="far",
-    )(*far, far_weights)
+    )(place, *far, *ring)
     near = lax.all_to_all(near, ("y", "x", "c"), 0, 0, tiled=True)
     far = [far[0]] + [shift(far[k], 8 - k) for k in range(1, 8)]
 
@@ -224,7 +240,7 @@
         out_specs=vmem(),
         compiler_params=params(),
         name="close",
-    )(place, my_routes, my_gates, hidden, gain_out.reshape(1, 1536), near, *far)
+    )(place, my_routes, my_gates, hidden, gain_out.reshape(1, 1536), keep(near), *far)
     return lax.all_to_all(finished, "tp", 0, 0, tiled=True).reshape(512, 192)
 
 

time: 242 us -> 265 us (1.095); the launches traced: 241 us -> 261 us
  starting transfers between devices: 74.3 us -> 114 us
  between operations: 13.9 us -> 0.6 us
  blocking collectives: 19.5 us -> 14.4 us
  local copies, waits for them, and re-layouts: 13.1 us -> 9.74 us
  waiting for transfers between devices: 96.3 us -> 99.1 us
    ppermute x1 -> x11, waiting for transfers between devices: 0.01 us -> 74.2 us  [the longest x4 37.3 us: per_device(): across = lambda v, a, b, c, d: lax.ppermute(v, ('h', 'y'), [(a, b), (c, d)])]
    all_to_all x1, waiting for transfers between devices: 36.8 us -> 0.01 us  [per_device(): parts = lax.all_to_all(parts, 'tp', 0, 0, tiled=True)]
    ppermute x1 -> x11, starting transfers between devices: 0.69 us -> 24.8 us  [the longest x7 21.4 us: per_device(): lax.ppermute(v, 'tp', [(i, (i + d) % 8) for i in range(8)])]
    all_gather x2 -> x0, waiting for transfers between devices: 17.3 us -> none  [the longest x1 14.5 us: per_device(): pieces = lax.all_gather(crossed, 'y', axis=0, tiled=False)]
    all_to_all x1, starting transfers between devices: 8.17 us -> 24.1 us  [per_device(): received = lax.all_to_all(send, ('y', 'x', 'c'), 0, 0, tiled=True)]
    all_to_all x1, waiting for transfers between devices: 13.4 us -> 0.01 us  [per_device(): received = lax.all_to_all(send, ('y', 'x', 'c'), 0, 0, tiled=True)]
    all_to_all x1, waiting for transfers between devices: 7.94 us -> 0.01 us  [per_device(): near = lax.all_to_all(near, ('y', 'x', 'c'), 0, 0, tiled=True)]
    all_to_all x1, blocking collectives: 19.5 us -> 14.4 us  [per_device(): return lax.all_to_all(finished, 'tp', 0, 0, tiled=True).reshape(512, 192)]
  transfers between devices with their start and end apart: 21 -> 29, of which waited for: 9 -> 9; matrix products, arithmetic and copies ran while one was open for 2% -> 2% of each run, Pallas kernels for 9% -> 3%
where the time goes in v2:
time: 265 us; the launch traced here: 261 us
  starting transfers between devices  114 us (43%)
  waiting for transfers between devices  99.1 us (37%)
  Pallas kernels  22.7 us (9%)
  blocking collectives  14.4 us (5%)
  local copies, waits for them, and re-layouts  9.74 us (4%)
    ppermute x14, starting transfers between devices, per_device(): lax.ppermute(v, ('x', 'c'), [(i, (i + k) % 8) for i in range(8)])  38.6 us
    ppermute x4, waiting for transfers between devices, per_device(): across = lambda v, a, b, c, d: lax.ppermute(v, ('h', 'y'), [(a, b), (c, d)])  37.3 us
    ppermute x7, waiting for transfers between devices, per_device(): lax.ppermute(v, 'tp', [(i, (i + d) % 8) for i in range(8)])  36.9 us
    all_to_all x1, starting transfers between devices, per_device(): received = lax.all_to_all(send, ('y', 'x', 'c'), 0, 0, tiled=True)  24.1 us
    ppermute x7, starting transfers between devices, per_device(): lax.ppermute(v, 'tp', [(i, (i + d) % 8) for i in range(8)])  21.4 us
    all_to_all x1, waiting for transfers between devices, per_device(): lax.all_to_all(jnp.broadcast_to(w_out.T[None], (64, 24, 192)), EP, 0, 0,...  17 us
    all_to_all x1, blocking collectives, per_device(): return lax.all_to_all(finished, 'tp', 0, 0, tiled=True).reshape(512, 192)  14.4 us
    all_to_all x1, starting transfers between devices, per_device(): lax.all_to_all(jnp.broadcast_to(w_out.T[None], (64, 24, 192)), EP, 0, 0,...  10.5 us
  transfers between devices with their start and end apart: 29, of which 9 were waited for; matrix products, arithmetic and copies ran while one was open for 2% of the time, Pallas kernels for 3%

profile of v2, /device:TPU:57, one launch (start us, length us, event | category | flops | bytes accessed | tf_op | source)
XLA Modules:
  0.0 260.6 jit_solution(7496768252250843820)
XLA Ops:
  1.7 10.5 %all-to-all-start = ((bf16[64,24,192]{2,1,0:T(8,128)(2,1)}), bf16[64,24,192]{2,1,0:T(8,128)(2,1)S(1)}, u32[]{:S(2)}, u32[]{:S(2)}) async-start(bf16[64,24,192]{2,1,0:T(8,128)(2,1)} %broadcast_in_dim.2), calls=%async_computation | async-start | bytes 1572864 | tf_op jit(solution)/shard_map/all_to_all | solution.py:170
  16.8 17.0 %all-to-all-done.w_ref = bf16[64,24,192]{2,1,0:T(8,128)(2,1)S(1)} async-done(((bf16[64,24,192]{2,1,0:T(8,128)(2,1)}), bf16[64,24,192]{2,1,0:T(8,128)(2,1)S(1)}, u32[]{:S(2)}, u32[]{:S(2)}) %all-to-all-start) | async-done | bytes 589856 | tf_op jit(solution)/shard_map/all_to_all | solution.py:170
  33.8 3.2 %project.1 = bf16[8,64,1536]{2,1,0:T(8,128)(2,1)} custom-call(s32[6]{0:T(128)} %stack.27.place_ref, bf16[192,512]{1,0:T(8,128)(2,1)} %bitcast.11, bf16[192,512]{1,0:T(8,128)(2,1)} %bitcast.12, bf16[64,24,192]{2,1,0:T(8,128)(2,1)S(1)} %all-to-all-done.w_ref), custom_call_target="tpu_custom_call" | custom-call | tf_op jit(solution)/shard_map/project/pallas_call | solution.py:175
  37.1 10.0 %all-to-all-start.1 = ((bf16[8,64,1536]{2,1,0:T(8,128)(2,1)}), bf16[8,64,1536]{2,1,0:T(8,128)(2,1)S(1)}, u32[]{:S(2)}, u32[]{:S(2)}) async-start(bf16[8,64,1536]{2,1,0:T(8,128)(2,1)} %project.1), calls=%async_computation.1 | async-start | bytes 3145728 | tf_op jit(solution)/shard_map/all_to_all | solution.py:183
  49.1 37.3 %collective-permute-done.3 = bf16[576,512]{1,0:T(8,128)(2,1)S(1)} collective-permute-done((bf16[576,512]{1,0:T(8,128)(2,1)S(1)}, bf16[576,512]{1,0:T(8,128)(2,1)S(1)}, u32[]{:S(2)}, u32[]{:S(2)}) %collective-permute-start.3) | collective-permute-done | bytes 589856 | tf_op jit(solution)/shard_map/ppermute | solution.py:167
  86.6 3.2 %collective-permute-start.4 = (bf16[576,512]{1,0:T(8,128)(2,1)S(1)}, bf16[576,512]{1,0:T(8,128)(2,1)S(1)}, u32[]{:S(2)}, u32[]{:S(2)}) collective-permute-start(bf16[576,512]{1,0:T(8,128)(2,1)S(1)} %add_add_fusion.refs_8_), channel_id=1, source_target_pairs={{0,64},{64,128},{128,192},{192,256},{256,320},{320,384},{384,448},... | collective-permute-start | bytes 1769480 | tf_op jit(solution)/shard_map/ppermute | solution.py:185
  89.8 3.3 %collective-permute-start.5 = (bf16[576,512]{1,0:T(8,128)(2,1)S(1)}, bf16[576,512]{1,0:T(8,128)(2,1)S(1)}, u32[]{:S(2)}, u32[]{:S(2)}) collective-permute-start(bf16[576,512]{1,0:T(8,128)(2,1)S(1)} %add_add_fusion.refs_8_), channel_id=1, source_target_pairs={{0,448},{64,0},{128,64},{192,128},{256,192},{320,256},{384,320},{4... | collective-permute-start | bytes 1769480 | tf_op jit(solution)/shard_map/ppermute | solution.py:185
  94.5 8.7 %collective-permute-done.4.refs_9_ = bf16[576,512]{1,0:T(8,128)(2,1)S(1)} collective-permute-done((bf16[576,512]{1,0:T(8,128)(2,1)S(1)}, bf16[576,512]{1,0:T(8,128)(2,1)S(1)}, u32[]{:S(2)}, u32[]{:S(2)}) %collective-permute-start.4) | collective-permute-done | bytes 589856 | tf_op jit(solution)/shard_map/ppermute | solution.py:185
  104.5 3.2 %mix.1 = (bf16[32,16,1536]{2,1,0:T(8,128)(2,1)}, f32[64,1536]{1,0:T(8,128)}, bf16[16,1536]{1,0:T(8,128)(2,1)}, bf16[16,1536]{1,0:T(8,128)(2,1)}, bf16[16,1536]{1...) custom-call(s32[6]{0:T(128)} %stack.27.place_ref, ...), custom_call_target="tpu_custom_call" | custom-call | tf_op jit(solution)/shard_map/mix/pallas_call | solution.py:191
  107.7 24.1 %all-to-all-start.2 = ((bf16[32,16,1536]{2,1,0:T(8,128)(2,1)}), bf16[32,16,1536]{2,1,0:T(8,128)(2,1)S(1)}, u32[]{:S(2)}, u32[]{:S(2)}) async-start(bf16[32,16,1536]{2,1,0:T(8,128)(2,1)} %get-tuple-element.50), calls=%async_computation.2 | async-start | bytes 3145728 | tf_op jit(solution)/shard_map/all_to_all | solution.py:202
  133.7 4.6 %collective-permute-start.14 = (bf16[576,512]{1,0:T(8,128)(2,1)S(1)}, bf16[576,512]{1,0:T(8,128)(2,1)S(1)}, u32[]{:S(2)}, u32[]{:S(2)}) collective-permute-start(bf16[576,512]{1,0:T(8,128)(2,1)S(1)} %collective-permute-done.5.refs_10_), channel_id=1, source_target_pairs={{0,448},{64,0},{128,64},{192,128},{256,192},{320,256},{384,320},{4... | collective-permute-start | bytes 1769480 | tf_op jit(solution)/shard_map/ppermute | solution.py:185
  138.3 11.1 %collective-permute-done.13.refs_11_ = bf16[576,512]{1,0:T(8,128)(2,1)S(1)} collective-permute-done((bf16[576,512]{1,0:T(8,128)(2,1)S(1)}, bf16[576,512]{1,0:T(8,128)(2,1)S(1)}, u32[]{:S(2)}, u32[]{:S(2)}) %collective-permute-start.13) | collective-permute-done | bytes 589856 | tf_op jit(solution)/shard_map/ppermute | solution.py:185
  151.4 4.6 %collective-permute-start.16 = (bf16[576,512]{1,0:T(8,128)(2,1)S(1)}, bf16[576,512]{1,0:T(8,128)(2,1)S(1)}, u32[]{:S(2)}, u32[]{:S(2)}) collective-permute-start(bf16[576,512]{1,0:T(8,128)(2,1)S(1)} %collective-permute-done.14.refs_12_), channel_id=1, source_target_pairs={{0,448},{64,0},{128,64},{192,128},{256,192},{320,256},{384,320},{4... | collective-permute-start | bytes 1769480 | tf_op jit(solution)/shard_map/ppermute | solution.py:185
  156.0 6.0 %collective-permute-start.10 = (bf16[16,1536]{1,0:T(8,128)(2,1)S(1)}, bf16[16,1536]{1,0:T(8,128)(2,1)S(1)}, u32[]{:S(2)}, u32[]{:S(2)}) collective-permute-start(bf16[16,1536]{1,0:T(8,128)(2,1)S(1)} %copy-done.26), channel_id=1, source_target_pairs={{0,5},{1,6},{2,7},{3,0},{4,1},{5,2},{6,3},{7,4},{8,13},{9,14},{10,... | collective-permute-start | bytes 147464 | tf_op jit(solution)/shard_map/ppermute | solution.py:200
  169.8 5.9 %collective-permute-start.8 = (bf16[16,1536]{1,0:T(8,128)(2,1)}, bf16[16,1536]{1,0:T(8,128)(2,1)S(1)}, u32[]{:S(2)}, u32[]{:S(2)}) collective-permute-start(bf16[16,1536]{1,0:T(8,128)(2,1)} %get-tuple-element.54), channel_id=1, source_target_pairs={{0,3},{1,4},{2,5},{3,6},{4,7},{5,0},{6,1},{7,2},{8,11},{9,12},{10,... | collective-permute-start | bytes 147464 | tf_op jit(solution)/shard_map/ppermute | solution.py:200
  177.7 4.6 %collective-permute-done.9.refs_4_ = bf16[16,1536]{1,0:T(8,128)(2,1)S(1)} collective-permute-done((bf16[16,1536]{1,0:T(8,128)(2,1)}, bf16[16,1536]{1,0:T(8,128)(2,1)S(1)}, u32[]{:S(2)}, u32[]{:S(2)}) %collective-permute-start.9) | collective-permute-done | bytes 49184 | tf_op jit(solution)/shard_map/ppermute | solution.py:200
  184.1 6.5 %near.1 = bf16[32,16,1536]{2,1,0:T(8,128)(2,1)} custom-call(bf16[32,16,1536]{2,1,0:T(8,128)(2,1)} %copy-done.1, bf16[1,1536,512]{2,1,0:T(8,128)(2,1)} %wg_ref.3, bf16[1,1536,512]{2,1,0:T(8,128)(2,1)} %wu_ref.3, bf16[1,512,1536]{2,1,0:T(8,128)(2,1)} %wd_ref.3), custom_call_target="tpu_custom_call" | custom-call | tf_op jit(solution)/shard_map/near/pallas_call | solution.py:210
  190.6 6.1 %all-to-all-start.3 = ((bf16[32,16,1536]{2,1,0:T(8,128)(2,1)}), bf16[32,16,1536]{2,1,0:T(8,128)(2,1)S(1)}, u32[]{:S(2)}, u32[]{:S(2)}) async-start(bf16[32,16,1536]{2,1,0:T(8,128)(2,1)} %near.1), calls=%async_computation.3 | async-start | bytes 3145728 | tf_op jit(solution)/shard_map/all_to_all | solution.py:233
  198.6 15.7 %collective-permute-done.17.refs_15_ = bf16[576,512]{1,0:T(8,128)(2,1)S(1)} collective-permute-done((bf16[576,512]{1,0:T(8,128)(2,1)S(1)}, bf16[576,512]{1,0:T(8,128)(2,1)S(1)}, u32[]{:S(2)}, u32[]{:S(2)}) %collective-permute-start.17) | collective-permute-done | bytes 589856 | tf_op jit(solution)/shard_map/ppermute | solution.py:185
  215.2 4.4 %far.1 = (bf16[16,1536]{1,0:T(8,128)(2,1)}, bf16[16,1536]{1,0:T(8,128)(2,1)}, bf16[16,1536]{1,0:T(8,128)(2,1)}, bf16[16,1536]{1,0:T(8,128)(2,1)}, bf16[16,1536]{...) custom-call(s32[6]{0:T(128)} %stack.27.place_ref, ...), custom_call_target="tpu_custom_call" | custom-call | tf_op jit(solution)/shard_map/far/pallas_call | solution.py:224
  220.7 4.3 %collective-permute-start.19 = (bf16[16,1536]{1,0:T(8,128)(2,1)}, bf16[16,1536]{1,0:T(8,128)(2,1)S(1)}, u32[]{:S(2)}, u32[]{:S(2)}) collective-permute-start(bf16[16,1536]{1,0:T(8,128)(2,1)} %get-tuple-element.79), channel_id=1, source_target_pairs={{0,6},{1,7},{2,0},{3,1},{4,2},{5,3},{6,4},{7,5},{8,14},{9,15},{10,... | collective-permute-start | bytes 147464 | tf_op jit(solution)/shard_map/ppermute | solution.py:200
  227.7 3.8 %collective-permute-start.21 = (bf16[16,1536]{1,0:T(8,128)(2,1)}, bf16[16,1536]{1,0:T(8,128)(2,1)S(1)}, u32[]{:S(2)}, u32[]{:S(2)}) collective-permute-start(bf16[16,1536]{1,0:T(8,128)(2,1)} %get-tuple-element.81), channel_id=1, source_target_pairs={{0,4},{1,5},{2,6},{3,7},{4,0},{5,1},{6,2},{7,3},{8,12},{9,13},{10,... | collective-permute-start | bytes 147464 | tf_op jit(solution)/shard_map/ppermute | solution.py:200
  231.5 3.4 %collective-permute-start.22 = (bf16[16,1536]{1,0:T(8,128)(2,1)}, bf16[16,1536]{1,0:T(8,128)(2,1)S(1)}, u32[]{:S(2)}, u32[]{:S(2)}) collective-permute-start(bf16[16,1536]{1,0:T(8,128)(2,1)} %get-tuple-element.82), channel_id=1, source_target_pairs={{0,3},{1,4},{2,5},{3,6},{4,7},{5,0},{6,1},{7,2},{8,11},{9,12},{10,... | collective-permute-start | bytes 147464 | tf_op jit(solution)/shard_map/ppermute | solution.py:200
  245.4 14.4 %all_to_all.25 = bf16[8,64,192]{2,1,0:T(8,128)(2,1)S(1)} all-to-all(bf16[8,64,192]{2,1,0:T(8,128)(2,1)} %close.1), channel_id=1, replica_groups=mesh['tp'=8,'h'=2,'y'=4,'x'=4,'c'=2] {'tp'}, dimensions={0} | all-to-all | bytes 393216 | tf_op jit(solution)/shard_map/all_to_all | solution.py:244
  (105 shorter events, 44.4 us)
Async XLA Ops:
  1.7 32.1 %all-to-all-start = ((bf16[64,24,192]{2,1,0:T(8,128)(2,1)}), bf16[64,24,192]{2,1,0:T(8,128)(2,1)S(1)}, u32[]{:S(2)}, u32[]{:S(2)}) async-start(bf16[64,24,192]{2,1,0:T(8,128)(2,1)} %broadcast_in_dim.2), calls=%async_computation | async-start | bytes 1572864 | tf_op jit(solution)/shard_map/all_to_all | solution.py:170
  37.1 67.5 %all-to-all-start.1 = ((bf16[8,64,1536]{2,1,0:T(8,128)(2,1)}), bf16[8,64,1536]{2,1,0:T(8,128)(2,1)S(1)}, u32[]{:S(2)}, u32[]{:S(2)}) async-start(bf16[8,64,1536]{2,1,0:T(8,128)(2,1)} %project.1), calls=%async_computation.1 | async-start | bytes 3145728 | tf_op jit(solution)/shard_map/all_to_all | solution.py:183
  47.8 38.6 %collective-permute-start.3 = (bf16[576,512]{1,0:T(8,128)(2,1)S(1)}, bf16[576,512]{1,0:T(8,128)(2,1)S(1)}, u32[]{:S(2)}, u32[]{:S(2)}) collective-permute-start(bf16[576,512]{1,0:T(8,128)(2,1)S(1)} %collective-permute-done.1), channel_id=1, source_target_pairs={{8,0},{48,56},{9,1},{49,57},{10,2},{50,58},{11,3},{51,59},{12,4},{... | collective-permute-start | bytes 1769480 | tf_op jit(solution)/shard_map/ppermute | solution.py:167
  86.6 16.5 %collective-permute-start.4 = (bf16[576,512]{1,0:T(8,128)(2,1)S(1)}, bf16[576,512]{1,0:T(8,128)(2,1)S(1)}, u32[]{:S(2)}, u32[]{:S(2)}) collective-permute-start(bf16[576,512]{1,0:T(8,128)(2,1)S(1)} %add_add_fusion.refs_8_), channel_id=1, source_target_pairs={{0,64},{64,128},{128,192},{192,256},{256,320},{320,384},{384,448},... | collective-permute-start | bytes 1769480 | tf_op jit(solution)/shard_map/ppermute | solution.py:185
  89.8 14.7 %collective-permute-start.5 = (bf16[576,512]{1,0:T(8,128)(2,1)S(1)}, bf16[576,512]{1,0:T(8,128)(2,1)S(1)}, u32[]{:S(2)}, u32[]{:S(2)}) collective-permute-start(bf16[576,512]{1,0:T(8,128)(2,1)S(1)} %add_add_fusion.refs_8_), channel_id=1, source_target_pairs={{0,448},{64,0},{128,64},{192,128},{256,192},{320,256},{384,320},{4... | collective-permute-start | bytes 1769480 | tf_op jit(solution)/shard_map/ppermute | solution.py:185
  107.7 75.2 %all-to-all-start.2 = ((bf16[32,16,1536]{2,1,0:T(8,128)(2,1)}), bf16[32,16,1536]{2,1,0:T(8,128)(2,1)S(1)}, u32[]{:S(2)}, u32[]{:S(2)}) async-start(bf16[32,16,1536]{2,1,0:T(8,128)(2,1)} %get-tuple-element.50), calls=%async_computation.2 | async-start | bytes 3145728 | tf_op jit(solution)/shard_map/all_to_all | solution.py:202
  131.8 17.7 %collective-permute-start.13 = (bf16[576,512]{1,0:T(8,128)(2,1)S(1)}, bf16[576,512]{1,0:T(8,128)(2,1)S(1)}, u32[]{:S(2)}, u32[]{:S(2)}) collective-permute-start(bf16[576,512]{1,0:T(8,128)(2,1)S(1)} %collective-permute-done.4.refs_9_), channel_id=1, source_target_pairs={{0,64},{64,128},{128,192},{192,256},{256,320},{320,384},{384,448},... | collective-permute-start | bytes 1769480 | tf_op jit(solution)/shard_map/ppermute | solution.py:185
  133.7 17.6 %collective-permute-start.14 = (bf16[576,512]{1,0:T(8,128)(2,1)S(1)}, bf16[576,512]{1,0:T(8,128)(2,1)S(1)}, u32[]{:S(2)}, u32[]{:S(2)}) collective-permute-start(bf16[576,512]{1,0:T(8,128)(2,1)S(1)} %collective-permute-done.5.refs_10_), channel_id=1, source_target_pairs={{0,448},{64,0},{128,64},{192,128},{256,192},{320,256},{384,320},{4... | collective-permute-start | bytes 1769480 | tf_op jit(solution)/shard_map/ppermute | solution.py:185
  149.5 32.8 %collective-permute-start.15 = (bf16[576,512]{1,0:T(8,128)(2,1)S(1)}, bf16[576,512]{1,0:T(8,128)(2,1)S(1)}, u32[]{:S(2)}, u32[]{:S(2)}) collective-permute-start(bf16[576,512]{1,0:T(8,128)(2,1)S(1)} %collective-permute-done.13.refs_11_), channel_id=1, source_target_pairs={{0,64},{64,128},{128,192},{192,256},{256,320},{320,384},{384,448},... | collective-permute-start | bytes 1769480 | tf_op jit(solution)/shard_map/ppermute | solution.py:185
  151.4 31.5 %collective-permute-start.16 = (bf16[576,512]{1,0:T(8,128)(2,1)S(1)}, bf16[576,512]{1,0:T(8,128)(2,1)S(1)}, u32[]{:S(2)}, u32[]{:S(2)}) collective-permute-start(bf16[576,512]{1,0:T(8,128)(2,1)S(1)} %collective-permute-done.14.refs_12_), channel_id=1, source_target_pairs={{0,448},{64,0},{128,64},{192,128},{256,192},{320,256},{384,320},{4... | collective-permute-start | bytes 1769480 | tf_op jit(solution)/shard_map/ppermute | solution.py:185
  156.0 8.5 %collective-permute-start.10 = (bf16[16,1536]{1,0:T(8,128)(2,1)S(1)}, bf16[16,1536]{1,0:T(8,128)(2,1)S(1)}, u32[]{:S(2)}, u32[]{:S(2)}) collective-permute-start(bf16[16,1536]{1,0:T(8,128)(2,1)S(1)} %copy-done.26), channel_id=1, source_target_pairs={{0,5},{1,6},{2,7},{3,0},{4,1},{5,2},{6,3},{7,4},{8,13},{9,14},{10,... | collective-permute-start | bytes 147464 | tf_op jit(solution)/shard_map/ppermute | solution.py:200
  162.0 5.9 %collective-permute-start.11 = (bf16[16,1536]{1,0:T(8,128)(2,1)}, bf16[16,1536]{1,0:T(8,128)(2,1)S(1)}, u32[]{:S(2)}, u32[]{:S(2)}) collective-permute-start(bf16[16,1536]{1,0:T(8,128)(2,1)} %get-tuple-element.57), channel_id=1, source_target_pairs={{0,6},{1,7},{2,0},{3,1},{4,2},{5,3},{6,4},{7,5},{8,14},{9,15},{10,... | collective-permute-start | bytes 147464 | tf_op jit(solution)/shard_map/ppermute | solution.py:200
  164.5 11.2 %collective-permute-start.6 = (bf16[16,1536]{1,0:T(8,128)(2,1)}, bf16[16,1536]{1,0:T(8,128)(2,1)S(1)}, u32[]{:S(2)}, u32[]{:S(2)}) collective-permute-start(bf16[16,1536]{1,0:T(8,128)(2,1)} %get-tuple-element.52), channel_id=1, source_target_pairs={{0,1},{1,2},{2,3},{3,4},{4,5},{5,6},{6,7},{7,0},{8,9},{9,10},{10,1... | collective-permute-start | bytes 147464 | tf_op jit(solution)/shard_map/ppermute | solution.py:200
  167.9 9.8 %collective-permute-start.7 = (bf16[16,1536]{1,0:T(8,128)(2,1)}, bf16[16,1536]{1,0:T(8,128)(2,1)S(1)}, u32[]{:S(2)}, u32[]{:S(2)}) collective-permute-start(bf16[16,1536]{1,0:T(8,128)(2,1)} %get-tuple-element.53), channel_id=1, source_target_pairs={{0,2},{1,3},{2,4},{3,5},{4,6},{5,7},{6,0},{7,1},{8,10},{9,11},{10,... | collective-permute-start | bytes 147464 | tf_op jit(solution)/shard_map/ppermute | solution.py:200
  169.8 7.9 %collective-permute-start.8 = (bf16[16,1536]{1,0:T(8,128)(2,1)}, bf16[16,1536]{1,0:T(8,128)(2,1)S(1)}, u32[]{:S(2)}, u32[]{:S(2)}) collective-permute-start(bf16[16,1536]{1,0:T(8,128)(2,1)} %get-tuple-element.54), channel_id=1, source_target_pairs={{0,3},{1,4},{2,5},{3,6},{4,7},{5,0},{6,1},{7,2},{8,11},{9,12},{10,... | collective-permute-start | bytes 147464 | tf_op jit(solution)/shard_map/ppermute | solution.py:200
  175.7 6.5 %collective-permute-start.9 = (bf16[16,1536]{1,0:T(8,128)(2,1)}, bf16[16,1536]{1,0:T(8,128)(2,1)S(1)}, u32[]{:S(2)}, u32[]{:S(2)}) collective-permute-start(bf16[16,1536]{1,0:T(8,128)(2,1)} %get-tuple-element.55), channel_id=1, source_target_pairs={{0,4},{1,5},{2,6},{3,7},{4,0},{5,1},{6,2},{7,3},{8,12},{9,13},{10,... | collective-permute-start | bytes 147464 | tf_op jit(solution)/shard_map/ppermute | solution.py:200
  190.6 51.4 %all-to-all-start.3 = ((bf16[32,16,1536]{2,1,0:T(8,128)(2,1)}), bf16[32,16,1536]{2,1,0:T(8,128)(2,1)S(1)}, u32[]{:S(2)}, u32[]{:S(2)}) async-start(bf16[32,16,1536]{2,1,0:T(8,128)(2,1)} %near.1), calls=%async_computation.3 | async-start | bytes 3145728 | tf_op jit(solution)/shard_map/all_to_all | solution.py:233
  196.7 17.7 %collective-permute-start.17 = (bf16[576,512]{1,0:T(8,128)(2,1)S(1)}, bf16[576,512]{1,0:T(8,128)(2,1)S(1)}, u32[]{:S(2)}, u32[]{:S(2)}) collective-permute-start(bf16[576,512]{1,0:T(8,128)(2,1)S(1)} %collective-permute-done.15.refs_13_), channel_id=1, source_target_pairs={{0,64},{64,128},{128,192},{192,256},{256,320},{320,384},{384,448},... | collective-permute-start | bytes 1769480 | tf_op jit(solution)/shard_map/ppermute | solution.py:185
  219.5 15.4 %collective-permute-start.18 = (bf16[16,1536]{1,0:T(8,128)(2,1)}, bf16[16,1536]{1,0:T(8,128)(2,1)S(1)}, u32[]{:S(2)}, u32[]{:S(2)}) collective-permute-start(bf16[16,1536]{1,0:T(8,128)(2,1)} %get-tuple-element.78), channel_id=1, source_target_pairs={{0,7},{1,0},{2,1},{3,2},{4,3},{5,4},{6,5},{7,6},{8,15},{9,8},{10,9... | collective-permute-start | bytes 147464 | tf_op jit(solution)/shard_map/ppermute | solution.py:200
  220.7 16.7 %collective-permute-start.19 = (bf16[16,1536]{1,0:T(8,128)(2,1)}, bf16[16,1536]{1,0:T(8,128)(2,1)S(1)}, u32[]{:S(2)}, u32[]{:S(2)}) collective-permute-start(bf16[16,1536]{1,0:T(8,128)(2,1)} %get-tuple-element.79), channel_id=1, source_target_pairs={{0,6},{1,7},{2,0},{3,1},{4,2},{5,3},{6,4},{7,5},{8,14},{9,15},{10,... | collective-permute-start | bytes 147464 | tf_op jit(solution)/shard_map/ppermute | solution.py:200
  225.1 15.2 %collective-permute-start.20 = (bf16[16,1536]{1,0:T(8,128)(2,1)}, bf16[16,1536]{1,0:T(8,128)(2,1)S(1)}, u32[]{:S(2)}, u32[]{:S(2)}) collective-permute-start(bf16[16,1536]{1,0:T(8,128)(2,1)} %get-tuple-element.80), channel_id=1, source_target_pairs={{0,5},{1,6},{2,7},{3,0},{4,1},{5,2},{6,3},{7,4},{8,13},{9,14},{10,... | collective-permute-start | bytes 147464 | tf_op jit(solution)/shard_map/ppermute | solution.py:200
  227.7 12.6 %collective-permute-start.21 = (bf16[16,1536]{1,0:T(8,128)(2,1)}, bf16[16,1536]{1,0:T(8,128)(2,1)S(1)}, u32[]{:S(2)}, u32[]{:S(2)}) collective-permute-start(bf16[16,1536]{1,0:T(8,128)(2,1)} %get-tuple-element.81), channel_id=1, source_target_pairs={{0,4},{1,5},{2,6},{3,7},{4,0},{5,1},{6,2},{7,3},{8,12},{9,13},{10,... | collective-permute-start | bytes 147464 | tf_op jit(solution)/shard_map/ppermute | solution.py:200
  231.5 8.8 %collective-permute-start.22 = (bf16[16,1536]{1,0:T(8,128)(2,1)}, bf16[16,1536]{1,0:T(8,128)(2,1)S(1)}, u32[]{:S(2)}, u32[]{:S(2)}) collective-permute-start(bf16[16,1536]{1,0:T(8,128)(2,1)} %get-tuple-element.82), channel_id=1, source_target_pairs={{0,3},{1,4},{2,5},{3,6},{4,7},{5,0},{6,1},{7,2},{8,11},{9,12},{10,... | collective-permute-start | bytes 147464 | tf_op jit(solution)/shard_map/ppermute | solution.py:200
  234.9 7.0 %collective-permute-start.23 = (bf16[16,1536]{1,0:T(8,128)(2,1)}, bf16[16,1536]{1,0:T(8,128)(2,1)S(1)}, u32[]{:S(2)}, u32[]{:S(2)}) collective-permute-start(bf16[16,1536]{1,0:T(8,128)(2,1)} %get-tuple-element.83), channel_id=1, source_target_pairs={{0,2},{1,3},{2,4},{3,5},{4,6},{5,7},{6,0},{7,1},{8,10},{9,11},{10,... | collective-permute-start | bytes 147464 | tf_op jit(solution)/shard_map/ppermute | solution.py:200
  (32 other events, 531.6 us)

commit v3 on v0

--- a/solution.py
+++ b/solution.py
@@ -131,6 +131,10 @@
 
 def vmem():
     return pl.BlockSpec(memory_space=pltpu.VMEM)
+
+
+def keep(value):
+    return pltpu.with_memory_space_constraint(value, pltpu.VMEM)
 
 
 def per_device(attn, resid, w_out, gain_mix, gain_out, routes, gates, w_gate, w_up, w_down):
@@ -157,10 +161,13 @@
         compiler_params=params(),
         name="piece",
     )(place, w_gate, w_up, w_down)
-    crossed = lax.ppermute(piece, ("h", "y"), [(4, 3), (3, 4)])
+    across = lambda v, a, b, c, d: lax.ppermute(v, ("h", "y"), [(a, b), (c, d)])
+    step_1 = across(piece, 4, 3, 3, 4)
+    step_3 = across(piece, 4, 1, 3, 6)
     columns = lax.all_to_all(jnp.broadcast_to(w_out.T[None], (64, 24, 192)), EP, 0, 0, tiled=True)
-    crossed, _ = lax.optimization_barrier((crossed, columns))
-    pieces = lax.all_gather(crossed, "y", axis=0, tiled=False)
+    columns, step_1, step_3 = lax.optimization_barrier((columns, step_1, step_3))
+    step_2 = across(step_1, 3, 2, 4, 5)
+    step_4 = across(step_3, 1, 0, 6, 7)
 
     parts = pl.pallas_call(
         project_kernel,
@@ -169,8 +176,12 @@
         out_specs=vmem(),
         compiler_params=params(),
         name="project",
-    )(place, attn.T, resid.T, columns)
+    )(place, attn.T, resid.T, keep(columns))
     parts = lax.all_to_all(parts, "tp", 0, 0, tiled=True)
+    far_piece = (step_1 + step_2) + (step_3 + step_4)
+    parts, far_piece = lax.optimization_barrier((parts, far_piece))
+    far_weights = lax.all_gather(far_piece, "tp", axis=0, tiled=False)
+
     rows = shape((CAP, 1536), BF)
     send, hidden, *far = pl.pallas_call(
         mix_kernel,
@@ -179,11 +190,7 @@
         out_specs=(vmem(),) * 10,
         compiler_params=params(),
         name="mix",
-    )(place, parts, my_routes, gain_mix.reshape(1, 1536))
-
-    pieces, _ = lax.optimization_barrier((pieces, send))
-    far_piece = lax.dynamic_index_in_dim(pieces, 3 - 3 * h, 0, keepdims=False)
-    far_weights = lax.all_gather(far_piece, "tp", axis=0, tiled=False)
+    )(place, keep(parts), my_routes, gain_mix.reshape(1, 1536))
 
     shift = lambda v, k: lax.ppermute(v, ("x", "c"), [(i, (i + k) % 8) for i in range(8)])
     far = far[0:1] + [shift(far[k], k) for k in range(1, 8)]
@@ -224,7 +231,7 @@
         out_specs=vmem(),
         compiler_params=params(),
         name="close",
-    )(place, my_routes, my_gates, hidden, gain_out.reshape(1, 1536), near, *far)
+    )(place, my_routes, my_gates, hidden, gain_out.reshape(1, 1536), keep(near), *far)
     return lax.all_to_all(finished, "tp", 0, 0, tiled=True).reshape(512, 192)
 
 

time: 242 us -> 247 us (1.021); the launches traced: 241 us -> 243 us
  starting transfers between devices: 74.3 us -> 97.6 us
  waiting for transfers between devices: 96.3 us -> 83.9 us
  local copies, waits for them, and re-layouts: 13.1 us -> 8.43 us
  blocking collectives: 19.5 us -> 15.7 us
    ppermute x1 -> x4, waiting for transfers between devices: 0.01 us -> 37.3 us  [per_device(): across = lambda v, a, b, c, d: lax.ppermute(v, ('h', 'y'), [(a, b), (c, d)])]
    all_to_all x1, waiting for transfers between devices: 36.8 us -> 0.01 us  [per_device(): parts = lax.all_to_all(parts, 'tp', 0, 0, tiled=True)]
    all_to_all x1, starting transfers between devices: 8.17 us -> 31.2 us  [per_device(): received = lax.all_to_all(send, ('y', 'x', 'c'), 0, 0, tiled=True)]
    all_gather x1 -> x0, waiting for transfers between devices: 14.5 us -> none  [per_device(): pieces = lax.all_gather(crossed, 'y', axis=0, tiled=False)]
    all_to_all x1, blocking collectives: 19.5 us -> 15.7 us  [per_device(): return lax.all_to_all(finished, 'tp', 0, 0, tiled=True).reshape(512, 192)]
    all_gather x1, waiting for transfers between devices: 2.78 us -> 0.02 us  [per_device(): far_weights = lax.all_gather(far_piece, 'tp', axis=0, tiled=False)]
    all_to_all x1, waiting for transfers between devices: 7.94 us -> 10.7 us  [per_device(): near = lax.all_to_all(near, ('y', 'x', 'c'), 0, 0, tiled=True)]
    ppermute x1 -> x4, starting transfers between devices: 0.69 us -> 3.38 us  [per_device(): across = lambda v, a, b, c, d: lax.ppermute(v, ('h', 'y'), [(a, b), (c, d)])]
  transfers between devices with their start and end apart: 21 -> 23, of which waited for: 9 -> 8; matrix products, arithmetic and copies ran while one was open for 2% -> 2% of each run, Pallas kernels for 9% -> 7%
where the time goes in v3:
time: 247 us; the launch traced here: 243 us
  starting transfers between devices  97.6 us (40%)
  waiting for transfers between devices  83.9 us (34%)
  Pallas kernels  22.6 us (9%)
  blocking collectives  15.7 us (6%)
  between operations  13.9 us (6%)
  local copies, waits for them, and re-layouts  8.43 us (3%)
    ppermute x4, waiting for transfers between devices, per_device(): across = lambda v, a, b, c, d: lax.ppermute(v, ('h', 'y'), [(a, b), (c, d)])  37.3 us
    ppermute x14, starting transfers between devices, per_device(): lax.ppermute(v, ('x', 'c'), [(i, (i + k) % 8) for i in range(8)])  34.8 us
    all_to_all x1, starting transfers between devices, per_device(): received = lax.all_to_all(send, ('y', 'x', 'c'), 0, 0, tiled=True)  31.2 us
    all_to_all x1, waiting for transfers between devices, per_device(): lax.all_to_all(jnp.broadcast_to(w_out.T[None], (64, 24, 192)), EP, 0, 0,...  17 us
    all_to_all x1, blocking collectives, per_device(): return lax.all_to_all(finished, 'tp', 0, 0, tiled=True).reshape(512, 192)  15.7 us
    all_to_all x1, waiting for transfers between devices, per_device(): received = lax.all_to_all(send, ('y', 'x', 'c'), 0, 0, tiled=True)  13 us
    all_to_all x1, waiting for transfers between devices, per_device(): near = lax.all_to_all(near, ('y', 'x', 'c'), 0, 0, tiled=True)  10.7 us
    all_to_all x1, starting transfers between devices, per_device(): lax.all_to_all(jnp.broadcast_to(w_out.T[None], (64, 24, 192)), EP, 0, 0,...  10.5 us
  transfers between devices with their start and end apart: 23, of which 8 were waited for; matrix products, arithmetic and copies ran while one was open for 2% of the time, Pallas kernels for 7%

profile of v3, /device:TPU:57, one launch (start us, length us, event | category | flops | bytes accessed | tf_op | source)
XLA Modules:
  0.0 243.1 jit_solution(4720648279261110437)
XLA Ops:
  8.2 10.5 %all-to-all-start = ((bf16[64,24,192]{2,1,0:T(8,128)(2,1)}), bf16[64,24,192]{2,1,0:T(8,128)(2,1)S(1)}, u32[]{:S(2)}, u32[]{:S(2)}) async-start(bf16[64,24,192]{2,1,0:T(8,128)(2,1)} %broadcast_in_dim.2), calls=%async_computation | async-start | bytes 1572864 | tf_op jit(solution)/shard_map/all_to_all | solution.py:167
  19.3 2.6 %piece.1 = bf16[576,512]{1,0:T(8,128)(2,1)} custom-call(s32[6]{0:T(128)} %stack.27.place_ref, bf16[1,1536,512]{2,1,0:T(8,128)(2,1)} %wg_ref.3, bf16[1,1536,512]{2,1,0:T(8,128)(2,1)} %wu_ref.3, bf16[1,512,1536]{2,1,0:T(8,128)(2,1)} %wd_ref.3), custom_call_target="tpu_custom_call" | custom-call | tf_op jit(solution)/shard_map/piece/pallas_call | solution.py:148
  23.4 17.0 %all-to-all-done.w_ref = bf16[64,24,192]{2,1,0:T(8,128)(2,1)S(1)} async-done(((bf16[64,24,192]{2,1,0:T(8,128)(2,1)}), bf16[64,24,192]{2,1,0:T(8,128)(2,1)S(1)}, u32[]{:S(2)}, u32[]{:S(2)}) %all-to-all-start) | async-done | bytes 589856 | tf_op jit(solution)/shard_map/all_to_all | solution.py:167
  40.3 3.2 %project.1 = bf16[8,64,1536]{2,1,0:T(8,128)(2,1)} custom-call(s32[6]{0:T(128)} %stack.27.place_ref, bf16[192,512]{1,0:T(8,128)(2,1)} %bitcast.13, bf16[192,512]{1,0:T(8,128)(2,1)} %bitcast.14, bf16[64,24,192]{2,1,0:T(8,128)(2,1)S(1)} %all-to-all-done.w_ref), custom_call_target="tpu_custom_call" | custom-call | tf_op jit(solution)/shard_map/project/pallas_call | solution.py:172
  43.6 10.0 %all-to-all-start.1 = ((bf16[8,64,1536]{2,1,0:T(8,128)(2,1)}), bf16[8,64,1536]{2,1,0:T(8,128)(2,1)S(1)}, u32[]{:S(2)}, u32[]{:S(2)}) async-start(bf16[8,64,1536]{2,1,0:T(8,128)(2,1)} %project.1), calls=%async_computation.1 | async-start | bytes 3145728 | tf_op jit(solution)/shard_map/all_to_all | solution.py:180
  55.7 37.3 %collective-permute-done.3 = bf16[576,512]{1,0:T(8,128)(2,1)S(1)} collective-permute-done((bf16[576,512]{1,0:T(8,128)(2,1)S(1)}, bf16[576,512]{1,0:T(8,128)(2,1)S(1)}, u32[]{:S(2)}, u32[]{:S(2)}) %collective-permute-start.3) | collective-permute-done | bytes 589856 | tf_op jit(solution)/shard_map/ppermute | solution.py:164
  95.5 3.1 %mix.1 = (bf16[32,16,1536]{2,1,0:T(8,128)(2,1)}, f32[64,1536]{1,0:T(8,128)}, bf16[16,1536]{1,0:T(8,128)(2,1)}, bf16[16,1536]{1,0:T(8,128)(2,1)}, bf16[16,1536]{1...) custom-call(s32[6]{0:T(128)} %stack.27.place_ref, ...), custom_call_target="tpu_custom_call" | custom-call | tf_op jit(solution)/shard_map/mix/pallas_call | solution.py:186
  98.6 31.2 %all-to-all-start.2 = ((bf16[32,16,1536]{2,1,0:T(8,128)(2,1)}), bf16[32,16,1536]{2,1,0:T(8,128)(2,1)S(1)}, u32[]{:S(2)}, u32[]{:S(2)}) async-start(bf16[32,16,1536]{2,1,0:T(8,128)(2,1)} %get-tuple-element.42), calls=%async_computation.2 | async-start | bytes 3145728 | tf_op jit(solution)/shard_map/all_to_all | solution.py:197
  131.6 3.1 %collective-permute-start.5 = (bf16[16,1536]{1,0:T(8,128)(2,1)S(1)}, bf16[16,1536]{1,0:T(8,128)(2,1)S(1)}, u32[]{:S(2)}, u32[]{:S(2)}) collective-permute-start(bf16[16,1536]{1,0:T(8,128)(2,1)S(1)} %copy-done.22), channel_id=1, source_target_pairs={{0,2},{1,3},{2,4},{3,5},{4,6},{5,7},{6,0},{7,1},{8,10},{9,11},{10,... | collective-permute-start | bytes 147464 | tf_op jit(solution)/shard_map/ppermute | solution.py:195
  134.7 3.7 %collective-permute-start.6 = (bf16[16,1536]{1,0:T(8,128)(2,1)S(1)}, bf16[16,1536]{1,0:T(8,128)(2,1)S(1)}, u32[]{:S(2)}, u32[]{:S(2)}) collective-permute-start(bf16[16,1536]{1,0:T(8,128)(2,1)S(1)} %copy-done.21), channel_id=1, source_target_pairs={{0,3},{1,4},{2,5},{3,6},{4,7},{5,0},{6,1},{7,2},{8,11},{9,12},{10,... | collective-permute-start | bytes 147464 | tf_op jit(solution)/shard_map/ppermute | solution.py:195
  138.5 3.7 %collective-permute-start.7 = (bf16[16,1536]{1,0:T(8,128)(2,1)S(1)}, bf16[16,1536]{1,0:T(8,128)(2,1)S(1)}, u32[]{:S(2)}, u32[]{:S(2)}) collective-permute-start(bf16[16,1536]{1,0:T(8,128)(2,1)S(1)} %copy-done.20), channel_id=1, source_target_pairs={{0,4},{1,5},{2,6},{3,7},{4,0},{5,1},{6,2},{7,3},{8,12},{9,13},{10,... | collective-permute-start | bytes 147464 | tf_op jit(solution)/shard_map/ppermute | solution.py:195
  142.2 2.4 collective-permute-done.10.refs_7_
  152.3 13.0 %all-to-all-done.2.x_ref = bf16[32,16,1536]{2,1,0:T(8,128)(2,1)S(1)} async-done(((bf16[32,16,1536]{2,1,0:T(8,128)(2,1)}), bf16[32,16,1536]{2,1,0:T(8,128)(2,1)S(1)}, u32[]{:S(2)}, u32[]{:S(2)}) %all-to-all-start.2) | async-done | bytes 1572896 | tf_op jit(solution)/shard_map/all_to_all | solution.py:197
  166.5 6.5 %near.1 = bf16[32,16,1536]{2,1,0:T(8,128)(2,1)} custom-call(bf16[32,16,1536]{2,1,0:T(8,128)(2,1)} %copy-done.1, bf16[1,1536,512]{2,1,0:T(8,128)(2,1)} %wg_ref.3, bf16[1,1536,512]{2,1,0:T(8,128)(2,1)} %wu_ref.3, bf16[1,512,1536]{2,1,0:T(8,128)(2,1)} %wd_ref.3), custom_call_target="tpu_custom_call" | custom-call | tf_op jit(solution)/shard_map/near/pallas_call | solution.py:201
  173.1 7.7 %all-to-all-start.3 = ((bf16[32,16,1536]{2,1,0:T(8,128)(2,1)}), bf16[32,16,1536]{2,1,0:T(8,128)(2,1)S(1)}, u32[]{:S(2)}, u32[]{:S(2)}) async-start(bf16[32,16,1536]{2,1,0:T(8,128)(2,1)} %near.1), calls=%async_computation.3 | async-start | bytes 3145728 | tf_op jit(solution)/shard_map/all_to_all | solution.py:224
  180.8 4.2 %far.1 = (bf16[16,1536]{1,0:T(8,128)(2,1)}, bf16[16,1536]{1,0:T(8,128)(2,1)}, bf16[16,1536]{1,0:T(8,128)(2,1)}, bf16[16,1536]{1,0:T(8,128)(2,1)}, bf16[16,1536]{...) custom-call(bf16[16,1536]{1,0:T(8,128)(2,1)} %get-tuple-element.52.refs_0_, ...), custom_call_target="tpu_custom_call" | custom-call | tf_op jit(solution)/shard_map/far/pallas_call | solution.py:215
  185.4 4.3 %collective-permute-start.12 = (bf16[16,1536]{1,0:T(8,128)(2,1)}, bf16[16,1536]{1,0:T(8,128)(2,1)S(1)}, u32[]{:S(2)}, u32[]{:S(2)}) collective-permute-start(bf16[16,1536]{1,0:T(8,128)(2,1)} %get-tuple-element.63), channel_id=1, source_target_pairs={{0,6},{1,7},{2,0},{3,1},{4,2},{5,3},{6,4},{7,5},{8,14},{9,15},{10,... | collective-permute-start | bytes 147464 | tf_op jit(solution)/shard_map/ppermute | solution.py:195
  189.7 2.9 %collective-permute-start.13 = (bf16[16,1536]{1,0:T(8,128)(2,1)}, bf16[16,1536]{1,0:T(8,128)(2,1)S(1)}, u32[]{:S(2)}, u32[]{:S(2)}) collective-permute-start(bf16[16,1536]{1,0:T(8,128)(2,1)} %get-tuple-element.64), channel_id=1, source_target_pairs={{0,5},{1,6},{2,7},{3,0},{4,1},{5,2},{6,3},{7,4},{8,13},{9,14},{10,... | collective-permute-start | bytes 147464 | tf_op jit(solution)/shard_map/ppermute | solution.py:195
  192.7 4.3 %collective-permute-start.14 = (bf16[16,1536]{1,0:T(8,128)(2,1)}, bf16[16,1536]{1,0:T(8,128)(2,1)S(1)}, u32[]{:S(2)}, u32[]{:S(2)}) collective-permute-start(bf16[16,1536]{1,0:T(8,128)(2,1)} %get-tuple-element.65), channel_id=1, source_target_pairs={{0,4},{1,5},{2,6},{3,7},{4,0},{5,1},{6,2},{7,3},{8,12},{9,13},{10,... | collective-permute-start | bytes 147464 | tf_op jit(solution)/shard_map/ppermute | solution.py:195
  197.0 2.5 %collective-permute-start.15 = (bf16[16,1536]{1,0:T(8,128)(2,1)}, bf16[16,1536]{1,0:T(8,128)(2,1)S(1)}, u32[]{:S(2)}, u32[]{:S(2)}) collective-permute-start(bf16[16,1536]{1,0:T(8,128)(2,1)} %get-tuple-element.66), channel_id=1, source_target_pairs={{0,3},{1,4},{2,5},{3,6},{4,7},{5,0},{6,1},{7,2},{8,11},{9,12},{10,... | collective-permute-start | bytes 147464 | tf_op jit(solution)/shard_map/ppermute | solution.py:195
  199.6 2.8 %collective-permute-start.16 = (bf16[16,1536]{1,0:T(8,128)(2,1)}, bf16[16,1536]{1,0:T(8,128)(2,1)S(1)}, u32[]{:S(2)}, u32[]{:S(2)}) collective-permute-start(bf16[16,1536]{1,0:T(8,128)(2,1)} %get-tuple-element.67), channel_id=1, source_target_pairs={{0,2},{1,3},{2,4},{3,5},{4,6},{5,7},{6,0},{7,1},{8,10},{9,11},{10,... | collective-permute-start | bytes 147464 | tf_op jit(solution)/shard_map/ppermute | solution.py:195
  205.5 10.7 %all-to-all-done.3.near_ref = bf16[32,16,1536]{2,1,0:T(8,128)(2,1)S(1)} async-done(((bf16[32,16,1536]{2,1,0:T(8,128)(2,1)}), bf16[32,16,1536]{2,1,0:T(8,128)(2,1)S(1)}, u32[]{:S(2)}, u32[]{:S(2)}) %all-to-all-start.3) | async-done | bytes 1572896 | tf_op jit(solution)/shard_map/all_to_all | solution.py:224
  216.9 2.8 %close.1 = bf16[8,64,192]{2,1,0:T(8,128)(2,1)} custom-call(s32[6]{0:T(128)} %stack.27.place_ref, s32[64,8]{1,0:T(8,128)} %copy.14.routes_ref, f32[64,8]{1,0:T(8,128)} %copy.15.gates_ref, f32[64,1536]{1,0:T(8,128)} %get-tuple-element.41.hid_ref, f32[1,1536]{1,0:T(1,128)} %reshape.11.gain_ref, bf16[32,16,1536]{2,1,0:T(8,128)(2,1)S(1)} %all-to-all-done.3.near_ref, ...), custom_call_target="tpu_custom_call" | custom-call | tf_op jit(solution)/shard_map/close/pallas_call | solution.py:227
  219.8 15.7 %all_to_all.25 = bf16[8,64,192]{2,1,0:T(8,128)(2,1)S(1)} all-to-all(bf16[8,64,192]{2,1,0:T(8,128)(2,1)} %close.1), channel_id=1, replica_groups=mesh['tp'=8,'h'=2,'y'=4,'x'=4,'c'=2] {'tp'}, dimensions={0} | all-to-all | bytes 393216 | tf_op jit(solution)/shard_map/all_to_all | solution.py:235
  (90 shorter events, 23.8 us)
Async XLA Ops:
  6.5 87.5 %copy-start = (s32[512,8]{0,1:T(8,128)S(1)}, s32[512,8]{0,1:T(8,128)}, u32[]{:S(2)}) copy-start(s32[512,8]{0,1:T(8,128)} %param.15) | copy-start | bytes 49156
  8.2 32.1 %all-to-all-start = ((bf16[64,24,192]{2,1,0:T(8,128)(2,1)}), bf16[64,24,192]{2,1,0:T(8,128)(2,1)S(1)}, u32[]{:S(2)}, u32[]{:S(2)}) async-start(bf16[64,24,192]{2,1,0:T(8,128)(2,1)} %broadcast_in_dim.2), calls=%async_computation | async-start | bytes 1572864 | tf_op jit(solution)/shard_map/all_to_all | solution.py:167
  22.0 1.4 collective-permute-start
  22.6 0.7 collective-permute-start.1
  43.6 50.5 %all-to-all-start.1 = ((bf16[8,64,1536]{2,1,0:T(8,128)(2,1)}), bf16[8,64,1536]{2,1,0:T(8,128)(2,1)S(1)}, u32[]{:S(2)}, u32[]{:S(2)}) async-start(bf16[8,64,1536]{2,1,0:T(8,128)(2,1)} %project.1), calls=%async_computation.1 | async-start | bytes 3145728 | tf_op jit(solution)/shard_map/all_to_all | solution.py:180
  53.6 127.2 %all-gather.3.cloned.1.call-start = ((), (), s32[]{:S(2)}) async-start(), calls=%async_computation.5 | async-start | bytes 5308416 | tf_op jit(solution)/shard_map/all_gather | solution.py:183
  53.7 2.0 collective-permute-start.2
  54.4 38.6 %collective-permute-start.3 = (bf16[576,512]{1,0:T(8,128)(2,1)S(1)}, bf16[576,512]{1,0:T(8,128)(2,1)S(1)}, u32[]{:S(2)}, u32[]{:S(2)}) collective-permute-start(bf16[576,512]{1,0:T(8,128)(2,1)S(1)} %collective-permute-done.1), channel_id=1, source_target_pairs={{8,0},{48,56},{9,1},{49,57},{10,2},{50,58},{11,3},{51,59},{12,4},{... | collective-permute-start | bytes 1769480 | tf_op jit(solution)/shard_map/ppermute | solution.py:164
  98.6 66.6 %all-to-all-start.2 = ((bf16[32,16,1536]{2,1,0:T(8,128)(2,1)}), bf16[32,16,1536]{2,1,0:T(8,128)(2,1)S(1)}, u32[]{:S(2)}, u32[]{:S(2)}) async-start(bf16[32,16,1536]{2,1,0:T(8,128)(2,1)} %get-tuple-element.42), calls=%async_computation.2 | async-start | bytes 3145728 | tf_op jit(solution)/shard_map/all_to_all | solution.py:197
  129.9 14.8 %collective-permute-start.10 = (bf16[16,1536]{1,0:T(8,128)(2,1)S(1)}, bf16[16,1536]{1,0:T(8,128)(2,1)S(1)}, u32[]{:S(2)}, u32[]{:S(2)}) collective-permute-start(bf16[16,1536]{1,0:T(8,128)(2,1)S(1)} %copy-done.24), channel_id=1, source_target_pairs={{0,7},{1,0},{2,1},{3,2},{4,3},{5,4},{6,5},{7,6},{8,15},{9,8},{10,9... | collective-permute-start | bytes 147464 | tf_op jit(solution)/shard_map/ppermute | solution.py:195
  130.2 16.6 %collective-permute-start.4 = (bf16[16,1536]{1,0:T(8,128)(2,1)S(1)}, bf16[16,1536]{1,0:T(8,128)(2,1)S(1)}, u32[]{:S(2)}, u32[]{:S(2)}) collective-permute-start(bf16[16,1536]{1,0:T(8,128)(2,1)S(1)} %copy-done.23), channel_id=1, source_target_pairs={{0,1},{1,2},{2,3},{3,4},{4,5},{5,6},{6,7},{7,0},{8,9},{9,10},{10,1... | collective-permute-start | bytes 147464 | tf_op jit(solution)/shard_map/ppermute | solution.py:195
  131.6 17.1 %collective-permute-start.5 = (bf16[16,1536]{1,0:T(8,128)(2,1)S(1)}, bf16[16,1536]{1,0:T(8,128)(2,1)S(1)}, u32[]{:S(2)}, u32[]{:S(2)}) collective-permute-start(bf16[16,1536]{1,0:T(8,128)(2,1)S(1)} %copy-done.22), channel_id=1, source_target_pairs={{0,2},{1,3},{2,4},{3,5},{4,6},{5,7},{6,0},{7,1},{8,10},{9,11},{10,... | collective-permute-start | bytes 147464 | tf_op jit(solution)/shard_map/ppermute | solution.py:195
  134.7 14.0 %collective-permute-start.6 = (bf16[16,1536]{1,0:T(8,128)(2,1)S(1)}, bf16[16,1536]{1,0:T(8,128)(2,1)S(1)}, u32[]{:S(2)}, u32[]{:S(2)}) collective-permute-start(bf16[16,1536]{1,0:T(8,128)(2,1)S(1)} %copy-done.21), channel_id=1, source_target_pairs={{0,3},{1,4},{2,5},{3,6},{4,7},{5,0},{6,1},{7,2},{8,11},{9,12},{10,... | collective-permute-start | bytes 147464 | tf_op jit(solution)/shard_map/ppermute | solution.py:195
  138.5 11.8 %collective-permute-start.7 = (bf16[16,1536]{1,0:T(8,128)(2,1)S(1)}, bf16[16,1536]{1,0:T(8,128)(2,1)S(1)}, u32[]{:S(2)}, u32[]{:S(2)}) collective-permute-start(bf16[16,1536]{1,0:T(8,128)(2,1)S(1)} %copy-done.20), channel_id=1, source_target_pairs={{0,4},{1,5},{2,6},{3,7},{4,0},{5,1},{6,2},{7,3},{8,12},{9,13},{10,... | collective-permute-start | bytes 147464 | tf_op jit(solution)/shard_map/ppermute | solution.py:195
  144.6 7.0 %collective-permute-start.8 = (bf16[16,1536]{1,0:T(8,128)(2,1)S(1)}, bf16[16,1536]{1,0:T(8,128)(2,1)S(1)}, u32[]{:S(2)}, u32[]{:S(2)}) collective-permute-start(bf16[16,1536]{1,0:T(8,128)(2,1)S(1)} %copy-done.19), channel_id=1, source_target_pairs={{0,5},{1,6},{2,7},{3,0},{4,1},{5,2},{6,3},{7,4},{8,13},{9,14},{10,... | collective-permute-start | bytes 147464 | tf_op jit(solution)/shard_map/ppermute | solution.py:195
  146.8 5.5 %collective-permute-start.9 = (bf16[16,1536]{1,0:T(8,128)(2,1)S(1)}, bf16[16,1536]{1,0:T(8,128)(2,1)S(1)}, u32[]{:S(2)}, u32[]{:S(2)}) collective-permute-start(bf16[16,1536]{1,0:T(8,128)(2,1)S(1)} %copy-done.18), channel_id=1, source_target_pairs={{0,6},{1,7},{2,0},{3,1},{4,2},{5,3},{6,4},{7,5},{8,14},{9,15},{10,... | collective-permute-start | bytes 147464 | tf_op jit(solution)/shard_map/ppermute | solution.py:195
  173.1 43.1 %all-to-all-start.3 = ((bf16[32,16,1536]{2,1,0:T(8,128)(2,1)}), bf16[32,16,1536]{2,1,0:T(8,128)(2,1)S(1)}, u32[]{:S(2)}, u32[]{:S(2)}) async-start(bf16[32,16,1536]{2,1,0:T(8,128)(2,1)} %near.1), calls=%async_computation.3 | async-start | bytes 3145728 | tf_op jit(solution)/shard_map/all_to_all | solution.py:224
  185.0 14.5 %collective-permute-start.11 = (bf16[16,1536]{1,0:T(8,128)(2,1)}, bf16[16,1536]{1,0:T(8,128)(2,1)S(1)}, u32[]{:S(2)}, u32[]{:S(2)}) collective-permute-start(bf16[16,1536]{1,0:T(8,128)(2,1)} %get-tuple-element.62), channel_id=1, source_target_pairs={{0,7},{1,0},{2,1},{3,2},{4,3},{5,4},{6,5},{7,6},{8,15},{9,8},{10,9... | collective-permute-start | bytes 147464 | tf_op jit(solution)/shard_map/ppermute | solution.py:195
  185.4 17.0 %collective-permute-start.12 = (bf16[16,1536]{1,0:T(8,128)(2,1)}, bf16[16,1536]{1,0:T(8,128)(2,1)S(1)}, u32[]{:S(2)}, u32[]{:S(2)}) collective-permute-start(bf16[16,1536]{1,0:T(8,128)(2,1)} %get-tuple-element.63), channel_id=1, source_target_pairs={{0,6},{1,7},{2,0},{3,1},{4,2},{5,3},{6,4},{7,5},{8,14},{9,15},{10,... | collective-permute-start | bytes 147464 | tf_op jit(solution)/shard_map/ppermute | solution.py:195
  189.7 26.5 %collective-permute-start.13 = (bf16[16,1536]{1,0:T(8,128)(2,1)}, bf16[16,1536]{1,0:T(8,128)(2,1)S(1)}, u32[]{:S(2)}, u32[]{:S(2)}) collective-permute-start(bf16[16,1536]{1,0:T(8,128)(2,1)} %get-tuple-element.64), channel_id=1, source_target_pairs={{0,5},{1,6},{2,7},{3,0},{4,1},{5,2},{6,3},{7,4},{8,13},{9,14},{10,... | collective-permute-start | bytes 147464 | tf_op jit(solution)/shard_map/ppermute | solution.py:195
  192.7 23.5 %collective-permute-start.14 = (bf16[16,1536]{1,0:T(8,128)(2,1)}, bf16[16,1536]{1,0:T(8,128)(2,1)S(1)}, u32[]{:S(2)}, u32[]{:S(2)}) collective-permute-start(bf16[16,1536]{1,0:T(8,128)(2,1)} %get-tuple-element.65), channel_id=1, source_target_pairs={{0,4},{1,5},{2,6},{3,7},{4,0},{5,1},{6,2},{7,3},{8,12},{9,13},{10,... | collective-permute-start | bytes 147464 | tf_op jit(solution)/shard_map/ppermute | solution.py:195
  197.0 19.2 %collective-permute-start.15 = (bf16[16,1536]{1,0:T(8,128)(2,1)}, bf16[16,1536]{1,0:T(8,128)(2,1)S(1)}, u32[]{:S(2)}, u32[]{:S(2)}) collective-permute-start(bf16[16,1536]{1,0:T(8,128)(2,1)} %get-tuple-element.66), channel_id=1, source_target_pairs={{0,3},{1,4},{2,5},{3,6},{4,7},{5,0},{6,1},{7,2},{8,11},{9,12},{10,... | collective-permute-start | bytes 147464 | tf_op jit(solution)/shard_map/ppermute | solution.py:195
  199.6 16.7 %collective-permute-start.16 = (bf16[16,1536]{1,0:T(8,128)(2,1)}, bf16[16,1536]{1,0:T(8,128)(2,1)S(1)}, u32[]{:S(2)}, u32[]{:S(2)}) collective-permute-start(bf16[16,1536]{1,0:T(8,128)(2,1)} %get-tuple-element.67), channel_id=1, source_target_pairs={{0,2},{1,3},{2,4},{3,5},{4,6},{5,7},{6,0},{7,1},{8,10},{9,11},{10,... | collective-permute-start | bytes 147464 | tf_op jit(solution)/shard_map/ppermute | solution.py:195
  202.4 13.9 %collective-permute-start.17 = (bf16[16,1536]{1,0:T(8,128)(2,1)}, bf16[16,1536]{1,0:T(8,128)(2,1)S(1)}, u32[]{:S(2)}, u32[]{:S(2)}) collective-permute-start(bf16[16,1536]{1,0:T(8,128)(2,1)} %get-tuple-element.68), channel_id=1, source_target_pairs={{0,1},{1,2},{2,3},{3,4},{4,5},{5,6},{6,7},{7,0},{8,9},{9,10},{10,1... | collective-permute-start | bytes 147464 | tf_op jit(solution)/shard_map/ppermute | solution.py:195
  (24 other events, 534.7 us)
Sparse Core Ops, SparseCore 0:
  94.2 80.2 all-gather.2

commit v4 on v0

--- a/solution.py
+++ b/solution.py
@@ -131,6 +131,10 @@
 
 def vmem():
     return pl.BlockSpec(memory_space=pltpu.VMEM)
+
+
+def keep(value):
+    return pltpu.with_memory_space_constraint(value, pltpu.VMEM)
 
 
 def per_device(attn, resid, w_out, gain_mix, gain_out, routes, gates, w_gate, w_up, w_down):
@@ -159,7 +163,6 @@
     )(place, w_gate, w_up, w_down)
     crossed = lax.ppermute(piece, ("h", "y"), [(4, 3), (3, 4)])
     columns = lax.all_to_all(jnp.broadcast_to(w_out.T[None], (64, 24, 192)), EP, 0, 0, tiled=True)
-    crossed, _ = lax.optimization_barrier((crossed, columns))
     pieces = lax.all_gather(crossed, "y", axis=0, tiled=False)
 
     parts = pl.pallas_call(
@@ -169,7 +172,7 @@
         out_specs=vmem(),
         compiler_params=params(),
         name="project",
-    )(place, attn.T, resid.T, columns)
+    )(place, attn.T, resid.T, keep(columns))
     parts = lax.all_to_all(parts, "tp", 0, 0, tiled=True)
     rows = shape((CAP, 1536), BF)
     send, hidden, *far = pl.pallas_call(
@@ -179,7 +182,7 @@
         out_specs=(vmem(),) * 10,
         compiler_params=params(),
         name="mix",
-    )(place, parts, my_routes, gain_mix.reshape(1, 1536))
+    )(place, keep(parts), my_routes, gain_mix.reshape(1, 1536))
 
     pieces, _ = lax.optimization_barrier((pieces, send))
     far_piece = lax.dynamic_index_in_dim(pieces, 3 - 3 * h, 0, keepdims=False)
@@ -224,7 +227,7 @@
         out_specs=vmem(),
         compiler_params=params(),
         name="close",
-    )(place, my_routes, my_gates, hidden, gain_out.reshape(1, 1536), near, *far)
+    )(place, my_routes, my_gates, hidden, gain_out.reshape(1, 1536), keep(near), *far)
     return lax.all_to_all(finished, "tp", 0, 0, tiled=True).reshape(512, 192)
 
 

time: 242 us -> 229 us (0.946)
  waiting for transfers between devices: 96.3 us -> 85.4 us
  starting transfers between devices: 74.3 us -> 79 us
  blocking collectives: 19.5 us -> 16.6 us
  local copies, waits for them, and re-layouts: 13.1 us -> 10.5 us
    all_gather x1, waiting for transfers between devices: 14.5 us -> 1.39 us  [per_device(): pieces = lax.all_gather(crossed, 'y', axis=0, tiled=False)]
    all_to_all x1, blocking collectives: 19.5 us -> 16.6 us  [per_device(): return lax.all_to_all(finished, 'tp', 0, 0, tiled=True).reshape(512, 192)]
    all_to_all x1, starting transfers between devices: 8.17 us -> 11.1 us  [per_device(): received = lax.all_to_all(send, ('y', 'x', 'c'), 0, 0, tiled=True)]
    all_gather x1, waiting for transfers between devices: 2.78 us -> 0.02 us  [per_device(): far_weights = lax.all_gather(far_piece, 'tp', axis=0, tiled=False)]
    all_to_all x1, waiting for transfers between devices: 7.94 us -> 10.7 us  [per_device(): near = lax.all_to_all(near, ('y', 'x', 'c'), 0, 0, tiled=True)]
    unnamed x60 -> x56, local copies, waits for them, and re-layouts: 5.91 us -> 4.12 us
  transfers between devices with their start and end apart: 21 -> 21, of which waited for: 9 -> 8; matrix products, arithmetic and copies ran while one was open for 2% -> 2% of each run, Pallas kernels for 9% -> 7%
where the time goes in v4:
time: 229 us; the launch traced here: 228 us
  waiting for transfers between devices  85.4 us (37%)
  starting transfers between devices  79 us (34%)
  Pallas kernels  22.7 us (10%)
  blocking collectives  16.6 us (7%)
  between operations  13.9 us (6%)
  local copies, waits for them, and re-layouts  10.5 us (5%)
    ppermute x14, starting transfers between devices, per_device(): lax.ppermute(v, ('x', 'c'), [(i, (i + k) % 8) for i in range(8)])  37 us
    all_to_all x1, waiting for transfers between devices, per_device(): parts = lax.all_to_all(parts, 'tp', 0, 0, tiled=True)  36.8 us
    all_to_all x1, waiting for transfers between devices, per_device(): lax.all_to_all(jnp.broadcast_to(w_out.T[None], (64, 24, 192)), EP, 0, 0,...  19.8 us
    all_to_all x1, blocking collectives, per_device(): return lax.all_to_all(finished, 'tp', 0, 0, tiled=True).reshape(512, 192)  16.6 us
    all_to_all x1, waiting for transfers between devices, per_device(): received = lax.all_to_all(send, ('y', 'x', 'c'), 0, 0, tiled=True)  13.4 us
    all_to_all x1, starting transfers between devices, per_device(): lax.all_to_all(jnp.broadcast_to(w_out.T[None], (64, 24, 192)), EP, 0, 0,...  12.2 us
    all_to_all x1, starting transfers between devices, per_device(): received = lax.all_to_all(send, ('y', 'x', 'c'), 0, 0, tiled=True)  11.1 us
    all_to_all x1, waiting for transfers between devices, per_device(): near = lax.all_to_all(near, ('y', 'x', 'c'), 0, 0, tiled=True)  10.7 us
  transfers between devices with their start and end apart: 21, of which 8 were waited for; matrix products, arithmetic and copies ran while one was open for 2% of the time, Pallas kernels for 7%

profile of v4, /device:TPU:57, one launch (start us, length us, event | category | flops | bytes accessed | tf_op | source)
XLA Modules:
  0.0 228.0 jit_solution(12086275742748054125)
XLA Ops:
  7.2 2.8 %piece.1 = bf16[576,512]{1,0:T(8,128)(2,1)} custom-call(s32[6]{0:T(128)} %stack.27.place_ref, bf16[1,1536,512]{2,1,0:T(8,128)(2,1)} %wg_ref.3, bf16[1,1536,512]{2,1,0:T(8,128)(2,1)} %wu_ref.3, bf16[1,512,1536]{2,1,0:T(8,128)(2,1)} %wd_ref.3), custom_call_target="tpu_custom_call" | custom-call | tf_op jit(solution)/shard_map/piece/pallas_call | solution.py:148
  11.6 12.2 %all-to-all-start = ((bf16[64,24,192]{2,1,0:T(8,128)(2,1)}), bf16[64,24,192]{2,1,0:T(8,128)(2,1)S(1)}, u32[]{:S(2)}, u32[]{:S(2)}) async-start(bf16[64,24,192]{2,1,0:T(8,128)(2,1)} %broadcast_in_dim.2), calls=%async_computation | async-start | bytes 1572864 | tf_op jit(solution)/shard_map/all_to_all | solution.py:165
  24.8 19.8 %all-to-all-done.w_ref = bf16[64,24,192]{2,1,0:T(8,128)(2,1)S(1)} async-done(((bf16[64,24,192]{2,1,0:T(8,128)(2,1)}), bf16[64,24,192]{2,1,0:T(8,128)(2,1)S(1)}, u32[]{:S(2)}, u32[]{:S(2)}) %all-to-all-start) | async-done | bytes 589856 | tf_op jit(solution)/shard_map/all_to_all | solution.py:165
  44.5 3.2 %project.1 = bf16[8,64,1536]{2,1,0:T(8,128)(2,1)} custom-call(s32[6]{0:T(128)} %stack.27.place_ref, bf16[192,512]{1,0:T(8,128)(2,1)} %bitcast.12, bf16[192,512]{1,0:T(8,128)(2,1)} %bitcast.13, bf16[64,24,192]{2,1,0:T(8,128)(2,1)S(1)} %all-to-all-done.w_ref), custom_call_target="tpu_custom_call" | custom-call | tf_op jit(solution)/shard_map/project/pallas_call | solution.py:168
  47.8 10.2 %all-to-all-start.1 = ((bf16[8,64,1536]{2,1,0:T(8,128)(2,1)}), bf16[8,64,1536]{2,1,0:T(8,128)(2,1)S(1)}, u32[]{:S(2)}, u32[]{:S(2)}) async-start(bf16[8,64,1536]{2,1,0:T(8,128)(2,1)} %project.1), calls=%async_computation.1 | async-start | bytes 3145728 | tf_op jit(solution)/shard_map/all_to_all | solution.py:176
  59.4 36.8 %all-to-all-done.1.part_ref = bf16[8,64,1536]{2,1,0:T(8,128)(2,1)S(1)} async-done(((bf16[8,64,1536]{2,1,0:T(8,128)(2,1)}), bf16[8,64,1536]{2,1,0:T(8,128)(2,1)S(1)}, u32[]{:S(2)}, u32[]{:S(2)}) %all-to-all-start.1) | async-done | bytes 1572896 | tf_op jit(solution)/shard_map/all_to_all | solution.py:176
  96.2 3.1 %mix.1 = (bf16[32,16,1536]{2,1,0:T(8,128)(2,1)}, f32[64,1536]{1,0:T(8,128)}, bf16[16,1536]{1,0:T(8,128)(2,1)}, bf16[16,1536]{1,0:T(8,128)(2,1)}, bf16[16,1536]{1...) custom-call(s32[6]{0:T(128)} %stack.27.place_ref, ...), custom_call_target="tpu_custom_call" | custom-call | tf_op jit(solution)/shard_map/mix/pallas_call | solution.py:178
  102.8 11.1 %all-to-all-start.2 = ((bf16[32,16,1536]{2,1,0:T(8,128)(2,1)}), bf16[32,16,1536]{2,1,0:T(8,128)(2,1)S(1)}, u32[]{:S(2)}, u32[]{:S(2)}) async-start(bf16[32,16,1536]{2,1,0:T(8,128)(2,1)} %get-tuple-element.34), calls=%async_computation.2 | async-start | bytes 3145728 | tf_op jit(solution)/shard_map/all_to_all | solution.py:193
  115.3 3.1 %collective-permute-start.1 = (bf16[16,1536]{1,0:T(8,128)(2,1)S(1)}, bf16[16,1536]{1,0:T(8,128)(2,1)S(1)}, u32[]{:S(2)}, u32[]{:S(2)}) collective-permute-start(bf16[16,1536]{1,0:T(8,128)(2,1)S(1)} %copy-done.25), channel_id=1, source_target_pairs={{0,2},{1,3},{2,4},{3,5},{4,6},{5,7},{6,0},{7,1},{8,10},{9,11},{10,... | collective-permute-start | bytes 147464 | tf_op jit(solution)/shard_map/ppermute | solution.py:191
  118.4 3.6 %collective-permute-start.2 = (bf16[16,1536]{1,0:T(8,128)(2,1)S(1)}, bf16[16,1536]{1,0:T(8,128)(2,1)S(1)}, u32[]{:S(2)}, u32[]{:S(2)}) collective-permute-start(bf16[16,1536]{1,0:T(8,128)(2,1)S(1)} %copy-done.24), channel_id=1, source_target_pairs={{0,3},{1,4},{2,5},{3,6},{4,7},{5,0},{6,1},{7,2},{8,11},{9,12},{10,... | collective-permute-start | bytes 147464 | tf_op jit(solution)/shard_map/ppermute | solution.py:191
  124.5 3.8 %collective-permute-start.4 = (bf16[16,1536]{1,0:T(8,128)(2,1)S(1)}, bf16[16,1536]{1,0:T(8,128)(2,1)S(1)}, u32[]{:S(2)}, u32[]{:S(2)}) collective-permute-start(bf16[16,1536]{1,0:T(8,128)(2,1)S(1)} %copy-done.22), channel_id=1, source_target_pairs={{0,5},{1,6},{2,7},{3,0},{4,1},{5,2},{6,3},{7,4},{8,13},{9,14},{10,... | collective-permute-start | bytes 147464 | tf_op jit(solution)/shard_map/ppermute | solution.py:191
  128.3 2.5 %collective-permute-start.5 = (bf16[16,1536]{1,0:T(8,128)(2,1)S(1)}, bf16[16,1536]{1,0:T(8,128)(2,1)S(1)}, u32[]{:S(2)}, u32[]{:S(2)}) collective-permute-start(bf16[16,1536]{1,0:T(8,128)(2,1)S(1)} %copy-done.21), channel_id=1, source_target_pairs={{0,6},{1,7},{2,0},{3,1},{4,2},{5,3},{6,4},{7,5},{8,14},{9,15},{10,... | collective-permute-start | bytes 147464 | tf_op jit(solution)/shard_map/ppermute | solution.py:191
  135.9 13.4 %all-to-all-done.2.x_ref = bf16[32,16,1536]{2,1,0:T(8,128)(2,1)S(1)} async-done(((bf16[32,16,1536]{2,1,0:T(8,128)(2,1)}), bf16[32,16,1536]{2,1,0:T(8,128)(2,1)S(1)}, u32[]{:S(2)}, u32[]{:S(2)}) %all-to-all-start.2) | async-done | bytes 1572896 | tf_op jit(solution)/shard_map/all_to_all | solution.py:193
  150.5 6.5 %near.1 = bf16[32,16,1536]{2,1,0:T(8,128)(2,1)} custom-call(bf16[32,16,1536]{2,1,0:T(8,128)(2,1)} %copy-done.1, bf16[1,1536,512]{2,1,0:T(8,128)(2,1)} %wg_ref.3, bf16[1,1536,512]{2,1,0:T(8,128)(2,1)} %wu_ref.3, bf16[1,512,1536]{2,1,0:T(8,128)(2,1)} %wd_ref.3), custom_call_target="tpu_custom_call" | custom-call | tf_op jit(solution)/shard_map/near/pallas_call | solution.py:197
  157.1 7.7 %all-to-all-start.3 = ((bf16[32,16,1536]{2,1,0:T(8,128)(2,1)}), bf16[32,16,1536]{2,1,0:T(8,128)(2,1)S(1)}, u32[]{:S(2)}, u32[]{:S(2)}) async-start(bf16[32,16,1536]{2,1,0:T(8,128)(2,1)} %near.1), calls=%async_computation.3 | async-start | bytes 3145728 | tf_op jit(solution)/shard_map/all_to_all | solution.py:220
  164.9 4.2 %far.1 = (bf16[16,1536]{1,0:T(8,128)(2,1)}, bf16[16,1536]{1,0:T(8,128)(2,1)}, bf16[16,1536]{1,0:T(8,128)(2,1)}, bf16[16,1536]{1,0:T(8,128)(2,1)}, bf16[16,1536]{...) custom-call(bf16[16,1536]{1,0:T(8,128)(2,1)} %get-tuple-element.44.refs_0_, ...), custom_call_target="tpu_custom_call" | custom-call | tf_op jit(solution)/shard_map/far/pallas_call | solution.py:211
  169.6 4.3 %collective-permute-start.9 = (bf16[16,1536]{1,0:T(8,128)(2,1)}, bf16[16,1536]{1,0:T(8,128)(2,1)S(1)}, u32[]{:S(2)}, u32[]{:S(2)}) collective-permute-start(bf16[16,1536]{1,0:T(8,128)(2,1)} %get-tuple-element.55), channel_id=1, source_target_pairs={{0,6},{1,7},{2,0},{3,1},{4,2},{5,3},{6,4},{7,5},{8,14},{9,15},{10,... | collective-permute-start | bytes 147464 | tf_op jit(solution)/shard_map/ppermute | solution.py:191
  173.9 2.8 %collective-permute-start.10 = (bf16[16,1536]{1,0:T(8,128)(2,1)}, bf16[16,1536]{1,0:T(8,128)(2,1)S(1)}, u32[]{:S(2)}, u32[]{:S(2)}) collective-permute-start(bf16[16,1536]{1,0:T(8,128)(2,1)} %get-tuple-element.56), channel_id=1, source_target_pairs={{0,5},{1,6},{2,7},{3,0},{4,1},{5,2},{6,3},{7,4},{8,13},{9,14},{10,... | collective-permute-start | bytes 147464 | tf_op jit(solution)/shard_map/ppermute | solution.py:191
  176.7 4.3 %collective-permute-start.11 = (bf16[16,1536]{1,0:T(8,128)(2,1)}, bf16[16,1536]{1,0:T(8,128)(2,1)S(1)}, u32[]{:S(2)}, u32[]{:S(2)}) collective-permute-start(bf16[16,1536]{1,0:T(8,128)(2,1)} %get-tuple-element.57), channel_id=1, source_target_pairs={{0,4},{1,5},{2,6},{3,7},{4,0},{5,1},{6,2},{7,3},{8,12},{9,13},{10,... | collective-permute-start | bytes 147464 | tf_op jit(solution)/shard_map/ppermute | solution.py:191
  181.0 2.7 %collective-permute-start.12 = (bf16[16,1536]{1,0:T(8,128)(2,1)}, bf16[16,1536]{1,0:T(8,128)(2,1)S(1)}, u32[]{:S(2)}, u32[]{:S(2)}) collective-permute-start(bf16[16,1536]{1,0:T(8,128)(2,1)} %get-tuple-element.58), channel_id=1, source_target_pairs={{0,3},{1,4},{2,5},{3,6},{4,7},{5,0},{6,1},{7,2},{8,11},{9,12},{10,... | collective-permute-start | bytes 147464 | tf_op jit(solution)/shard_map/ppermute | solution.py:191
  183.8 2.6 %collective-permute-start.13 = (bf16[16,1536]{1,0:T(8,128)(2,1)}, bf16[16,1536]{1,0:T(8,128)(2,1)S(1)}, u32[]{:S(2)}, u32[]{:S(2)}) collective-permute-start(bf16[16,1536]{1,0:T(8,128)(2,1)} %get-tuple-element.59), channel_id=1, source_target_pairs={{0,2},{1,3},{2,4},{3,5},{4,6},{5,7},{6,0},{7,1},{8,10},{9,11},{10,... | collective-permute-start | bytes 147464 | tf_op jit(solution)/shard_map/ppermute | solution.py:191
  189.6 10.7 %all-to-all-done.3.near_ref = bf16[32,16,1536]{2,1,0:T(8,128)(2,1)S(1)} async-done(((bf16[32,16,1536]{2,1,0:T(8,128)(2,1)}), bf16[32,16,1536]{2,1,0:T(8,128)(2,1)S(1)}, u32[]{:S(2)}, u32[]{:S(2)}) %all-to-all-start.3) | async-done | bytes 1572896 | tf_op jit(solution)/shard_map/all_to_all | solution.py:220
  201.0 2.8 %close.1 = bf16[8,64,192]{2,1,0:T(8,128)(2,1)} custom-call(s32[6]{0:T(128)} %stack.27.place_ref, s32[64,8]{1,0:T(8,128)} %copy.17.routes_ref, f32[64,8]{1,0:T(8,128)} %copy.18.gates_ref, f32[64,1536]{1,0:T(8,128)} %get-tuple-element.33.hid_ref, f32[1,1536]{1,0:T(1,128)} %reshape.11.gain_ref, bf16[32,16,1536]{2,1,0:T(8,128)(2,1)S(1)} %all-to-all-done.3.near_ref, ...), custom_call_target="tpu_custom_call" | custom-call | tf_op jit(solution)/shard_map/close/pallas_call | solution.py:223
  203.8 16.6 %all_to_all.25 = bf16[8,64,192]{2,1,0:T(8,128)(2,1)S(1)} all-to-all(bf16[8,64,192]{2,1,0:T(8,128)(2,1)} %close.1), channel_id=1, replica_groups=mesh['tp'=8,'h'=2,'y'=4,'x'=4,'c'=2] {'tp'}, dimensions={0} | all-to-all | bytes 393216 | tf_op jit(solution)/shard_map/all_to_all | solution.py:231
  (91 shorter events, 23.4 us)
Async XLA Ops:
  6.5 51.4 %copy-start = (s32[512,8]{0,1:T(8,128)S(1)}, s32[512,8]{0,1:T(8,128)}, u32[]{:S(2)}) copy-start(s32[512,8]{0,1:T(8,128)} %param.15) | copy-start | bytes 49156
  10.0 13.9 %collective-permute-start.7 = (bf16[576,512]{1,0:T(8,128)(2,1)}, bf16[576,512]{1,0:T(8,128)(2,1)S(1)}, u32[]{:S(2)}, u32[]{:S(2)}) collective-permute-start(bf16[576,512]{1,0:T(8,128)(2,1)} %piece.1), channel_id=1, source_target_pairs={{32,24},{24,32},{33,25},{25,33},{34,26},{26,34},{35,27},{27,35},{3... | collective-permute-start | bytes 1769480 | tf_op jit(solution)/shard_map/ppermute | solution.py:164
  11.6 32.9 %all-to-all-start = ((bf16[64,24,192]{2,1,0:T(8,128)(2,1)}), bf16[64,24,192]{2,1,0:T(8,128)(2,1)S(1)}, u32[]{:S(2)}, u32[]{:S(2)}) async-start(bf16[64,24,192]{2,1,0:T(8,128)(2,1)} %broadcast_in_dim.2), calls=%async_computation | async-start | bytes 1572864 | tf_op jit(solution)/shard_map/all_to_all | solution.py:165
  23.9 76.8 %all-gather.6.cloned.1.call-start = ((), (), s32[]{:S(2)}) async-start(), calls=%async_computation.6 | async-start | bytes 2949120 | tf_op jit(solution)/shard_map/all_gather | solution.py:166
  47.8 48.4 %all-to-all-start.1 = ((bf16[8,64,1536]{2,1,0:T(8,128)(2,1)}), bf16[8,64,1536]{2,1,0:T(8,128)(2,1)S(1)}, u32[]{:S(2)}, u32[]{:S(2)}) async-start(bf16[8,64,1536]{2,1,0:T(8,128)(2,1)} %project.1), calls=%async_computation.1 | async-start | bytes 3145728 | tf_op jit(solution)/shard_map/all_to_all | solution.py:176
  57.9 106.9 %all-gather.4.cloned.1.call-start = ((), (), s32[]{:S(2)}) async-start(), calls=%async_computation.5 | async-start | bytes 5308416 | tf_op jit(solution)/shard_map/all_gather | solution.py:189
  102.8 28.1 %copy-start.20 = (bf16[16,1536]{1,0:T(8,128)(2,1)S(1)}, bf16[16,1536]{1,0:T(8,128)(2,1)}, u32[]{:S(2)}) copy-start(bf16[16,1536]{1,0:T(8,128)(2,1)} %get-tuple-element.42) | copy-start | bytes 147460
  102.8 46.5 %all-to-all-start.2 = ((bf16[32,16,1536]{2,1,0:T(8,128)(2,1)}), bf16[32,16,1536]{2,1,0:T(8,128)(2,1)S(1)}, u32[]{:S(2)}, u32[]{:S(2)}) async-start(bf16[32,16,1536]{2,1,0:T(8,128)(2,1)} %get-tuple-element.34), calls=%async_computation.2 | async-start | bytes 3145728 | tf_op jit(solution)/shard_map/all_to_all | solution.py:193
  113.9 14.4 %collective-permute-start = (bf16[16,1536]{1,0:T(8,128)(2,1)S(1)}, bf16[16,1536]{1,0:T(8,128)(2,1)S(1)}, u32[]{:S(2)}, u32[]{:S(2)}) collective-permute-start(bf16[16,1536]{1,0:T(8,128)(2,1)S(1)} %copy-done.26), channel_id=1, source_target_pairs={{0,1},{1,2},{2,3},{3,4},{4,5},{5,6},{6,7},{7,0},{8,9},{9,10},{10,1... | collective-permute-start | bytes 147464 | tf_op jit(solution)/shard_map/ppermute | solution.py:191
  115.3 15.5 %collective-permute-start.1 = (bf16[16,1536]{1,0:T(8,128)(2,1)S(1)}, bf16[16,1536]{1,0:T(8,128)(2,1)S(1)}, u32[]{:S(2)}, u32[]{:S(2)}) collective-permute-start(bf16[16,1536]{1,0:T(8,128)(2,1)S(1)} %copy-done.25), channel_id=1, source_target_pairs={{0,2},{1,3},{2,4},{3,5},{4,6},{5,7},{6,0},{7,1},{8,10},{9,11},{10,... | collective-permute-start | bytes 147464 | tf_op jit(solution)/shard_map/ppermute | solution.py:191
  118.4 14.2 %collective-permute-start.2 = (bf16[16,1536]{1,0:T(8,128)(2,1)S(1)}, bf16[16,1536]{1,0:T(8,128)(2,1)S(1)}, u32[]{:S(2)}, u32[]{:S(2)}) collective-permute-start(bf16[16,1536]{1,0:T(8,128)(2,1)S(1)} %copy-done.24), channel_id=1, source_target_pairs={{0,3},{1,4},{2,5},{3,6},{4,7},{5,0},{6,1},{7,2},{8,11},{9,12},{10,... | collective-permute-start | bytes 147464 | tf_op jit(solution)/shard_map/ppermute | solution.py:191
  122.0 12.4 %collective-permute-start.3 = (bf16[16,1536]{1,0:T(8,128)(2,1)S(1)}, bf16[16,1536]{1,0:T(8,128)(2,1)S(1)}, u32[]{:S(2)}, u32[]{:S(2)}) collective-permute-start(bf16[16,1536]{1,0:T(8,128)(2,1)S(1)} %copy-done.23), channel_id=1, source_target_pairs={{0,4},{1,5},{2,6},{3,7},{4,0},{5,1},{6,2},{7,3},{8,12},{9,13},{10,... | collective-permute-start | bytes 147464 | tf_op jit(solution)/shard_map/ppermute | solution.py:191
  124.5 10.3 %collective-permute-start.4 = (bf16[16,1536]{1,0:T(8,128)(2,1)S(1)}, bf16[16,1536]{1,0:T(8,128)(2,1)S(1)}, u32[]{:S(2)}, u32[]{:S(2)}) collective-permute-start(bf16[16,1536]{1,0:T(8,128)(2,1)S(1)} %copy-done.22), channel_id=1, source_target_pairs={{0,5},{1,6},{2,7},{3,0},{4,1},{5,2},{6,3},{7,4},{8,13},{9,14},{10,... | collective-permute-start | bytes 147464 | tf_op jit(solution)/shard_map/ppermute | solution.py:191
  128.3 28.7 %copy-start.3 = (bf16[16,1536]{1,0:T(8,128)(2,1)}, bf16[16,1536]{1,0:T(8,128)(2,1)S(1)}, u32[]{:S(2)}) copy-start(bf16[16,1536]{1,0:T(8,128)(2,1)S(1)} %collective-permute-done.refs_1_) | copy-start | bytes 147460
  128.3 6.5 %collective-permute-start.5 = (bf16[16,1536]{1,0:T(8,128)(2,1)S(1)}, bf16[16,1536]{1,0:T(8,128)(2,1)S(1)}, u32[]{:S(2)}, u32[]{:S(2)}) collective-permute-start(bf16[16,1536]{1,0:T(8,128)(2,1)S(1)} %copy-done.21), channel_id=1, source_target_pairs={{0,6},{1,7},{2,0},{3,1},{4,2},{5,3},{6,4},{7,5},{8,14},{9,15},{10,... | collective-permute-start | bytes 147464 | tf_op jit(solution)/shard_map/ppermute | solution.py:191
  130.9 5.0 %collective-permute-start.6 = (bf16[16,1536]{1,0:T(8,128)(2,1)S(1)}, bf16[16,1536]{1,0:T(8,128)(2,1)S(1)}, u32[]{:S(2)}, u32[]{:S(2)}) collective-permute-start(bf16[16,1536]{1,0:T(8,128)(2,1)S(1)} %copy-done.20), channel_id=1, source_target_pairs={{0,7},{1,0},{2,1},{3,2},{4,3},{5,4},{6,5},{7,6},{8,15},{9,8},{10,9... | collective-permute-start | bytes 147464 | tf_op jit(solution)/shard_map/ppermute | solution.py:191
  157.1 43.2 %all-to-all-start.3 = ((bf16[32,16,1536]{2,1,0:T(8,128)(2,1)}), bf16[32,16,1536]{2,1,0:T(8,128)(2,1)S(1)}, u32[]{:S(2)}, u32[]{:S(2)}) async-start(bf16[32,16,1536]{2,1,0:T(8,128)(2,1)} %near.1), calls=%async_computation.3 | async-start | bytes 3145728 | tf_op jit(solution)/shard_map/all_to_all | solution.py:220
  169.1 14.7 %collective-permute-start.8 = (bf16[16,1536]{1,0:T(8,128)(2,1)}, bf16[16,1536]{1,0:T(8,128)(2,1)S(1)}, u32[]{:S(2)}, u32[]{:S(2)}) collective-permute-start(bf16[16,1536]{1,0:T(8,128)(2,1)} %get-tuple-element.54), channel_id=1, source_target_pairs={{0,7},{1,0},{2,1},{3,2},{4,3},{5,4},{6,5},{7,6},{8,15},{9,8},{10,9... | collective-permute-start | bytes 147464 | tf_op jit(solution)/shard_map/ppermute | solution.py:191
  169.6 16.8 %collective-permute-start.9 = (bf16[16,1536]{1,0:T(8,128)(2,1)}, bf16[16,1536]{1,0:T(8,128)(2,1)S(1)}, u32[]{:S(2)}, u32[]{:S(2)}) collective-permute-start(bf16[16,1536]{1,0:T(8,128)(2,1)} %get-tuple-element.55), channel_id=1, source_target_pairs={{0,6},{1,7},{2,0},{3,1},{4,2},{5,3},{6,4},{7,5},{8,14},{9,15},{10,... | collective-permute-start | bytes 147464 | tf_op jit(solution)/shard_map/ppermute | solution.py:191
  173.9 26.3 %collective-permute-start.10 = (bf16[16,1536]{1,0:T(8,128)(2,1)}, bf16[16,1536]{1,0:T(8,128)(2,1)S(1)}, u32[]{:S(2)}, u32[]{:S(2)}) collective-permute-start(bf16[16,1536]{1,0:T(8,128)(2,1)} %get-tuple-element.56), channel_id=1, source_target_pairs={{0,5},{1,6},{2,7},{3,0},{4,1},{5,2},{6,3},{7,4},{8,13},{9,14},{10,... | collective-permute-start | bytes 147464 | tf_op jit(solution)/shard_map/ppermute | solution.py:191
  176.7 23.5 %collective-permute-start.11 = (bf16[16,1536]{1,0:T(8,128)(2,1)}, bf16[16,1536]{1,0:T(8,128)(2,1)S(1)}, u32[]{:S(2)}, u32[]{:S(2)}) collective-permute-start(bf16[16,1536]{1,0:T(8,128)(2,1)} %get-tuple-element.57), channel_id=1, source_target_pairs={{0,4},{1,5},{2,6},{3,7},{4,0},{5,1},{6,2},{7,3},{8,12},{9,13},{10,... | collective-permute-start | bytes 147464 | tf_op jit(solution)/shard_map/ppermute | solution.py:191
  181.0 19.2 %collective-permute-start.12 = (bf16[16,1536]{1,0:T(8,128)(2,1)}, bf16[16,1536]{1,0:T(8,128)(2,1)S(1)}, u32[]{:S(2)}, u32[]{:S(2)}) collective-permute-start(bf16[16,1536]{1,0:T(8,128)(2,1)} %get-tuple-element.58), channel_id=1, source_target_pairs={{0,3},{1,4},{2,5},{3,6},{4,7},{5,0},{6,1},{7,2},{8,11},{9,12},{10,... | collective-permute-start | bytes 147464 | tf_op jit(solution)/shard_map/ppermute | solution.py:191
  183.8 16.5 %collective-permute-start.13 = (bf16[16,1536]{1,0:T(8,128)(2,1)}, bf16[16,1536]{1,0:T(8,128)(2,1)S(1)}, u32[]{:S(2)}, u32[]{:S(2)}) collective-permute-start(bf16[16,1536]{1,0:T(8,128)(2,1)} %get-tuple-element.59), channel_id=1, source_target_pairs={{0,2},{1,3},{2,4},{3,5},{4,6},{5,7},{6,0},{7,1},{8,10},{9,11},{10,... | collective-permute-start | bytes 147464 | tf_op jit(solution)/shard_map/ppermute | solution.py:191
  186.4 13.9 %collective-permute-start.14 = (bf16[16,1536]{1,0:T(8,128)(2,1)}, bf16[16,1536]{1,0:T(8,128)(2,1)S(1)}, u32[]{:S(2)}, u32[]{:S(2)}) collective-permute-start(bf16[16,1536]{1,0:T(8,128)(2,1)} %get-tuple-element.60), channel_id=1, source_target_pairs={{0,1},{1,2},{2,3},{3,4},{4,5},{5,6},{6,7},{7,0},{8,9},{9,10},{10,1... | collective-permute-start | bytes 147464 | tf_op jit(solution)/shard_map/ppermute | solution.py:191
  (24 other events, 319.1 us)
Sparse Core Ops, SparseCore 0:
  26.8 73.8 all-gather.5
  102.8 61.8 all-gather.3

commit v5 on v4

--- a/solution.py
+++ b/solution.py
@@ -32,11 +32,33 @@
     out_ref[...] = part.astype(BF).reshape(8, 64, 1536)
 
 
-def piece_kernel(place_ref, wg_ref, wu_ref, wd_ref, out_ref):
-    out_ref[0:192, :] = wg_ref[0]
-    out_ref[192:384, :] = wu_ref[0]
-    for i in range(3):
-        out_ref[384 + i * 64 : 448 + i * 64, :] = wd_ref[0, :, i * 512 : (i + 1) * 512]
+def piece_kernel(place_ref, wg_ref, wu_ref, wd_ref, out_ref, sems):
+    tp = place_ref[4]
+    wide, thin = pl.ds(pl.multiple_of(tp * 192, 64), 192), pl.ds(pl.multiple_of(tp * 64, 64), 64)
+    moves = [(wg_ref.at[0, wide, :], 0, 192), (wu_ref.at[0, wide, :], 192, 192)]
+    moves += [(wd_ref.at[0, thin, i * 512 : (i + 1) * 512], 384 + i * 64, 64) for i in range(3)]
+    copies = [
+        pltpu.make_async_copy(source, out_ref.at[at : at + count, :], sems.at[i])
+        for i, (source, at, count) in enumerate(moves)
+    ]
+    for copy in copies:
+        copy.start()
+    for copy in copies:
+        copy.wait()
+
+
+def choose_kernel(place_ref, pieces_ref, out_ref, sems):
+    from_row = 3 - 3 * place_ref[3]
+    copies = [
+        pltpu.make_async_copy(
+            pieces_ref.at[from_row, i * 144 : (i + 1) * 144, :], out_ref.at[i * 144 : (i + 1) * 144, :], sems.at[i]
+        )
+        for i in range(4)
+    ]
+    for copy in copies:
+        copy.start()
+    for copy in copies:
+        copy.wait()
 
 
 def one_hot_rows(routed, expert, rank_of):
@@ -86,7 +108,8 @@
 
 
 def near_kernel(x_ref, wg_ref, wu_ref, wd_ref, out_ref):
-    y = expert(x_ref[...].reshape(256, 1536), wg_ref[0], wu_ref[0], wd_ref[0])
+    half = pl.ds(pl.program_id(0) * 16, 16)
+    y = expert(x_ref[half].reshape(256, 1536), wg_ref[0], wu_ref[0], wd_ref[0])
     out_ref[...] = y.reshape(16, CAP, 1536)
 
 
@@ -145,19 +168,13 @@
     my_routes = lax.dynamic_slice_in_dim(routes, tp * 64, 64, 0)
     my_gates = lax.dynamic_slice_in_dim(gates, tp * 64, 64, 0)
 
+    anywhere = pl.BlockSpec(memory_space=pltpu.HBM)
     piece = pl.pallas_call(
         piece_kernel,
-        grid_spec=pltpu.PrefetchScalarGridSpec(
-            num_scalar_prefetch=1,
-            grid=(1,),
-            in_specs=[
-                pl.BlockSpec((1, 192, 512), lambda i, p: (0, p[4], 0)),
-                pl.BlockSpec((1, 192, 512), lambda i, p: (0, p[4], 0)),
-                pl.BlockSpec((1, 64, 1536), lambda i, p: (0, p[4], 0)),
-            ],
-            out_specs=pl.BlockSpec((576, 512), lambda i, p: (0, 0)),
-        ),
         out_shape=shape((576, 512), BF),
+        in_specs=[smem()] + [anywhere] * 3,
+        out_specs=anywhere,
+        scratch_shapes=[pltpu.SemaphoreType.DMA((5,))],
         compiler_params=params(),
         name="piece",
     )(place, w_gate, w_up, w_down)
@@ -185,7 +202,15 @@
     )(place, keep(parts), my_routes, gain_mix.reshape(1, 1536))
 
     pieces, _ = lax.optimization_barrier((pieces, send))
-    far_piece = lax.dynamic_index_in_dim(pieces, 3 - 3 * h, 0, keepdims=False)
+    far_piece = pl.pallas_call(
+        choose_kernel,
+        out_shape=shape((576, 512), BF),
+        in_specs=[smem(), anywhere],
+        out_specs=anywhere,
+        scratch_shapes=[pltpu.SemaphoreType.DMA((4,))],
+        compiler_params=params(),
+        name="choose",
+    )(place, pieces)
     far_weights = lax.all_gather(far_piece, "tp", axis=0, tiled=False)
 
     shift = lambda v, k: lax.ppermute(v, ("x", "c"), [(i, (i + k) % 8) for i in range(8)])
@@ -193,21 +218,15 @@
     received = lax.all_to_all(send, ("y", "x", "c"), 0, 0, tiled=True)
     received, far = lax.optimization_barrier((received, far))
 
-    whole = lambda *dims: pl.BlockSpec(dims, lambda i: (0,) * len(dims))
     near = pl.pallas_call(
         near_kernel,
         grid=(2,),
         out_shape=shape((32, CAP, 1536), BF),
-        in_specs=[
-            pl.BlockSpec((16, CAP, 1536), lambda i: (i, 0, 0)),
-            whole(1, 1536, 512),
-            whole(1, 1536, 512),
-            whole(1, 512, 1536),
-        ],
+        in_specs=[vmem()] * 4,
         out_specs=pl.BlockSpec((16, CAP, 1536), lambda i: (i, 0, 0)),
-        compiler_params=params(),
+        compiler_params=pltpu.CompilerParams(vmem_limit_bytes=40 * 1024 * 1024),
         name="near",
-    )(received, w_gate, w_up, w_down)
+    )(keep(received), keep(w_gate), w_up, w_down)
     far = pl.pallas_call(
         far_kernel,
         out_shape=(rows,) * 8,

time: 229 us -> 263 us (1.15)
  Pallas kernels: 22.7 us -> 56.7 us
    pallas_call x1 -> x2, Pallas kernels: 2.79 us -> 39.5 us  [the longest x1 19.8 us: per_device(): pl.pallas_call(piece_kernel, out_shape=shape((576, 512), BF), in_specs=[s...]
    pallas_call x1, Pallas kernels: 6.51 us -> 3.86 us  [per_device(): pl.pallas_call(near_kernel, grid=(2,), out_shape=shape((32, CAP, 1536), B...]
    unnamed x56 -> x52, local copies, waits for them, and re-layouts: 4.12 us -> 5.76 us
  transfers between devices with their start and end apart: 21 -> 21, of which waited for: 8 -> 9; matrix products, arithmetic and copies ran while one was open for 2% -> 2% of each run, Pallas kernels for 7% -> 6%
where the time goes in v5:
time: 263 us; the launch traced here: 262 us
  waiting for transfers between devices  85.5 us (33%)
  starting transfers between devices  78.8 us (30%)
  Pallas kernels  56.7 us (22%)
  blocking collectives  16.7 us (6%)
  between operations  13.8 us (5%)
  local copies, waits for them, and re-layouts  10.2 us (4%)
    ppermute x14, starting transfers between devices, per_device(): lax.ppermute(v, ('x', 'c'), [(i, (i + k) % 8) for i in range(8)])  37 us
    all_to_all x1, waiting for transfers between devices, per_device(): parts = lax.all_to_all(parts, 'tp', 0, 0, tiled=True)  36.8 us
    pallas_call x1, Pallas kernels, per_device(): pl.pallas_call(piece_kernel, out_shape=shape((576, 512), BF), in_specs=[s...  19.8 us
    all_to_all x1, waiting for transfers between devices, per_device(): lax.all_to_all(jnp.broadcast_to(w_out.T[None], (64, 24, 192)), EP, 0, 0,...  19.7 us
    pallas_call x1, Pallas kernels, per_device(): pl.pallas_call(choose_kernel, out_shape=shape((576, 512), BF), in_specs=[...  19.7 us
    all_to_all x1, blocking collectives, per_device(): return lax.all_to_all(finished, 'tp', 0, 0, tiled=True).reshape(512, 192)  16.7 us
    all_to_all x1, waiting for transfers between devices, per_device(): received = lax.all_to_all(send, ('y', 'x', 'c'), 0, 0, tiled=True)  13.1 us
    all_to_all x1, starting transfers between devices, per_device(): lax.all_to_all(jnp.broadcast_to(w_out.T[None], (64, 24, 192)), EP, 0, 0,...  12.2 us
  transfers between devices with their start and end apart: 21, of which 9 were waited for; matrix products, arithmetic and copies ran while one was open for 2% of the time, Pallas kernels for 6%

profile of v5, /device:TPU:57, one launch (start us, length us, event | category | flops | bytes accessed | tf_op | source)
XLA Modules:
  0.0 261.7 jit_solution(7215168138704022511)
XLA Ops:
  7.2 19.8 %piece.1 = bf16[576,512]{1,0:T(8,128)(2,1)} custom-call(s32[6]{0:T(128)} %stack.27.place_ref, bf16[1,1536,512]{2,1,0:T(8,128)(2,1)} %wg_ref.3, bf16[1,1536,512]{2,1,0:T(8,128)(2,1)} %wu_ref.3, bf16[1,512,1536]{2,1,0:T(8,128)(2,1)} %wd_ref.3), custom_call_target="tpu_custom_call" | custom-call | tf_op jit(solution)/shard_map/piece/pallas_call | solution.py:172
  28.7 12.2 %all-to-all-start = ((bf16[64,24,192]{2,1,0:T(8,128)(2,1)}), bf16[64,24,192]{2,1,0:T(8,128)(2,1)S(1)}, u32[]{:S(2)}, u32[]{:S(2)}) async-start(bf16[64,24,192]{2,1,0:T(8,128)(2,1)} %broadcast_in_dim.2), calls=%async_computation | async-start | bytes 1572864 | tf_op jit(solution)/shard_map/all_to_all | solution.py:182
  41.8 19.7 %all-to-all-done.w_ref = bf16[64,24,192]{2,1,0:T(8,128)(2,1)S(1)} async-done(((bf16[64,24,192]{2,1,0:T(8,128)(2,1)}), bf16[64,24,192]{2,1,0:T(8,128)(2,1)S(1)}, u32[]{:S(2)}, u32[]{:S(2)}) %all-to-all-start) | async-done | bytes 589856 | tf_op jit(solution)/shard_map/all_to_all | solution.py:182
  61.6 3.2 %project.1 = bf16[8,64,1536]{2,1,0:T(8,128)(2,1)} custom-call(s32[6]{0:T(128)} %stack.27.place_ref, bf16[192,512]{1,0:T(8,128)(2,1)} %bitcast.15, bf16[192,512]{1,0:T(8,128)(2,1)} %bitcast.16, bf16[64,24,192]{2,1,0:T(8,128)(2,1)S(1)} %all-to-all-done.w_ref), custom_call_target="tpu_custom_call" | custom-call | tf_op jit(solution)/shard_map/project/pallas_call | solution.py:185
  64.8 10.2 %all-to-all-start.1 = ((bf16[8,64,1536]{2,1,0:T(8,128)(2,1)}), bf16[8,64,1536]{2,1,0:T(8,128)(2,1)S(1)}, u32[]{:S(2)}, u32[]{:S(2)}) async-start(bf16[8,64,1536]{2,1,0:T(8,128)(2,1)} %project.1), calls=%async_computation.1 | async-start | bytes 3145728 | tf_op jit(solution)/shard_map/all_to_all | solution.py:193
  76.4 36.8 %all-to-all-done.1.part_ref = bf16[8,64,1536]{2,1,0:T(8,128)(2,1)S(1)} async-done(((bf16[8,64,1536]{2,1,0:T(8,128)(2,1)}), bf16[8,64,1536]{2,1,0:T(8,128)(2,1)S(1)}, u32[]{:S(2)}, u32[]{:S(2)}) %all-to-all-start.1) | async-done | bytes 1572896 | tf_op jit(solution)/shard_map/all_to_all | solution.py:193
  113.2 3.1 %mix.1 = (bf16[32,16,1536]{2,1,0:T(8,128)(2,1)}, f32[64,1536]{1,0:T(8,128)}, bf16[16,1536]{1,0:T(8,128)(2,1)}, bf16[16,1536]{1,0:T(8,128)(2,1)}, bf16[16,1536]{1...) custom-call(s32[6]{0:T(128)} %stack.27.place_ref, ...), custom_call_target="tpu_custom_call" | custom-call | tf_op jit(solution)/shard_map/mix/pallas_call | solution.py:195
  117.8 19.7 %choose.1 = bf16[576,512]{1,0:T(8,128)(2,1)} custom-call(s32[6]{0:T(128)} %stack.27.place_ref, bf16[4,576,512]{2,1,0:T(8,128)(2,1)} %bitcast.13), custom_call_target="tpu_custom_call" | custom-call | tf_op jit(solution)/shard_map/choose/pallas_call | solution.py:205
  137.5 11.0 %all-to-all-start.2 = ((bf16[32,16,1536]{2,1,0:T(8,128)(2,1)}), bf16[32,16,1536]{2,1,0:T(8,128)(2,1)S(1)}, u32[]{:S(2)}, u32[]{:S(2)}) async-start(bf16[32,16,1536]{2,1,0:T(8,128)(2,1)} %get-tuple-element.34), calls=%async_computation.2 | async-start | bytes 3145728 | tf_op jit(solution)/shard_map/all_to_all | solution.py:218
  150.0 3.1 %collective-permute-start.1 = (bf16[16,1536]{1,0:T(8,128)(2,1)S(1)}, bf16[16,1536]{1,0:T(8,128)(2,1)S(1)}, u32[]{:S(2)}, u32[]{:S(2)}) collective-permute-start(bf16[16,1536]{1,0:T(8,128)(2,1)S(1)} %copy-done.23), channel_id=1, source_target_pairs={{0,2},{1,3},{2,4},{3,5},{4,6},{5,7},{6,0},{7,1},{8,10},{9,11},{10,... | collective-permute-start | bytes 147464 | tf_op jit(solution)/shard_map/ppermute | solution.py:216
  153.1 3.6 %collective-permute-start.2 = (bf16[16,1536]{1,0:T(8,128)(2,1)}, bf16[16,1536]{1,0:T(8,128)(2,1)S(1)}, u32[]{:S(2)}, u32[]{:S(2)}) collective-permute-start(bf16[16,1536]{1,0:T(8,128)(2,1)} %get-tuple-element.38), channel_id=1, source_target_pairs={{0,3},{1,4},{2,5},{3,6},{4,7},{5,0},{6,1},{7,2},{8,11},{9,12},{10,... | collective-permute-start | bytes 147464 | tf_op jit(solution)/shard_map/ppermute | solution.py:216
  159.1 3.8 %collective-permute-start.4 = (bf16[16,1536]{1,0:T(8,128)(2,1)}, bf16[16,1536]{1,0:T(8,128)(2,1)S(1)}, u32[]{:S(2)}, u32[]{:S(2)}) collective-permute-start(bf16[16,1536]{1,0:T(8,128)(2,1)} %get-tuple-element.40), channel_id=1, source_target_pairs={{0,5},{1,6},{2,7},{3,0},{4,1},{5,2},{6,3},{7,4},{8,13},{9,14},{10,... | collective-permute-start | bytes 147464 | tf_op jit(solution)/shard_map/ppermute | solution.py:216
  163.0 2.5 collective-permute-start.5
  170.8 13.1 %all-to-all-done.2.x_ref = bf16[32,16,1536]{2,1,0:T(8,128)(2,1)S(1)} async-done(((bf16[32,16,1536]{2,1,0:T(8,128)(2,1)}), bf16[32,16,1536]{2,1,0:T(8,128)(2,1)S(1)}, u32[]{:S(2)}, u32[]{:S(2)}) %all-to-all-start.2) | async-done | bytes 1572896 | tf_op jit(solution)/shard_map/all_to_all | solution.py:218
  186.8 3.9 %near.1 = bf16[32,16,1536]{2,1,0:T(8,128)(2,1)} custom-call(bf16[32,16,1536]{2,1,0:T(8,128)(2,1)S(1)} %all-to-all-done.2.x_ref, bf16[1,1536,512]{2,1,0:T(8,128)(2,1)S(1)} %copy-done.1, bf16[1,1536,512]{2,1,0:T(8,128)(2,1)S(1)} %copy-done.2, bf16[1,512,1536]{2,1,0:T(8,128)(2,1)S(1)} %copy-done.3), custom_call_target="tpu_custom_call" | custom-call | tf_op jit(solution)/shard_map/near/pallas_call | solution.py:221
  190.7 7.7 %all-to-all-start.3 = ((bf16[32,16,1536]{2,1,0:T(8,128)(2,1)}), bf16[32,16,1536]{2,1,0:T(8,128)(2,1)S(1)}, u32[]{:S(2)}, u32[]{:S(2)}) async-start(bf16[32,16,1536]{2,1,0:T(8,128)(2,1)} %near.1), calls=%async_computation.3 | async-start | bytes 3145728 | tf_op jit(solution)/shard_map/all_to_all | solution.py:239
  199.5 4.2 %far.1 = (bf16[16,1536]{1,0:T(8,128)(2,1)}, bf16[16,1536]{1,0:T(8,128)(2,1)}, bf16[16,1536]{1,0:T(8,128)(2,1)}, bf16[16,1536]{1,0:T(8,128)(2,1)}, bf16[16,1536]{...) custom-call(bf16[16,1536]{1,0:T(8,128)(2,1)} %get-tuple-element.44.refs_0_, ...), custom_call_target="tpu_custom_call" | custom-call | tf_op jit(solution)/shard_map/far/pallas_call | solution.py:230
  204.4 4.3 %collective-permute-start.9 = (bf16[16,1536]{1,0:T(8,128)(2,1)}, bf16[16,1536]{1,0:T(8,128)(2,1)S(1)}, u32[]{:S(2)}, u32[]{:S(2)}) collective-permute-start(bf16[16,1536]{1,0:T(8,128)(2,1)} %get-tuple-element.55), channel_id=1, source_target_pairs={{0,6},{1,7},{2,0},{3,1},{4,2},{5,3},{6,4},{7,5},{8,14},{9,15},{10,... | collective-permute-start | bytes 147464 | tf_op jit(solution)/shard_map/ppermute | solution.py:216
  208.7 2.6 %collective-permute-start.10 = (bf16[16,1536]{1,0:T(8,128)(2,1)}, bf16[16,1536]{1,0:T(8,128)(2,1)S(1)}, u32[]{:S(2)}, u32[]{:S(2)}) collective-permute-start(bf16[16,1536]{1,0:T(8,128)(2,1)} %get-tuple-element.56), channel_id=1, source_target_pairs={{0,5},{1,6},{2,7},{3,0},{4,1},{5,2},{6,3},{7,4},{8,13},{9,14},{10,... | collective-permute-start | bytes 147464 | tf_op jit(solution)/shard_map/ppermute | solution.py:216
  211.4 4.3 %collective-permute-start.11 = (bf16[16,1536]{1,0:T(8,128)(2,1)}, bf16[16,1536]{1,0:T(8,128)(2,1)S(1)}, u32[]{:S(2)}, u32[]{:S(2)}) collective-permute-start(bf16[16,1536]{1,0:T(8,128)(2,1)} %get-tuple-element.57), channel_id=1, source_target_pairs={{0,4},{1,5},{2,6},{3,7},{4,0},{5,1},{6,2},{7,3},{8,12},{9,13},{10,... | collective-permute-start | bytes 147464 | tf_op jit(solution)/shard_map/ppermute | solution.py:216
  215.7 2.9 %collective-permute-start.12 = (bf16[16,1536]{1,0:T(8,128)(2,1)}, bf16[16,1536]{1,0:T(8,128)(2,1)S(1)}, u32[]{:S(2)}, u32[]{:S(2)}) collective-permute-start(bf16[16,1536]{1,0:T(8,128)(2,1)} %get-tuple-element.58), channel_id=1, source_target_pairs={{0,3},{1,4},{2,5},{3,6},{4,7},{5,0},{6,1},{7,2},{8,11},{9,12},{10,... | collective-permute-start | bytes 147464 | tf_op jit(solution)/shard_map/ppermute | solution.py:216
  224.2 9.6 %all-to-all-done.3.near_ref = bf16[32,16,1536]{2,1,0:T(8,128)(2,1)S(1)} async-done(((bf16[32,16,1536]{2,1,0:T(8,128)(2,1)}), bf16[32,16,1536]{2,1,0:T(8,128)(2,1)S(1)}, u32[]{:S(2)}, u32[]{:S(2)}) %all-to-all-start.3) | async-done | bytes 1572896 | tf_op jit(solution)/shard_map/all_to_all | solution.py:239
  234.6 2.8 %close.1 = bf16[8,64,192]{2,1,0:T(8,128)(2,1)} custom-call(s32[6]{0:T(128)} %stack.27.place_ref, s32[64,8]{1,0:T(8,128)} %copy.14.routes_ref, f32[64,8]{1,0:T(8,128)} %copy.15.gates_ref, f32[64,1536]{1,0:T(8,128)} %get-tuple-element.33.hid_ref, f32[1,1536]{1,0:T(1,128)} %reshape.11.gain_ref, bf16[32,16,1536]{2,1,0:T(8,128)(2,1)S(1)} %all-to-all-done.3.near_ref, ...), custom_call_target="tpu_custom_call" | custom-call | tf_op jit(solution)/shard_map/close/pallas_call | solution.py:242
  237.4 16.7 %all_to_all.25 = bf16[8,64,192]{2,1,0:T(8,128)(2,1)S(1)} all-to-all(bf16[8,64,192]{2,1,0:T(8,128)(2,1)} %close.1), channel_id=1, replica_groups=mesh['tp'=8,'h'=2,'y'=4,'x'=4,'c'=2] {'tp'}, dimensions={0} | all-to-all | bytes 393216 | tf_op jit(solution)/shard_map/all_to_all | solution.py:250
  (87 shorter events, 27.0 us)
Async XLA Ops:
  6.5 68.5 %copy-start = (s32[512,8]{0,1:T(8,128)S(1)}, s32[512,8]{0,1:T(8,128)}, u32[]{:S(2)}) copy-start(s32[512,8]{0,1:T(8,128)} %param.15) | copy-start | bytes 49156
  27.0 13.9 %collective-permute-start.7 = (bf16[576,512]{1,0:T(8,128)(2,1)}, bf16[576,512]{1,0:T(8,128)(2,1)S(1)}, u32[]{:S(2)}, u32[]{:S(2)}) collective-permute-start(bf16[576,512]{1,0:T(8,128)(2,1)} %piece.1), channel_id=1, source_target_pairs={{32,24},{24,32},{33,25},{25,33},{34,26},{26,34},{35,27},{27,35},{3... | collective-permute-start | bytes 1769480 | tf_op jit(solution)/shard_map/ppermute | solution.py:181
  28.7 32.9 %all-to-all-start = ((bf16[64,24,192]{2,1,0:T(8,128)(2,1)}), bf16[64,24,192]{2,1,0:T(8,128)(2,1)S(1)}, u32[]{:S(2)}, u32[]{:S(2)}) async-start(bf16[64,24,192]{2,1,0:T(8,128)(2,1)} %broadcast_in_dim.2), calls=%async_computation | async-start | bytes 1572864 | tf_op jit(solution)/shard_map/all_to_all | solution.py:182
  40.9 76.9 %all-gather.5.cloned.1.call-start = ((), (), s32[]{:S(2)}) async-start(), calls=%async_computation.5 | async-start | bytes 2949120 | tf_op jit(solution)/shard_map/all_gather | solution.py:183
  64.8 48.4 %all-to-all-start.1 = ((bf16[8,64,1536]{2,1,0:T(8,128)(2,1)}), bf16[8,64,1536]{2,1,0:T(8,128)(2,1)S(1)}, u32[]{:S(2)}, u32[]{:S(2)}) async-start(bf16[8,64,1536]{2,1,0:T(8,128)(2,1)} %project.1), calls=%async_computation.1 | async-start | bytes 3145728 | tf_op jit(solution)/shard_map/all_to_all | solution.py:193
  74.9 124.6 %all-gather.7.cloned.1.call-start = ((), (), s32[]{:S(2)}) async-start(), calls=%async_computation.6 | async-start | bytes 5308416 | tf_op jit(solution)/shard_map/all_gather | solution.py:214
  137.5 28.0 %copy-start.22 = (bf16[16,1536]{1,0:T(8,128)(2,1)S(1)}, bf16[16,1536]{1,0:T(8,128)(2,1)}, u32[]{:S(2)}) copy-start(bf16[16,1536]{1,0:T(8,128)(2,1)} %get-tuple-element.42) | copy-start | bytes 147460
  137.5 46.4 %copy-start.1 = (bf16[1,1536,512]{2,1,0:T(8,128)(2,1)S(1)}, bf16[1,1536,512]{2,1,0:T(8,128)(2,1)}, u32[]{:S(2)}) copy-start(bf16[1,1536,512]{2,1,0:T(8,128)(2,1)} %wg_ref.3) | copy-start | bytes 4718596
  137.5 46.4 %all-to-all-start.2 = ((bf16[32,16,1536]{2,1,0:T(8,128)(2,1)}), bf16[32,16,1536]{2,1,0:T(8,128)(2,1)S(1)}, u32[]{:S(2)}, u32[]{:S(2)}) async-start(bf16[32,16,1536]{2,1,0:T(8,128)(2,1)} %get-tuple-element.34), calls=%async_computation.2 | async-start | bytes 3145728 | tf_op jit(solution)/shard_map/all_to_all | solution.py:218
  148.5 14.4 %collective-permute-start = (bf16[16,1536]{1,0:T(8,128)(2,1)S(1)}, bf16[16,1536]{1,0:T(8,128)(2,1)S(1)}, u32[]{:S(2)}, u32[]{:S(2)}) collective-permute-start(bf16[16,1536]{1,0:T(8,128)(2,1)S(1)} %copy-done.24), channel_id=1, source_target_pairs={{0,1},{1,2},{2,3},{3,4},{4,5},{5,6},{6,7},{7,0},{8,9},{9,10},{10,1... | collective-permute-start | bytes 147464 | tf_op jit(solution)/shard_map/ppermute | solution.py:216
  150.0 15.5 %collective-permute-start.1 = (bf16[16,1536]{1,0:T(8,128)(2,1)S(1)}, bf16[16,1536]{1,0:T(8,128)(2,1)S(1)}, u32[]{:S(2)}, u32[]{:S(2)}) collective-permute-start(bf16[16,1536]{1,0:T(8,128)(2,1)S(1)} %copy-done.23), channel_id=1, source_target_pairs={{0,2},{1,3},{2,4},{3,5},{4,6},{5,7},{6,0},{7,1},{8,10},{9,11},{10,... | collective-permute-start | bytes 147464 | tf_op jit(solution)/shard_map/ppermute | solution.py:216
  153.1 14.2 %collective-permute-start.2 = (bf16[16,1536]{1,0:T(8,128)(2,1)}, bf16[16,1536]{1,0:T(8,128)(2,1)S(1)}, u32[]{:S(2)}, u32[]{:S(2)}) collective-permute-start(bf16[16,1536]{1,0:T(8,128)(2,1)} %get-tuple-element.38), channel_id=1, source_target_pairs={{0,3},{1,4},{2,5},{3,6},{4,7},{5,0},{6,1},{7,2},{8,11},{9,12},{10,... | collective-permute-start | bytes 147464 | tf_op jit(solution)/shard_map/ppermute | solution.py:216
  156.7 12.4 %collective-permute-start.3 = (bf16[16,1536]{1,0:T(8,128)(2,1)}, bf16[16,1536]{1,0:T(8,128)(2,1)S(1)}, u32[]{:S(2)}, u32[]{:S(2)}) collective-permute-start(bf16[16,1536]{1,0:T(8,128)(2,1)} %get-tuple-element.39), channel_id=1, source_target_pairs={{0,4},{1,5},{2,6},{3,7},{4,0},{5,1},{6,2},{7,3},{8,12},{9,13},{10,... | collective-permute-start | bytes 147464 | tf_op jit(solution)/shard_map/ppermute | solution.py:216
  159.1 10.4 %collective-permute-start.4 = (bf16[16,1536]{1,0:T(8,128)(2,1)}, bf16[16,1536]{1,0:T(8,128)(2,1)S(1)}, u32[]{:S(2)}, u32[]{:S(2)}) collective-permute-start(bf16[16,1536]{1,0:T(8,128)(2,1)} %get-tuple-element.40), channel_id=1, source_target_pairs={{0,5},{1,6},{2,7},{3,0},{4,1},{5,2},{6,3},{7,4},{8,13},{9,14},{10,... | collective-permute-start | bytes 147464 | tf_op jit(solution)/shard_map/ppermute | solution.py:216
  163.0 6.5 %collective-permute-start.5 = (bf16[16,1536]{1,0:T(8,128)(2,1)}, bf16[16,1536]{1,0:T(8,128)(2,1)S(1)}, u32[]{:S(2)}, u32[]{:S(2)}) collective-permute-start(bf16[16,1536]{1,0:T(8,128)(2,1)} %get-tuple-element.41), channel_id=1, source_target_pairs={{0,6},{1,7},{2,0},{3,1},{4,2},{5,3},{6,4},{7,5},{8,14},{9,15},{10,... | collective-permute-start | bytes 147464 | tf_op jit(solution)/shard_map/ppermute | solution.py:216
  165.5 5.3 %collective-permute-start.6 = (bf16[16,1536]{1,0:T(8,128)(2,1)S(1)}, bf16[16,1536]{1,0:T(8,128)(2,1)S(1)}, u32[]{:S(2)}, u32[]{:S(2)}) collective-permute-start(bf16[16,1536]{1,0:T(8,128)(2,1)S(1)} %copy-done.22), channel_id=1, source_target_pairs={{0,7},{1,0},{2,1},{3,2},{4,3},{5,4},{6,5},{7,6},{8,15},{9,8},{10,9... | collective-permute-start | bytes 147464 | tf_op jit(solution)/shard_map/ppermute | solution.py:216
  190.7 43.1 %all-to-all-start.3 = ((bf16[32,16,1536]{2,1,0:T(8,128)(2,1)}), bf16[32,16,1536]{2,1,0:T(8,128)(2,1)S(1)}, u32[]{:S(2)}, u32[]{:S(2)}) async-start(bf16[32,16,1536]{2,1,0:T(8,128)(2,1)} %near.1), calls=%async_computation.3 | async-start | bytes 3145728 | tf_op jit(solution)/shard_map/all_to_all | solution.py:239
  203.7 14.8 %collective-permute-start.8 = (bf16[16,1536]{1,0:T(8,128)(2,1)}, bf16[16,1536]{1,0:T(8,128)(2,1)S(1)}, u32[]{:S(2)}, u32[]{:S(2)}) collective-permute-start(bf16[16,1536]{1,0:T(8,128)(2,1)} %get-tuple-element.54), channel_id=1, source_target_pairs={{0,7},{1,0},{2,1},{3,2},{4,3},{5,4},{6,5},{7,6},{8,15},{9,8},{10,9... | collective-permute-start | bytes 147464 | tf_op jit(solution)/shard_map/ppermute | solution.py:216
  204.4 16.7 %collective-permute-start.9 = (bf16[16,1536]{1,0:T(8,128)(2,1)}, bf16[16,1536]{1,0:T(8,128)(2,1)S(1)}, u32[]{:S(2)}, u32[]{:S(2)}) collective-permute-start(bf16[16,1536]{1,0:T(8,128)(2,1)} %get-tuple-element.55), channel_id=1, source_target_pairs={{0,6},{1,7},{2,0},{3,1},{4,2},{5,3},{6,4},{7,5},{8,14},{9,15},{10,... | collective-permute-start | bytes 147464 | tf_op jit(solution)/shard_map/ppermute | solution.py:216
  208.7 25.1 %collective-permute-start.10 = (bf16[16,1536]{1,0:T(8,128)(2,1)}, bf16[16,1536]{1,0:T(8,128)(2,1)S(1)}, u32[]{:S(2)}, u32[]{:S(2)}) collective-permute-start(bf16[16,1536]{1,0:T(8,128)(2,1)} %get-tuple-element.56), channel_id=1, source_target_pairs={{0,5},{1,6},{2,7},{3,0},{4,1},{5,2},{6,3},{7,4},{8,13},{9,14},{10,... | collective-permute-start | bytes 147464 | tf_op jit(solution)/shard_map/ppermute | solution.py:216
  211.4 22.5 %collective-permute-start.11 = (bf16[16,1536]{1,0:T(8,128)(2,1)}, bf16[16,1536]{1,0:T(8,128)(2,1)S(1)}, u32[]{:S(2)}, u32[]{:S(2)}) collective-permute-start(bf16[16,1536]{1,0:T(8,128)(2,1)} %get-tuple-element.57), channel_id=1, source_target_pairs={{0,4},{1,5},{2,6},{3,7},{4,0},{5,1},{6,2},{7,3},{8,12},{9,13},{10,... | collective-permute-start | bytes 147464 | tf_op jit(solution)/shard_map/ppermute | solution.py:216
  215.7 18.2 %collective-permute-start.12 = (bf16[16,1536]{1,0:T(8,128)(2,1)}, bf16[16,1536]{1,0:T(8,128)(2,1)S(1)}, u32[]{:S(2)}, u32[]{:S(2)}) collective-permute-start(bf16[16,1536]{1,0:T(8,128)(2,1)} %get-tuple-element.58), channel_id=1, source_target_pairs={{0,3},{1,4},{2,5},{3,6},{4,7},{5,0},{6,1},{7,2},{8,11},{9,12},{10,... | collective-permute-start | bytes 147464 | tf_op jit(solution)/shard_map/ppermute | solution.py:216
  218.6 15.3 %collective-permute-start.13 = (bf16[16,1536]{1,0:T(8,128)(2,1)}, bf16[16,1536]{1,0:T(8,128)(2,1)S(1)}, u32[]{:S(2)}, u32[]{:S(2)}) collective-permute-start(bf16[16,1536]{1,0:T(8,128)(2,1)} %get-tuple-element.59), channel_id=1, source_target_pairs={{0,2},{1,3},{2,4},{3,5},{4,6},{5,7},{6,0},{7,1},{8,10},{9,11},{10,... | collective-permute-start | bytes 147464 | tf_op jit(solution)/shard_map/ppermute | solution.py:216
  221.1 12.8 %collective-permute-start.14 = (bf16[16,1536]{1,0:T(8,128)(2,1)}, bf16[16,1536]{1,0:T(8,128)(2,1)S(1)}, u32[]{:S(2)}, u32[]{:S(2)}) collective-permute-start(bf16[16,1536]{1,0:T(8,128)(2,1)} %get-tuple-element.60), channel_id=1, source_target_pairs={{0,1},{1,2},{2,3},{3,4},{4,5},{5,6},{6,7},{7,0},{8,9},{9,10},{10,1... | collective-permute-start | bytes 147464 | tf_op jit(solution)/shard_map/ppermute | solution.py:216
  (22 other events, 274.6 us)
Sparse Core Ops, SparseCore 0:
  43.8 73.9 all-gather.4
  137.6 61.8 all-gather.6

commit v6 on v4

--- a/solution.py
+++ b/solution.py
@@ -33,10 +33,10 @@
 
 
 def piece_kernel(place_ref, wg_ref, wu_ref, wd_ref, out_ref):
-    out_ref[0:192, :] = wg_ref[0]
-    out_ref[192:384, :] = wu_ref[0]
+    out_ref[0:48, :] = wg_ref[0]
+    out_ref[48:96, :] = wu_ref[0]
     for i in range(3):
-        out_ref[384 + i * 64 : 448 + i * 64, :] = wd_ref[0, :, i * 512 : (i + 1) * 512]
+        out_ref[96 + i * 16 : 112 + i * 16, :] = wd_ref[0, :, i * 512 : (i + 1) * 512]
 
 
 def one_hot_rows(routed, expert, rank_of):
@@ -86,17 +86,21 @@
 
 
 def near_kernel(x_ref, wg_ref, wu_ref, wd_ref, out_ref):
-    y = expert(x_ref[...].reshape(256, 1536), wg_ref[0], wu_ref[0], wd_ref[0])
+    half = pl.ds(pl.program_id(0) * 16, 16)
+    y = expert(x_ref[half].reshape(256, 1536), wg_ref[0], wu_ref[0], wd_ref[0])
     out_ref[...] = y.reshape(16, CAP, 1536)
 
 
 def far_kernel(*refs):
     x_refs, w_ref, out_refs, (wg_scr, wu_scr, wd_scr) = refs[0:8], refs[8], refs[9:17], refs[17:]
     for z in range(8):
-        wg_scr[z * 192 : (z + 1) * 192, :] = w_ref[z, 0:192, :]
-        wu_scr[z * 192 : (z + 1) * 192, :] = w_ref[z, 192:384, :]
-        for i in range(3):
-            wd_scr[z * 64 : (z + 1) * 64, i * 512 : (i + 1) * 512] = w_ref[z, 384 + i * 64 : 448 + i * 64, :]
+        for q in range(4):
+            block, at = z * 4 + q, q * 144
+            wg_scr[block * 48 : (block + 1) * 48, :] = w_ref[z, at : at + 48, :]
+            wu_scr[block * 48 : (block + 1) * 48, :] = w_ref[z, at + 48 : at + 96, :]
+            for i in range(3):
+                down = w_ref[z, at + 96 + i * 16 : at + 112 + i * 16, :]
+                wd_scr[block * 16 : (block + 1) * 16, i * 512 : (i + 1) * 512] = down
     x = jnp.concatenate([ref[...] for ref in x_refs], axis=0)
     y = expert(x, wg_scr[...], wu_scr[...], wd_scr[...])
     for k in range(8):
@@ -149,13 +153,13 @@
         piece_kernel,
         grid_spec=pltpu.PrefetchScalarGridSpec(
             num_scalar_prefetch=1,
-            grid=(1,),
+            grid=(4,),
             in_specs=[
-                pl.BlockSpec((1, 192, 512), lambda i, p: (0, p[4], 0)),
-                pl.BlockSpec((1, 192, 512), lambda i, p: (0, p[4], 0)),
-                pl.BlockSpec((1, 64, 1536), lambda i, p: (0, p[4], 0)),
+                pl.BlockSpec((1, 48, 512), lambda i, p: (0, p[4] * 4 + i, 0)),
+                pl.BlockSpec((1, 48, 512), lambda i, p: (0, p[4] * 4 + i, 0)),
+                pl.BlockSpec((1, 16, 1536), lambda i, p: (0, p[4] * 4 + i, 0)),
             ],
-            out_specs=pl.BlockSpec((576, 512), lambda i, p: (0, 0)),
+            out_specs=pl.BlockSpec((144, 512), lambda i, p: (i, 0)),
         ),
         out_shape=shape((576, 512), BF),
         compiler_params=params(),
@@ -193,21 +197,15 @@
     received = lax.all_to_all(send, ("y", "x", "c"), 0, 0, tiled=True)
     received, far = lax.optimization_barrier((received, far))
 
-    whole = lambda *dims: pl.BlockSpec(dims, lambda i: (0,) * len(dims))
     near = pl.pallas_call(
         near_kernel,
         grid=(2,),
         out_shape=shape((32, CAP, 1536), BF),
-        in_specs=[
-            pl.BlockSpec((16, CAP, 1536), lambda i: (i, 0, 0)),
-            whole(1, 1536, 512),
-            whole(1, 1536, 512),
-            whole(1, 512, 1536),
-        ],
+        in_specs=[vmem()] * 4,
         out_specs=pl.BlockSpec((16, CAP, 1536), lambda i: (i, 0, 0)),
-        compiler_params=params(),
+        compiler_params=pltpu.CompilerParams(vmem_limit_bytes=40 * 1024 * 1024),
         name="near",
-    )(received, w_gate, w_up, w_down)
+    )(keep(received), keep(w_gate), w_up, w_down)
     far = pl.pallas_call(
         far_kernel,
         out_shape=(rows,) * 8,

time: 229 us -> 229 us (level)
    pallas_call x1, Pallas kernels: 6.51 us -> 3.86 us  [per_device(): pl.pallas_call(near_kernel, grid=(2,), out_shape=shape((32, CAP, 1536), B...]
    unnamed x56 -> x52, local copies, waits for them, and re-layouts: 4.12 us -> 5.76 us
  transfers between devices with their start and end apart: 21 -> 21, of which waited for: 8 -> 9; matrix products, arithmetic and copies ran while one was open for 2% -> 2% of each run, Pallas kernels for 7% -> 6%
where the time goes in v6:
time: 229 us; the launch traced here: 228 us
  waiting for transfers between devices  85.5 us (37%)
  starting transfers between devices  78.8 us (34%)
  Pallas kernels  21.1 us (9%)
  blocking collectives  16.7 us (7%)
  between operations  13.8 us (6%)
  local copies, waits for them, and re-layouts  12.1 us (5%)
    ppermute x14, starting transfers between devices, per_device(): lax.ppermute(v, ('x', 'c'), [(i, (i + k) % 8) for i in range(8)])  37 us
    all_to_all x1, waiting for transfers between devices, per_device(): parts = lax.all_to_all(parts, 'tp', 0, 0, tiled=True)  36.8 us
    all_to_all x1, waiting for transfers between devices, per_device(): lax.all_to_all(jnp.broadcast_to(w_out.T[None], (64, 24, 192)), EP, 0, 0,...  19.7 us
    all_to_all x1, blocking collectives, per_device(): return lax.all_to_all(finished, 'tp', 0, 0, tiled=True).reshape(512, 192)  16.7 us
    all_to_all x1, waiting for transfers between devices, per_device(): received = lax.all_to_all(send, ('y', 'x', 'c'), 0, 0, tiled=True)  13.1 us
    all_to_all x1, starting transfers between devices, per_device(): lax.all_to_all(jnp.broadcast_to(w_out.T[None], (64, 24, 192)), EP, 0, 0,...  12.2 us
    all_to_all x1, starting transfers between devices, per_device(): received = lax.all_to_all(send, ('y', 'x', 'c'), 0, 0, tiled=True)  11 us
    all_to_all x1, starting transfers between devices, per_device(): parts = lax.all_to_all(parts, 'tp', 0, 0, tiled=True)  10.2 us
  transfers between devices with their start and end apart: 21, of which 9 were waited for; matrix products, arithmetic and copies ran while one was open for 2% of the time, Pallas kernels for 6%

profile of v6, /device:TPU:57, one launch (start us, length us, event | category | flops | bytes accessed | tf_op | source)
XLA Modules:
  0.0 228.0 jit_solution(12580830577523466314)
XLA Ops:
  7.2 3.9 %piece.1 = bf16[576,512]{1,0:T(8,128)(2,1)} custom-call(s32[6]{0:T(128)} %stack.27.place_ref, bf16[1,1536,512]{2,1,0:T(8,128)(2,1)} %wg_ref.3, bf16[1,1536,512]{2,1,0:T(8,128)(2,1)} %wu_ref.3, bf16[1,512,1536]{2,1,0:T(8,128)(2,1)} %wd_ref.3), custom_call_target="tpu_custom_call" | custom-call | tf_op jit(solution)/shard_map/piece/pallas_call | solution.py:152
  12.7 12.2 %all-to-all-start = ((bf16[64,24,192]{2,1,0:T(8,128)(2,1)}), bf16[64,24,192]{2,1,0:T(8,128)(2,1)S(1)}, u32[]{:S(2)}, u32[]{:S(2)}) async-start(bf16[64,24,192]{2,1,0:T(8,128)(2,1)} %broadcast_in_dim.2), calls=%async_computation | async-start | bytes 1572864 | tf_op jit(solution)/shard_map/all_to_all | solution.py:169
  25.9 19.7 %all-to-all-done.w_ref = bf16[64,24,192]{2,1,0:T(8,128)(2,1)S(1)} async-done(((bf16[64,24,192]{2,1,0:T(8,128)(2,1)}), bf16[64,24,192]{2,1,0:T(8,128)(2,1)S(1)}, u32[]{:S(2)}, u32[]{:S(2)}) %all-to-all-start) | async-done | bytes 589856 | tf_op jit(solution)/shard_map/all_to_all | solution.py:169
  45.6 3.2 %project.1 = bf16[8,64,1536]{2,1,0:T(8,128)(2,1)} custom-call(s32[6]{0:T(128)} %stack.27.place_ref, bf16[192,512]{1,0:T(8,128)(2,1)} %bitcast.12, bf16[192,512]{1,0:T(8,128)(2,1)} %bitcast.13, bf16[64,24,192]{2,1,0:T(8,128)(2,1)S(1)} %all-to-all-done.w_ref), custom_call_target="tpu_custom_call" | custom-call | tf_op jit(solution)/shard_map/project/pallas_call | solution.py:172
  48.8 10.2 %all-to-all-start.1 = ((bf16[8,64,1536]{2,1,0:T(8,128)(2,1)}), bf16[8,64,1536]{2,1,0:T(8,128)(2,1)S(1)}, u32[]{:S(2)}, u32[]{:S(2)}) async-start(bf16[8,64,1536]{2,1,0:T(8,128)(2,1)} %project.1), calls=%async_computation.1 | async-start | bytes 3145728 | tf_op jit(solution)/shard_map/all_to_all | solution.py:180
  60.4 36.8 %all-to-all-done.1.part_ref = bf16[8,64,1536]{2,1,0:T(8,128)(2,1)S(1)} async-done(((bf16[8,64,1536]{2,1,0:T(8,128)(2,1)}), bf16[8,64,1536]{2,1,0:T(8,128)(2,1)S(1)}, u32[]{:S(2)}, u32[]{:S(2)}) %all-to-all-start.1) | async-done | bytes 1572896 | tf_op jit(solution)/shard_map/all_to_all | solution.py:180
  97.3 3.1 %mix.1 = (bf16[32,16,1536]{2,1,0:T(8,128)(2,1)}, f32[64,1536]{1,0:T(8,128)}, bf16[16,1536]{1,0:T(8,128)(2,1)}, bf16[16,1536]{1,0:T(8,128)(2,1)}, bf16[16,1536]{1...) custom-call(s32[6]{0:T(128)} %stack.27.place_ref, ...), custom_call_target="tpu_custom_call" | custom-call | tf_op jit(solution)/shard_map/mix/pallas_call | solution.py:182
  103.8 11.0 %all-to-all-start.2 = ((bf16[32,16,1536]{2,1,0:T(8,128)(2,1)}), bf16[32,16,1536]{2,1,0:T(8,128)(2,1)S(1)}, u32[]{:S(2)}, u32[]{:S(2)}) async-start(bf16[32,16,1536]{2,1,0:T(8,128)(2,1)} %get-tuple-element.34), calls=%async_computation.2 | async-start | bytes 3145728 | tf_op jit(solution)/shard_map/all_to_all | solution.py:197
  116.3 3.1 %collective-permute-start.1 = (bf16[16,1536]{1,0:T(8,128)(2,1)S(1)}, bf16[16,1536]{1,0:T(8,128)(2,1)S(1)}, u32[]{:S(2)}, u32[]{:S(2)}) collective-permute-start(bf16[16,1536]{1,0:T(8,128)(2,1)S(1)} %copy-done.23), channel_id=1, source_target_pairs={{0,2},{1,3},{2,4},{3,5},{4,6},{5,7},{6,0},{7,1},{8,10},{9,11},{10,... | collective-permute-start | bytes 147464 | tf_op jit(solution)/shard_map/ppermute | solution.py:195
  119.4 3.6 %collective-permute-start.2 = (bf16[16,1536]{1,0:T(8,128)(2,1)}, bf16[16,1536]{1,0:T(8,128)(2,1)S(1)}, u32[]{:S(2)}, u32[]{:S(2)}) collective-permute-start(bf16[16,1536]{1,0:T(8,128)(2,1)} %get-tuple-element.38), channel_id=1, source_target_pairs={{0,3},{1,4},{2,5},{3,6},{4,7},{5,0},{6,1},{7,2},{8,11},{9,12},{10,... | collective-permute-start | bytes 147464 | tf_op jit(solution)/shard_map/ppermute | solution.py:195
  125.4 3.8 %collective-permute-start.4 = (bf16[16,1536]{1,0:T(8,128)(2,1)}, bf16[16,1536]{1,0:T(8,128)(2,1)S(1)}, u32[]{:S(2)}, u32[]{:S(2)}) collective-permute-start(bf16[16,1536]{1,0:T(8,128)(2,1)} %get-tuple-element.40), channel_id=1, source_target_pairs={{0,5},{1,6},{2,7},{3,0},{4,1},{5,2},{6,3},{7,4},{8,13},{9,14},{10,... | collective-permute-start | bytes 147464 | tf_op jit(solution)/shard_map/ppermute | solution.py:195
  129.2 2.5 %collective-permute-start.5 = (bf16[16,1536]{1,0:T(8,128)(2,1)}, bf16[16,1536]{1,0:T(8,128)(2,1)S(1)}, u32[]{:S(2)}, u32[]{:S(2)}) collective-permute-start(bf16[16,1536]{1,0:T(8,128)(2,1)} %get-tuple-element.41), channel_id=1, source_target_pairs={{0,6},{1,7},{2,0},{3,1},{4,2},{5,3},{6,4},{7,5},{8,14},{9,15},{10,... | collective-permute-start | bytes 147464 | tf_op jit(solution)/shard_map/ppermute | solution.py:195
  137.1 13.1 %all-to-all-done.2.x_ref = bf16[32,16,1536]{2,1,0:T(8,128)(2,1)S(1)} async-done(((bf16[32,16,1536]{2,1,0:T(8,128)(2,1)}), bf16[32,16,1536]{2,1,0:T(8,128)(2,1)S(1)}, u32[]{:S(2)}, u32[]{:S(2)}) %all-to-all-start.2) | async-done | bytes 1572896 | tf_op jit(solution)/shard_map/all_to_all | solution.py:197
  153.1 3.9 %near.1 = bf16[32,16,1536]{2,1,0:T(8,128)(2,1)} custom-call(bf16[32,16,1536]{2,1,0:T(8,128)(2,1)S(1)} %all-to-all-done.2.x_ref, bf16[1,1536,512]{2,1,0:T(8,128)(2,1)S(1)} %copy-done.1, bf16[1,1536,512]{2,1,0:T(8,128)(2,1)S(1)} %copy-done.2, bf16[1,512,1536]{2,1,0:T(8,128)(2,1)S(1)} %copy-done.3), custom_call_target="tpu_custom_call" | custom-call | tf_op jit(solution)/shard_map/near/pallas_call | solution.py:200
  157.0 7.7 %all-to-all-start.3 = ((bf16[32,16,1536]{2,1,0:T(8,128)(2,1)}), bf16[32,16,1536]{2,1,0:T(8,128)(2,1)S(1)}, u32[]{:S(2)}, u32[]{:S(2)}) async-start(bf16[32,16,1536]{2,1,0:T(8,128)(2,1)} %near.1), calls=%async_computation.3 | async-start | bytes 3145728 | tf_op jit(solution)/shard_map/all_to_all | solution.py:218
  165.8 4.2 %far.1 = (bf16[16,1536]{1,0:T(8,128)(2,1)}, bf16[16,1536]{1,0:T(8,128)(2,1)}, bf16[16,1536]{1,0:T(8,128)(2,1)}, bf16[16,1536]{1,0:T(8,128)(2,1)}, bf16[16,1536]{...) custom-call(bf16[16,1536]{1,0:T(8,128)(2,1)} %get-tuple-element.44.refs_0_, ...), custom_call_target="tpu_custom_call" | custom-call | tf_op jit(solution)/shard_map/far/pallas_call | solution.py:209
  170.7 4.3 %collective-permute-start.9 = (bf16[16,1536]{1,0:T(8,128)(2,1)}, bf16[16,1536]{1,0:T(8,128)(2,1)S(1)}, u32[]{:S(2)}, u32[]{:S(2)}) collective-permute-start(bf16[16,1536]{1,0:T(8,128)(2,1)} %get-tuple-element.55), channel_id=1, source_target_pairs={{0,6},{1,7},{2,0},{3,1},{4,2},{5,3},{6,4},{7,5},{8,14},{9,15},{10,... | collective-permute-start | bytes 147464 | tf_op jit(solution)/shard_map/ppermute | solution.py:195
  175.0 2.7 %collective-permute-start.10 = (bf16[16,1536]{1,0:T(8,128)(2,1)}, bf16[16,1536]{1,0:T(8,128)(2,1)S(1)}, u32[]{:S(2)}, u32[]{:S(2)}) collective-permute-start(bf16[16,1536]{1,0:T(8,128)(2,1)} %get-tuple-element.56), channel_id=1, source_target_pairs={{0,5},{1,6},{2,7},{3,0},{4,1},{5,2},{6,3},{7,4},{8,13},{9,14},{10,... | collective-permute-start | bytes 147464 | tf_op jit(solution)/shard_map/ppermute | solution.py:195
  177.6 4.3 %collective-permute-start.11 = (bf16[16,1536]{1,0:T(8,128)(2,1)}, bf16[16,1536]{1,0:T(8,128)(2,1)S(1)}, u32[]{:S(2)}, u32[]{:S(2)}) collective-permute-start(bf16[16,1536]{1,0:T(8,128)(2,1)} %get-tuple-element.57), channel_id=1, source_target_pairs={{0,4},{1,5},{2,6},{3,7},{4,0},{5,1},{6,2},{7,3},{8,12},{9,13},{10,... | collective-permute-start | bytes 147464 | tf_op jit(solution)/shard_map/ppermute | solution.py:195
  182.0 2.9 %collective-permute-start.12 = (bf16[16,1536]{1,0:T(8,128)(2,1)}, bf16[16,1536]{1,0:T(8,128)(2,1)S(1)}, u32[]{:S(2)}, u32[]{:S(2)}) collective-permute-start(bf16[16,1536]{1,0:T(8,128)(2,1)} %get-tuple-element.58), channel_id=1, source_target_pairs={{0,3},{1,4},{2,5},{3,6},{4,7},{5,0},{6,1},{7,2},{8,11},{9,12},{10,... | collective-permute-start | bytes 147464 | tf_op jit(solution)/shard_map/ppermute | solution.py:195
  184.8 2.5 %collective-permute-start.13 = (bf16[16,1536]{1,0:T(8,128)(2,1)}, bf16[16,1536]{1,0:T(8,128)(2,1)S(1)}, u32[]{:S(2)}, u32[]{:S(2)}) collective-permute-start(bf16[16,1536]{1,0:T(8,128)(2,1)} %get-tuple-element.59), channel_id=1, source_target_pairs={{0,2},{1,3},{2,4},{3,5},{4,6},{5,7},{6,0},{7,1},{8,10},{9,11},{10,... | collective-permute-start | bytes 147464 | tf_op jit(solution)/shard_map/ppermute | solution.py:195
  190.5 9.7 %all-to-all-done.3.near_ref = bf16[32,16,1536]{2,1,0:T(8,128)(2,1)S(1)} async-done(((bf16[32,16,1536]{2,1,0:T(8,128)(2,1)}), bf16[32,16,1536]{2,1,0:T(8,128)(2,1)S(1)}, u32[]{:S(2)}, u32[]{:S(2)}) %all-to-all-start.3) | async-done | bytes 1572896 | tf_op jit(solution)/shard_map/all_to_all | solution.py:218
  200.9 2.8 %close.1 = bf16[8,64,192]{2,1,0:T(8,128)(2,1)} custom-call(s32[6]{0:T(128)} %stack.27.place_ref, s32[64,8]{1,0:T(8,128)} %copy.17.routes_ref, f32[64,8]{1,0:T(8,128)} %copy.18.gates_ref, f32[64,1536]{1,0:T(8,128)} %get-tuple-element.33.hid_ref, f32[1,1536]{1,0:T(1,128)} %reshape.11.gain_ref, bf16[32,16,1536]{2,1,0:T(8,128)(2,1)S(1)} %all-to-all-done.3.near_ref, ...), custom_call_target="tpu_custom_call" | custom-call | tf_op jit(solution)/shard_map/close/pallas_call | solution.py:221
  203.7 16.7 %all_to_all.25 = bf16[8,64,192]{2,1,0:T(8,128)(2,1)S(1)} all-to-all(bf16[8,64,192]{2,1,0:T(8,128)(2,1)} %close.1), channel_id=1, replica_groups=mesh['tp'=8,'h'=2,'y'=4,'x'=4,'c'=2] {'tp'}, dimensions={0} | all-to-all | bytes 393216 | tf_op jit(solution)/shard_map/all_to_all | solution.py:229
  (87 shorter events, 26.4 us)
Async XLA Ops:
  6.5 52.5 %copy-start = (s32[512,8]{0,1:T(8,128)S(1)}, s32[512,8]{0,1:T(8,128)}, u32[]{:S(2)}) copy-start(s32[512,8]{0,1:T(8,128)} %param.15) | copy-start | bytes 49156
  11.1 13.9 %collective-permute-start.7 = (bf16[576,512]{1,0:T(8,128)(2,1)}, bf16[576,512]{1,0:T(8,128)(2,1)S(1)}, u32[]{:S(2)}, u32[]{:S(2)}) collective-permute-start(bf16[576,512]{1,0:T(8,128)(2,1)} %piece.1), channel_id=1, source_target_pairs={{32,24},{24,32},{33,25},{25,33},{34,26},{26,34},{35,27},{27,35},{3... | collective-permute-start | bytes 1769480 | tf_op jit(solution)/shard_map/ppermute | solution.py:168
  12.7 32.9 %all-to-all-start = ((bf16[64,24,192]{2,1,0:T(8,128)(2,1)}), bf16[64,24,192]{2,1,0:T(8,128)(2,1)S(1)}, u32[]{:S(2)}, u32[]{:S(2)}) async-start(bf16[64,24,192]{2,1,0:T(8,128)(2,1)} %broadcast_in_dim.2), calls=%async_computation | async-start | bytes 1572864 | tf_op jit(solution)/shard_map/all_to_all | solution.py:169
  24.9 76.9 %all-gather.6.cloned.1.call-start = ((), (), s32[]{:S(2)}) async-start(), calls=%async_computation.6 | async-start | bytes 2949120 | tf_op jit(solution)/shard_map/all_gather | solution.py:170
  48.8 48.4 %all-to-all-start.1 = ((bf16[8,64,1536]{2,1,0:T(8,128)(2,1)}), bf16[8,64,1536]{2,1,0:T(8,128)(2,1)S(1)}, u32[]{:S(2)}, u32[]{:S(2)}) async-start(bf16[8,64,1536]{2,1,0:T(8,128)(2,1)} %project.1), calls=%async_computation.1 | async-start | bytes 3145728 | tf_op jit(solution)/shard_map/all_to_all | solution.py:180
  59.0 106.8 %all-gather.4.cloned.1.call-start = ((), (), s32[]{:S(2)}) async-start(), calls=%async_computation.5 | async-start | bytes 5308416 | tf_op jit(solution)/shard_map/all_gather | solution.py:193
  103.8 28.0 %copy-start.22 = (bf16[16,1536]{1,0:T(8,128)(2,1)S(1)}, bf16[16,1536]{1,0:T(8,128)(2,1)}, u32[]{:S(2)}) copy-start(bf16[16,1536]{1,0:T(8,128)(2,1)} %get-tuple-element.42) | copy-start | bytes 147460
  103.8 46.4 %copy-start.1 = (bf16[1,1536,512]{2,1,0:T(8,128)(2,1)S(1)}, bf16[1,1536,512]{2,1,0:T(8,128)(2,1)}, u32[]{:S(2)}) copy-start(bf16[1,1536,512]{2,1,0:T(8,128)(2,1)} %wg_ref.3) | copy-start | bytes 4718596
  103.8 46.4 %all-to-all-start.2 = ((bf16[32,16,1536]{2,1,0:T(8,128)(2,1)}), bf16[32,16,1536]{2,1,0:T(8,128)(2,1)S(1)}, u32[]{:S(2)}, u32[]{:S(2)}) async-start(bf16[32,16,1536]{2,1,0:T(8,128)(2,1)} %get-tuple-element.34), calls=%async_computation.2 | async-start | bytes 3145728 | tf_op jit(solution)/shard_map/all_to_all | solution.py:197
  114.8 14.4 %collective-permute-start = (bf16[16,1536]{1,0:T(8,128)(2,1)S(1)}, bf16[16,1536]{1,0:T(8,128)(2,1)S(1)}, u32[]{:S(2)}, u32[]{:S(2)}) collective-permute-start(bf16[16,1536]{1,0:T(8,128)(2,1)S(1)} %copy-done.24), channel_id=1, source_target_pairs={{0,1},{1,2},{2,3},{3,4},{4,5},{5,6},{6,7},{7,0},{8,9},{9,10},{10,1... | collective-permute-start | bytes 147464 | tf_op jit(solution)/shard_map/ppermute | solution.py:195
  116.3 15.5 %collective-permute-start.1 = (bf16[16,1536]{1,0:T(8,128)(2,1)S(1)}, bf16[16,1536]{1,0:T(8,128)(2,1)S(1)}, u32[]{:S(2)}, u32[]{:S(2)}) collective-permute-start(bf16[16,1536]{1,0:T(8,128)(2,1)S(1)} %copy-done.23), channel_id=1, source_target_pairs={{0,2},{1,3},{2,4},{3,5},{4,6},{5,7},{6,0},{7,1},{8,10},{9,11},{10,... | collective-permute-start | bytes 147464 | tf_op jit(solution)/shard_map/ppermute | solution.py:195
  119.4 14.2 %collective-permute-start.2 = (bf16[16,1536]{1,0:T(8,128)(2,1)}, bf16[16,1536]{1,0:T(8,128)(2,1)S(1)}, u32[]{:S(2)}, u32[]{:S(2)}) collective-permute-start(bf16[16,1536]{1,0:T(8,128)(2,1)} %get-tuple-element.38), channel_id=1, source_target_pairs={{0,3},{1,4},{2,5},{3,6},{4,7},{5,0},{6,1},{7,2},{8,11},{9,12},{10,... | collective-permute-start | bytes 147464 | tf_op jit(solution)/shard_map/ppermute | solution.py:195
  122.9 12.4 %collective-permute-start.3 = (bf16[16,1536]{1,0:T(8,128)(2,1)}, bf16[16,1536]{1,0:T(8,128)(2,1)S(1)}, u32[]{:S(2)}, u32[]{:S(2)}) collective-permute-start(bf16[16,1536]{1,0:T(8,128)(2,1)} %get-tuple-element.39), channel_id=1, source_target_pairs={{0,4},{1,5},{2,6},{3,7},{4,0},{5,1},{6,2},{7,3},{8,12},{9,13},{10,... | collective-permute-start | bytes 147464 | tf_op jit(solution)/shard_map/ppermute | solution.py:195
  125.4 10.4 %collective-permute-start.4 = (bf16[16,1536]{1,0:T(8,128)(2,1)}, bf16[16,1536]{1,0:T(8,128)(2,1)S(1)}, u32[]{:S(2)}, u32[]{:S(2)}) collective-permute-start(bf16[16,1536]{1,0:T(8,128)(2,1)} %get-tuple-element.40), channel_id=1, source_target_pairs={{0,5},{1,6},{2,7},{3,0},{4,1},{5,2},{6,3},{7,4},{8,13},{9,14},{10,... | collective-permute-start | bytes 147464 | tf_op jit(solution)/shard_map/ppermute | solution.py:195
  129.2 6.5 %collective-permute-start.5 = (bf16[16,1536]{1,0:T(8,128)(2,1)}, bf16[16,1536]{1,0:T(8,128)(2,1)S(1)}, u32[]{:S(2)}, u32[]{:S(2)}) collective-permute-start(bf16[16,1536]{1,0:T(8,128)(2,1)} %get-tuple-element.41), channel_id=1, source_target_pairs={{0,6},{1,7},{2,0},{3,1},{4,2},{5,3},{6,4},{7,5},{8,14},{9,15},{10,... | collective-permute-start | bytes 147464 | tf_op jit(solution)/shard_map/ppermute | solution.py:195
  131.8 5.3 %collective-permute-start.6 = (bf16[16,1536]{1,0:T(8,128)(2,1)S(1)}, bf16[16,1536]{1,0:T(8,128)(2,1)S(1)}, u32[]{:S(2)}, u32[]{:S(2)}) collective-permute-start(bf16[16,1536]{1,0:T(8,128)(2,1)S(1)} %copy-done.22), channel_id=1, source_target_pairs={{0,7},{1,0},{2,1},{3,2},{4,3},{5,4},{6,5},{7,6},{8,15},{9,8},{10,9... | collective-permute-start | bytes 147464 | tf_op jit(solution)/shard_map/ppermute | solution.py:195
  157.0 43.1 %all-to-all-start.3 = ((bf16[32,16,1536]{2,1,0:T(8,128)(2,1)}), bf16[32,16,1536]{2,1,0:T(8,128)(2,1)S(1)}, u32[]{:S(2)}, u32[]{:S(2)}) async-start(bf16[32,16,1536]{2,1,0:T(8,128)(2,1)} %near.1), calls=%async_computation.3 | async-start | bytes 3145728 | tf_op jit(solution)/shard_map/all_to_all | solution.py:218
  170.0 14.8 %collective-permute-start.8 = (bf16[16,1536]{1,0:T(8,128)(2,1)}, bf16[16,1536]{1,0:T(8,128)(2,1)S(1)}, u32[]{:S(2)}, u32[]{:S(2)}) collective-permute-start(bf16[16,1536]{1,0:T(8,128)(2,1)} %get-tuple-element.54), channel_id=1, source_target_pairs={{0,7},{1,0},{2,1},{3,2},{4,3},{5,4},{6,5},{7,6},{8,15},{9,8},{10,9... | collective-permute-start | bytes 147464 | tf_op jit(solution)/shard_map/ppermute | solution.py:195
  170.7 16.7 %collective-permute-start.9 = (bf16[16,1536]{1,0:T(8,128)(2,1)}, bf16[16,1536]{1,0:T(8,128)(2,1)S(1)}, u32[]{:S(2)}, u32[]{:S(2)}) collective-permute-start(bf16[16,1536]{1,0:T(8,128)(2,1)} %get-tuple-element.55), channel_id=1, source_target_pairs={{0,6},{1,7},{2,0},{3,1},{4,2},{5,3},{6,4},{7,5},{8,14},{9,15},{10,... | collective-permute-start | bytes 147464 | tf_op jit(solution)/shard_map/ppermute | solution.py:195
  175.0 25.2 %collective-permute-start.10 = (bf16[16,1536]{1,0:T(8,128)(2,1)}, bf16[16,1536]{1,0:T(8,128)(2,1)S(1)}, u32[]{:S(2)}, u32[]{:S(2)}) collective-permute-start(bf16[16,1536]{1,0:T(8,128)(2,1)} %get-tuple-element.56), channel_id=1, source_target_pairs={{0,5},{1,6},{2,7},{3,0},{4,1},{5,2},{6,3},{7,4},{8,13},{9,14},{10,... | collective-permute-start | bytes 147464 | tf_op jit(solution)/shard_map/ppermute | solution.py:195
  177.6 22.5 %collective-permute-start.11 = (bf16[16,1536]{1,0:T(8,128)(2,1)}, bf16[16,1536]{1,0:T(8,128)(2,1)S(1)}, u32[]{:S(2)}, u32[]{:S(2)}) collective-permute-start(bf16[16,1536]{1,0:T(8,128)(2,1)} %get-tuple-element.57), channel_id=1, source_target_pairs={{0,4},{1,5},{2,6},{3,7},{4,0},{5,1},{6,2},{7,3},{8,12},{9,13},{10,... | collective-permute-start | bytes 147464 | tf_op jit(solution)/shard_map/ppermute | solution.py:195
  182.0 18.2 %collective-permute-start.12 = (bf16[16,1536]{1,0:T(8,128)(2,1)}, bf16[16,1536]{1,0:T(8,128)(2,1)S(1)}, u32[]{:S(2)}, u32[]{:S(2)}) collective-permute-start(bf16[16,1536]{1,0:T(8,128)(2,1)} %get-tuple-element.58), channel_id=1, source_target_pairs={{0,3},{1,4},{2,5},{3,6},{4,7},{5,0},{6,1},{7,2},{8,11},{9,12},{10,... | collective-permute-start | bytes 147464 | tf_op jit(solution)/shard_map/ppermute | solution.py:195
  184.8 15.3 %collective-permute-start.13 = (bf16[16,1536]{1,0:T(8,128)(2,1)}, bf16[16,1536]{1,0:T(8,128)(2,1)S(1)}, u32[]{:S(2)}, u32[]{:S(2)}) collective-permute-start(bf16[16,1536]{1,0:T(8,128)(2,1)} %get-tuple-element.59), channel_id=1, source_target_pairs={{0,2},{1,3},{2,4},{3,5},{4,6},{5,7},{6,0},{7,1},{8,10},{9,11},{10,... | collective-permute-start | bytes 147464 | tf_op jit(solution)/shard_map/ppermute | solution.py:195
  187.4 12.8 %collective-permute-start.14 = (bf16[16,1536]{1,0:T(8,128)(2,1)}, bf16[16,1536]{1,0:T(8,128)(2,1)S(1)}, u32[]{:S(2)}, u32[]{:S(2)}) collective-permute-start(bf16[16,1536]{1,0:T(8,128)(2,1)} %get-tuple-element.60), channel_id=1, source_target_pairs={{0,1},{1,2},{2,3},{3,4},{4,5},{5,6},{6,7},{7,0},{8,9},{9,10},{10,1... | collective-permute-start | bytes 147464 | tf_op jit(solution)/shard_map/ppermute | solution.py:195
  (22 other events, 259.7 us)
Sparse Core Ops, SparseCore 0:
  27.9 73.9 all-gather.5
  103.9 61.8 all-gather.3

commit v7 on v4

--- a/solution.py
+++ b/solution.py
@@ -86,7 +86,8 @@
 
 
 def near_kernel(x_ref, wg_ref, wu_ref, wd_ref, out_ref):
-    y = expert(x_ref[...].reshape(256, 1536), wg_ref[0], wu_ref[0], wd_ref[0])
+    half = pl.ds(pl.program_id(0) * 16, 16)
+    y = expert(x_ref[half].reshape(256, 1536), wg_ref[0], wu_ref[0], wd_ref[0])
     out_ref[...] = y.reshape(16, CAP, 1536)
 
 
@@ -193,21 +194,15 @@
     received = lax.all_to_all(send, ("y", "x", "c"), 0, 0, tiled=True)
     received, far = lax.optimization_barrier((received, far))
 
-    whole = lambda *dims: pl.BlockSpec(dims, lambda i: (0,) * len(dims))
     near = pl.pallas_call(
         near_kernel,
         grid=(2,),
         out_shape=shape((32, CAP, 1536), BF),
-        in_specs=[
-            pl.BlockSpec((16, CAP, 1536), lambda i: (i, 0, 0)),
-            whole(1, 1536, 512),
-            whole(1, 1536, 512),
-            whole(1, 512, 1536),
-        ],
+        in_specs=[vmem()] * 4,
         out_specs=pl.BlockSpec((16, CAP, 1536), lambda i: (i, 0, 0)),
-        compiler_params=params(),
+        compiler_params=pltpu.CompilerParams(vmem_limit_bytes=40 * 1024 * 1024),
         name="near",
-    )(received, w_gate, w_up, w_down)
+    )(keep(received), keep(w_gate), w_up, w_down)
     far = pl.pallas_call(
         far_kernel,
         out_shape=(rows,) * 8,

time: 229 us -> 228 us (level)
  Pallas kernels: 22.7 us -> 20 us
    pallas_call x1, Pallas kernels: 6.51 us -> 3.86 us  [per_device(): pl.pallas_call(near_kernel, grid=(2,), out_shape=shape((32, CAP, 1536), B...]
    unnamed x56 -> x52, local copies, waits for them, and re-layouts: 4.12 us -> 5.76 us
  transfers between devices with their start and end apart: 21 -> 21, of which waited for: 8 -> 9; matrix products, arithmetic and copies ran while one was open for 2% -> 2% of each run, Pallas kernels for 7% -> 6%
where the time goes in v7:
time: 228 us; the launch traced here: 227 us
  waiting for transfers between devices  85.5 us (38%)
  starting transfers between devices  78.8 us (35%)
  Pallas kernels  20 us (9%)
  blocking collectives  16.7 us (7%)
  between operations  13.8 us (6%)
  local copies, waits for them, and re-layouts  12.1 us (5%)
    ppermute x14, starting transfers between devices, per_device(): lax.ppermute(v, ('x', 'c'), [(i, (i + k) % 8) for i in range(8)])  37 us
    all_to_all x1, waiting for transfers between devices, per_device(): parts = lax.all_to_all(parts, 'tp', 0, 0, tiled=True)  36.8 us
    all_to_all x1, waiting for transfers between devices, per_device(): lax.all_to_all(jnp.broadcast_to(w_out.T[None], (64, 24, 192)), EP, 0, 0,...  19.7 us
    all_to_all x1, blocking collectives, per_device(): return lax.all_to_all(finished, 'tp', 0, 0, tiled=True).reshape(512, 192)  16.7 us
    all_to_all x1, waiting for transfers between devices, per_device(): received = lax.all_to_all(send, ('y', 'x', 'c'), 0, 0, tiled=True)  13.1 us
    all_to_all x1, starting transfers between devices, per_device(): lax.all_to_all(jnp.broadcast_to(w_out.T[None], (64, 24, 192)), EP, 0, 0,...  12.2 us
    all_to_all x1, starting transfers between devices, per_device(): received = lax.all_to_all(send, ('y', 'x', 'c'), 0, 0, tiled=True)  11 us
    all_to_all x1, starting transfers between devices, per_device(): parts = lax.all_to_all(parts, 'tp', 0, 0, tiled=True)  10.2 us
  transfers between devices with their start and end apart: 21, of which 9 were waited for; matrix products, arithmetic and copies ran while one was open for 2% of the time, Pallas kernels for 6%

profile of v7, /device:TPU:57, one launch (start us, length us, event | category | flops | bytes accessed | tf_op | source)
XLA Modules:
  0.0 226.9 jit_solution(3066980085243713371)
XLA Ops:
  7.2 2.8 %piece.1 = bf16[576,512]{1,0:T(8,128)(2,1)} custom-call(s32[6]{0:T(128)} %stack.27.place_ref, bf16[1,1536,512]{2,1,0:T(8,128)(2,1)} %wg_ref.3, bf16[1,1536,512]{2,1,0:T(8,128)(2,1)} %wu_ref.3, bf16[1,512,1536]{2,1,0:T(8,128)(2,1)} %wd_ref.3), custom_call_target="tpu_custom_call" | custom-call | tf_op jit(solution)/shard_map/piece/pallas_call | solution.py:149
  11.6 12.2 %all-to-all-start = ((bf16[64,24,192]{2,1,0:T(8,128)(2,1)}), bf16[64,24,192]{2,1,0:T(8,128)(2,1)S(1)}, u32[]{:S(2)}, u32[]{:S(2)}) async-start(bf16[64,24,192]{2,1,0:T(8,128)(2,1)} %broadcast_in_dim.2), calls=%async_computation | async-start | bytes 1572864 | tf_op jit(solution)/shard_map/all_to_all | solution.py:166
  24.8 19.7 %all-to-all-done.w_ref = bf16[64,24,192]{2,1,0:T(8,128)(2,1)S(1)} async-done(((bf16[64,24,192]{2,1,0:T(8,128)(2,1)}), bf16[64,24,192]{2,1,0:T(8,128)(2,1)S(1)}, u32[]{:S(2)}, u32[]{:S(2)}) %all-to-all-start) | async-done | bytes 589856 | tf_op jit(solution)/shard_map/all_to_all | solution.py:166
  44.5 3.2 %project.1 = bf16[8,64,1536]{2,1,0:T(8,128)(2,1)} custom-call(s32[6]{0:T(128)} %stack.27.place_ref, bf16[192,512]{1,0:T(8,128)(2,1)} %bitcast.12, bf16[192,512]{1,0:T(8,128)(2,1)} %bitcast.13, bf16[64,24,192]{2,1,0:T(8,128)(2,1)S(1)} %all-to-all-done.w_ref), custom_call_target="tpu_custom_call" | custom-call | tf_op jit(solution)/shard_map/project/pallas_call | solution.py:169
  47.7 10.2 %all-to-all-start.1 = ((bf16[8,64,1536]{2,1,0:T(8,128)(2,1)}), bf16[8,64,1536]{2,1,0:T(8,128)(2,1)S(1)}, u32[]{:S(2)}, u32[]{:S(2)}) async-start(bf16[8,64,1536]{2,1,0:T(8,128)(2,1)} %project.1), calls=%async_computation.1 | async-start | bytes 3145728 | tf_op jit(solution)/shard_map/all_to_all | solution.py:177
  59.3 36.8 %all-to-all-done.1.part_ref = bf16[8,64,1536]{2,1,0:T(8,128)(2,1)S(1)} async-done(((bf16[8,64,1536]{2,1,0:T(8,128)(2,1)}), bf16[8,64,1536]{2,1,0:T(8,128)(2,1)S(1)}, u32[]{:S(2)}, u32[]{:S(2)}) %all-to-all-start.1) | async-done | bytes 1572896 | tf_op jit(solution)/shard_map/all_to_all | solution.py:177
  96.2 3.1 %mix.1 = (bf16[32,16,1536]{2,1,0:T(8,128)(2,1)}, f32[64,1536]{1,0:T(8,128)}, bf16[16,1536]{1,0:T(8,128)(2,1)}, bf16[16,1536]{1,0:T(8,128)(2,1)}, bf16[16,1536]{1...) custom-call(s32[6]{0:T(128)} %stack.27.place_ref, ...), custom_call_target="tpu_custom_call" | custom-call | tf_op jit(solution)/shard_map/mix/pallas_call | solution.py:179
  102.7 11.0 %all-to-all-start.2 = ((bf16[32,16,1536]{2,1,0:T(8,128)(2,1)}), bf16[32,16,1536]{2,1,0:T(8,128)(2,1)S(1)}, u32[]{:S(2)}, u32[]{:S(2)}) async-start(bf16[32,16,1536]{2,1,0:T(8,128)(2,1)} %get-tuple-element.34), calls=%async_computation.2 | async-start | bytes 3145728 | tf_op jit(solution)/shard_map/all_to_all | solution.py:194
  115.2 3.1 %collective-permute-start.1 = (bf16[16,1536]{1,0:T(8,128)(2,1)S(1)}, bf16[16,1536]{1,0:T(8,128)(2,1)S(1)}, u32[]{:S(2)}, u32[]{:S(2)}) collective-permute-start(bf16[16,1536]{1,0:T(8,128)(2,1)S(1)} %copy-done.23), channel_id=1, source_target_pairs={{0,2},{1,3},{2,4},{3,5},{4,6},{5,7},{6,0},{7,1},{8,10},{9,11},{10,... | collective-permute-start | bytes 147464 | tf_op jit(solution)/shard_map/ppermute | solution.py:192
  118.3 3.6 %collective-permute-start.2 = (bf16[16,1536]{1,0:T(8,128)(2,1)}, bf16[16,1536]{1,0:T(8,128)(2,1)S(1)}, u32[]{:S(2)}, u32[]{:S(2)}) collective-permute-start(bf16[16,1536]{1,0:T(8,128)(2,1)} %get-tuple-element.38), channel_id=1, source_target_pairs={{0,3},{1,4},{2,5},{3,6},{4,7},{5,0},{6,1},{7,2},{8,11},{9,12},{10,... | collective-permute-start | bytes 147464 | tf_op jit(solution)/shard_map/ppermute | solution.py:192
  124.3 3.8 %collective-permute-start.4 = (bf16[16,1536]{1,0:T(8,128)(2,1)}, bf16[16,1536]{1,0:T(8,128)(2,1)S(1)}, u32[]{:S(2)}, u32[]{:S(2)}) collective-permute-start(bf16[16,1536]{1,0:T(8,128)(2,1)} %get-tuple-element.40), channel_id=1, source_target_pairs={{0,5},{1,6},{2,7},{3,0},{4,1},{5,2},{6,3},{7,4},{8,13},{9,14},{10,... | collective-permute-start | bytes 147464 | tf_op jit(solution)/shard_map/ppermute | solution.py:192
  128.2 2.5 %collective-permute-start.5 = (bf16[16,1536]{1,0:T(8,128)(2,1)}, bf16[16,1536]{1,0:T(8,128)(2,1)S(1)}, u32[]{:S(2)}, u32[]{:S(2)}) collective-permute-start(bf16[16,1536]{1,0:T(8,128)(2,1)} %get-tuple-element.41), channel_id=1, source_target_pairs={{0,6},{1,7},{2,0},{3,1},{4,2},{5,3},{6,4},{7,5},{8,14},{9,15},{10,... | collective-permute-start | bytes 147464 | tf_op jit(solution)/shard_map/ppermute | solution.py:192
  136.0 13.1 %all-to-all-done.2.x_ref = bf16[32,16,1536]{2,1,0:T(8,128)(2,1)S(1)} async-done(((bf16[32,16,1536]{2,1,0:T(8,128)(2,1)}), bf16[32,16,1536]{2,1,0:T(8,128)(2,1)S(1)}, u32[]{:S(2)}, u32[]{:S(2)}) %all-to-all-start.2) | async-done | bytes 1572896 | tf_op jit(solution)/shard_map/all_to_all | solution.py:194
  152.0 3.9 %near.1 = bf16[32,16,1536]{2,1,0:T(8,128)(2,1)} custom-call(bf16[32,16,1536]{2,1,0:T(8,128)(2,1)S(1)} %all-to-all-done.2.x_ref, bf16[1,1536,512]{2,1,0:T(8,128)(2,1)S(1)} %copy-done.1, bf16[1,1536,512]{2,1,0:T(8,128)(2,1)S(1)} %copy-done.2, bf16[1,512,1536]{2,1,0:T(8,128)(2,1)S(1)} %copy-done.3), custom_call_target="tpu_custom_call" | custom-call | tf_op jit(solution)/shard_map/near/pallas_call | solution.py:197
  155.9 7.7 %all-to-all-start.3 = ((bf16[32,16,1536]{2,1,0:T(8,128)(2,1)}), bf16[32,16,1536]{2,1,0:T(8,128)(2,1)S(1)}, u32[]{:S(2)}, u32[]{:S(2)}) async-start(bf16[32,16,1536]{2,1,0:T(8,128)(2,1)} %near.1), calls=%async_computation.3 | async-start | bytes 3145728 | tf_op jit(solution)/shard_map/all_to_all | solution.py:215
  164.7 4.2 %far.1 = (bf16[16,1536]{1,0:T(8,128)(2,1)}, bf16[16,1536]{1,0:T(8,128)(2,1)}, bf16[16,1536]{1,0:T(8,128)(2,1)}, bf16[16,1536]{1,0:T(8,128)(2,1)}, bf16[16,1536]{...) custom-call(bf16[16,1536]{1,0:T(8,128)(2,1)} %get-tuple-element.44.refs_0_, ...), custom_call_target="tpu_custom_call" | custom-call | tf_op jit(solution)/shard_map/far/pallas_call | solution.py:206
  169.6 4.3 %collective-permute-start.9 = (bf16[16,1536]{1,0:T(8,128)(2,1)}, bf16[16,1536]{1,0:T(8,128)(2,1)S(1)}, u32[]{:S(2)}, u32[]{:S(2)}) collective-permute-start(bf16[16,1536]{1,0:T(8,128)(2,1)} %get-tuple-element.55), channel_id=1, source_target_pairs={{0,6},{1,7},{2,0},{3,1},{4,2},{5,3},{6,4},{7,5},{8,14},{9,15},{10,... | collective-permute-start | bytes 147464 | tf_op jit(solution)/shard_map/ppermute | solution.py:192
  173.9 2.7 %collective-permute-start.10 = (bf16[16,1536]{1,0:T(8,128)(2,1)}, bf16[16,1536]{1,0:T(8,128)(2,1)S(1)}, u32[]{:S(2)}, u32[]{:S(2)}) collective-permute-start(bf16[16,1536]{1,0:T(8,128)(2,1)} %get-tuple-element.56), channel_id=1, source_target_pairs={{0,5},{1,6},{2,7},{3,0},{4,1},{5,2},{6,3},{7,4},{8,13},{9,14},{10,... | collective-permute-start | bytes 147464 | tf_op jit(solution)/shard_map/ppermute | solution.py:192
  176.6 4.3 %collective-permute-start.11 = (bf16[16,1536]{1,0:T(8,128)(2,1)}, bf16[16,1536]{1,0:T(8,128)(2,1)S(1)}, u32[]{:S(2)}, u32[]{:S(2)}) collective-permute-start(bf16[16,1536]{1,0:T(8,128)(2,1)} %get-tuple-element.57), channel_id=1, source_target_pairs={{0,4},{1,5},{2,6},{3,7},{4,0},{5,1},{6,2},{7,3},{8,12},{9,13},{10,... | collective-permute-start | bytes 147464 | tf_op jit(solution)/shard_map/ppermute | solution.py:192
  180.9 2.9 %collective-permute-start.12 = (bf16[16,1536]{1,0:T(8,128)(2,1)}, bf16[16,1536]{1,0:T(8,128)(2,1)S(1)}, u32[]{:S(2)}, u32[]{:S(2)}) collective-permute-start(bf16[16,1536]{1,0:T(8,128)(2,1)} %get-tuple-element.58), channel_id=1, source_target_pairs={{0,3},{1,4},{2,5},{3,6},{4,7},{5,0},{6,1},{7,2},{8,11},{9,12},{10,... | collective-permute-start | bytes 147464 | tf_op jit(solution)/shard_map/ppermute | solution.py:192
  183.8 2.5 %collective-permute-start.13 = (bf16[16,1536]{1,0:T(8,128)(2,1)}, bf16[16,1536]{1,0:T(8,128)(2,1)S(1)}, u32[]{:S(2)}, u32[]{:S(2)}) collective-permute-start(bf16[16,1536]{1,0:T(8,128)(2,1)} %get-tuple-element.59), channel_id=1, source_target_pairs={{0,2},{1,3},{2,4},{3,5},{4,6},{5,7},{6,0},{7,1},{8,10},{9,11},{10,... | collective-permute-start | bytes 147464 | tf_op jit(solution)/shard_map/ppermute | solution.py:192
  189.4 9.6 %all-to-all-done.3.near_ref = bf16[32,16,1536]{2,1,0:T(8,128)(2,1)S(1)} async-done(((bf16[32,16,1536]{2,1,0:T(8,128)(2,1)}), bf16[32,16,1536]{2,1,0:T(8,128)(2,1)S(1)}, u32[]{:S(2)}, u32[]{:S(2)}) %all-to-all-start.3) | async-done | bytes 1572896 | tf_op jit(solution)/shard_map/all_to_all | solution.py:215
  199.8 2.8 %close.1 = bf16[8,64,192]{2,1,0:T(8,128)(2,1)} custom-call(s32[6]{0:T(128)} %stack.27.place_ref, s32[64,8]{1,0:T(8,128)} %copy.17.routes_ref, f32[64,8]{1,0:T(8,128)} %copy.18.gates_ref, f32[64,1536]{1,0:T(8,128)} %get-tuple-element.33.hid_ref, f32[1,1536]{1,0:T(1,128)} %reshape.11.gain_ref, bf16[32,16,1536]{2,1,0:T(8,128)(2,1)S(1)} %all-to-all-done.3.near_ref, ...), custom_call_target="tpu_custom_call" | custom-call | tf_op jit(solution)/shard_map/close/pallas_call | solution.py:218
  202.6 16.7 %all_to_all.25 = bf16[8,64,192]{2,1,0:T(8,128)(2,1)S(1)} all-to-all(bf16[8,64,192]{2,1,0:T(8,128)(2,1)} %close.1), channel_id=1, replica_groups=mesh['tp'=8,'h'=2,'y'=4,'x'=4,'c'=2] {'tp'}, dimensions={0} | all-to-all | bytes 393216 | tf_op jit(solution)/shard_map/all_to_all | solution.py:226
  (87 shorter events, 26.4 us)
Async XLA Ops:
  6.5 51.4 %copy-start = (s32[512,8]{0,1:T(8,128)S(1)}, s32[512,8]{0,1:T(8,128)}, u32[]{:S(2)}) copy-start(s32[512,8]{0,1:T(8,128)} %param.15) | copy-start | bytes 49156
  10.0 13.9 %collective-permute-start.7 = (bf16[576,512]{1,0:T(8,128)(2,1)}, bf16[576,512]{1,0:T(8,128)(2,1)S(1)}, u32[]{:S(2)}, u32[]{:S(2)}) collective-permute-start(bf16[576,512]{1,0:T(8,128)(2,1)} %piece.1), channel_id=1, source_target_pairs={{32,24},{24,32},{33,25},{25,33},{34,26},{26,34},{35,27},{27,35},{3... | collective-permute-start | bytes 1769480 | tf_op jit(solution)/shard_map/ppermute | solution.py:165
  11.6 32.9 %all-to-all-start = ((bf16[64,24,192]{2,1,0:T(8,128)(2,1)}), bf16[64,24,192]{2,1,0:T(8,128)(2,1)S(1)}, u32[]{:S(2)}, u32[]{:S(2)}) async-start(bf16[64,24,192]{2,1,0:T(8,128)(2,1)} %broadcast_in_dim.2), calls=%async_computation | async-start | bytes 1572864 | tf_op jit(solution)/shard_map/all_to_all | solution.py:166
  23.8 76.9 %all-gather.6.cloned.1.call-start = ((), (), s32[]{:S(2)}) async-start(), calls=%async_computation.6 | async-start | bytes 2949120 | tf_op jit(solution)/shard_map/all_gather | solution.py:167
  47.7 48.4 %all-to-all-start.1 = ((bf16[8,64,1536]{2,1,0:T(8,128)(2,1)}), bf16[8,64,1536]{2,1,0:T(8,128)(2,1)S(1)}, u32[]{:S(2)}, u32[]{:S(2)}) async-start(bf16[8,64,1536]{2,1,0:T(8,128)(2,1)} %project.1), calls=%async_computation.1 | async-start | bytes 3145728 | tf_op jit(solution)/shard_map/all_to_all | solution.py:177
  57.9 106.8 %all-gather.4.cloned.1.call-start = ((), (), s32[]{:S(2)}) async-start(), calls=%async_computation.5 | async-start | bytes 5308416 | tf_op jit(solution)/shard_map/all_gather | solution.py:190
  102.7 28.0 %copy-start.22 = (bf16[16,1536]{1,0:T(8,128)(2,1)S(1)}, bf16[16,1536]{1,0:T(8,128)(2,1)}, u32[]{:S(2)}) copy-start(bf16[16,1536]{1,0:T(8,128)(2,1)} %get-tuple-element.42) | copy-start | bytes 147460
  102.7 46.4 %copy-start.1 = (bf16[1,1536,512]{2,1,0:T(8,128)(2,1)S(1)}, bf16[1,1536,512]{2,1,0:T(8,128)(2,1)}, u32[]{:S(2)}) copy-start(bf16[1,1536,512]{2,1,0:T(8,128)(2,1)} %wg_ref.3) | copy-start | bytes 4718596
  102.7 46.4 %all-to-all-start.2 = ((bf16[32,16,1536]{2,1,0:T(8,128)(2,1)}), bf16[32,16,1536]{2,1,0:T(8,128)(2,1)S(1)}, u32[]{:S(2)}, u32[]{:S(2)}) async-start(bf16[32,16,1536]{2,1,0:T(8,128)(2,1)} %get-tuple-element.34), calls=%async_computation.2 | async-start | bytes 3145728 | tf_op jit(solution)/shard_map/all_to_all | solution.py:194
  113.7 14.4 %collective-permute-start = (bf16[16,1536]{1,0:T(8,128)(2,1)S(1)}, bf16[16,1536]{1,0:T(8,128)(2,1)S(1)}, u32[]{:S(2)}, u32[]{:S(2)}) collective-permute-start(bf16[16,1536]{1,0:T(8,128)(2,1)S(1)} %copy-done.24), channel_id=1, source_target_pairs={{0,1},{1,2},{2,3},{3,4},{4,5},{5,6},{6,7},{7,0},{8,9},{9,10},{10,1... | collective-permute-start | bytes 147464 | tf_op jit(solution)/shard_map/ppermute | solution.py:192
  115.2 15.5 %collective-permute-start.1 = (bf16[16,1536]{1,0:T(8,128)(2,1)S(1)}, bf16[16,1536]{1,0:T(8,128)(2,1)S(1)}, u32[]{:S(2)}, u32[]{:S(2)}) collective-permute-start(bf16[16,1536]{1,0:T(8,128)(2,1)S(1)} %copy-done.23), channel_id=1, source_target_pairs={{0,2},{1,3},{2,4},{3,5},{4,6},{5,7},{6,0},{7,1},{8,10},{9,11},{10,... | collective-permute-start | bytes 147464 | tf_op jit(solution)/shard_map/ppermute | solution.py:192
  118.3 14.2 %collective-permute-start.2 = (bf16[16,1536]{1,0:T(8,128)(2,1)}, bf16[16,1536]{1,0:T(8,128)(2,1)S(1)}, u32[]{:S(2)}, u32[]{:S(2)}) collective-permute-start(bf16[16,1536]{1,0:T(8,128)(2,1)} %get-tuple-element.38), channel_id=1, source_target_pairs={{0,3},{1,4},{2,5},{3,6},{4,7},{5,0},{6,1},{7,2},{8,11},{9,12},{10,... | collective-permute-start | bytes 147464 | tf_op jit(solution)/shard_map/ppermute | solution.py:192
  121.9 12.4 %collective-permute-start.3 = (bf16[16,1536]{1,0:T(8,128)(2,1)}, bf16[16,1536]{1,0:T(8,128)(2,1)S(1)}, u32[]{:S(2)}, u32[]{:S(2)}) collective-permute-start(bf16[16,1536]{1,0:T(8,128)(2,1)} %get-tuple-element.39), channel_id=1, source_target_pairs={{0,4},{1,5},{2,6},{3,7},{4,0},{5,1},{6,2},{7,3},{8,12},{9,13},{10,... | collective-permute-start | bytes 147464 | tf_op jit(solution)/shard_map/ppermute | solution.py:192
  124.3 10.4 %collective-permute-start.4 = (bf16[16,1536]{1,0:T(8,128)(2,1)}, bf16[16,1536]{1,0:T(8,128)(2,1)S(1)}, u32[]{:S(2)}, u32[]{:S(2)}) collective-permute-start(bf16[16,1536]{1,0:T(8,128)(2,1)} %get-tuple-element.40), channel_id=1, source_target_pairs={{0,5},{1,6},{2,7},{3,0},{4,1},{5,2},{6,3},{7,4},{8,13},{9,14},{10,... | collective-permute-start | bytes 147464 | tf_op jit(solution)/shard_map/ppermute | solution.py:192
  128.2 6.5 %collective-permute-start.5 = (bf16[16,1536]{1,0:T(8,128)(2,1)}, bf16[16,1536]{1,0:T(8,128)(2,1)S(1)}, u32[]{:S(2)}, u32[]{:S(2)}) collective-permute-start(bf16[16,1536]{1,0:T(8,128)(2,1)} %get-tuple-element.41), channel_id=1, source_target_pairs={{0,6},{1,7},{2,0},{3,1},{4,2},{5,3},{6,4},{7,5},{8,14},{9,15},{10,... | collective-permute-start | bytes 147464 | tf_op jit(solution)/shard_map/ppermute | solution.py:192
  130.7 5.3 %collective-permute-start.6 = (bf16[16,1536]{1,0:T(8,128)(2,1)S(1)}, bf16[16,1536]{1,0:T(8,128)(2,1)S(1)}, u32[]{:S(2)}, u32[]{:S(2)}) collective-permute-start(bf16[16,1536]{1,0:T(8,128)(2,1)S(1)} %copy-done.22), channel_id=1, source_target_pairs={{0,7},{1,0},{2,1},{3,2},{4,3},{5,4},{6,5},{7,6},{8,15},{9,8},{10,9... | collective-permute-start | bytes 147464 | tf_op jit(solution)/shard_map/ppermute | solution.py:192
  155.9 43.1 %all-to-all-start.3 = ((bf16[32,16,1536]{2,1,0:T(8,128)(2,1)}), bf16[32,16,1536]{2,1,0:T(8,128)(2,1)S(1)}, u32[]{:S(2)}, u32[]{:S(2)}) async-start(bf16[32,16,1536]{2,1,0:T(8,128)(2,1)} %near.1), calls=%async_computation.3 | async-start | bytes 3145728 | tf_op jit(solution)/shard_map/all_to_all | solution.py:215
  168.9 14.8 %collective-permute-start.8 = (bf16[16,1536]{1,0:T(8,128)(2,1)}, bf16[16,1536]{1,0:T(8,128)(2,1)S(1)}, u32[]{:S(2)}, u32[]{:S(2)}) collective-permute-start(bf16[16,1536]{1,0:T(8,128)(2,1)} %get-tuple-element.54), channel_id=1, source_target_pairs={{0,7},{1,0},{2,1},{3,2},{4,3},{5,4},{6,5},{7,6},{8,15},{9,8},{10,9... | collective-permute-start | bytes 147464 | tf_op jit(solution)/shard_map/ppermute | solution.py:192
  169.6 16.7 %collective-permute-start.9 = (bf16[16,1536]{1,0:T(8,128)(2,1)}, bf16[16,1536]{1,0:T(8,128)(2,1)S(1)}, u32[]{:S(2)}, u32[]{:S(2)}) collective-permute-start(bf16[16,1536]{1,0:T(8,128)(2,1)} %get-tuple-element.55), channel_id=1, source_target_pairs={{0,6},{1,7},{2,0},{3,1},{4,2},{5,3},{6,4},{7,5},{8,14},{9,15},{10,... | collective-permute-start | bytes 147464 | tf_op jit(solution)/shard_map/ppermute | solution.py:192
  173.9 25.2 %collective-permute-start.10 = (bf16[16,1536]{1,0:T(8,128)(2,1)}, bf16[16,1536]{1,0:T(8,128)(2,1)S(1)}, u32[]{:S(2)}, u32[]{:S(2)}) collective-permute-start(bf16[16,1536]{1,0:T(8,128)(2,1)} %get-tuple-element.56), channel_id=1, source_target_pairs={{0,5},{1,6},{2,7},{3,0},{4,1},{5,2},{6,3},{7,4},{8,13},{9,14},{10,... | collective-permute-start | bytes 147464 | tf_op jit(solution)/shard_map/ppermute | solution.py:192
  176.6 22.5 %collective-permute-start.11 = (bf16[16,1536]{1,0:T(8,128)(2,1)}, bf16[16,1536]{1,0:T(8,128)(2,1)S(1)}, u32[]{:S(2)}, u32[]{:S(2)}) collective-permute-start(bf16[16,1536]{1,0:T(8,128)(2,1)} %get-tuple-element.57), channel_id=1, source_target_pairs={{0,4},{1,5},{2,6},{3,7},{4,0},{5,1},{6,2},{7,3},{8,12},{9,13},{10,... | collective-permute-start | bytes 147464 | tf_op jit(solution)/shard_map/ppermute | solution.py:192
  180.9 18.2 %collective-permute-start.12 = (bf16[16,1536]{1,0:T(8,128)(2,1)}, bf16[16,1536]{1,0:T(8,128)(2,1)S(1)}, u32[]{:S(2)}, u32[]{:S(2)}) collective-permute-start(bf16[16,1536]{1,0:T(8,128)(2,1)} %get-tuple-element.58), channel_id=1, source_target_pairs={{0,3},{1,4},{2,5},{3,6},{4,7},{5,0},{6,1},{7,2},{8,11},{9,12},{10,... | collective-permute-start | bytes 147464 | tf_op jit(solution)/shard_map/ppermute | solution.py:192
  183.8 15.3 %collective-permute-start.13 = (bf16[16,1536]{1,0:T(8,128)(2,1)}, bf16[16,1536]{1,0:T(8,128)(2,1)S(1)}, u32[]{:S(2)}, u32[]{:S(2)}) collective-permute-start(bf16[16,1536]{1,0:T(8,128)(2,1)} %get-tuple-element.59), channel_id=1, source_target_pairs={{0,2},{1,3},{2,4},{3,5},{4,6},{5,7},{6,0},{7,1},{8,10},{9,11},{10,... | collective-permute-start | bytes 147464 | tf_op jit(solution)/shard_map/ppermute | solution.py:192
  186.3 12.8 %collective-permute-start.14 = (bf16[16,1536]{1,0:T(8,128)(2,1)}, bf16[16,1536]{1,0:T(8,128)(2,1)S(1)}, u32[]{:S(2)}, u32[]{:S(2)}) collective-permute-start(bf16[16,1536]{1,0:T(8,128)(2,1)} %get-tuple-element.60), channel_id=1, source_target_pairs={{0,1},{1,2},{2,3},{3,4},{4,5},{5,6},{6,7},{7,0},{8,9},{9,10},{10,1... | collective-permute-start | bytes 147464 | tf_op jit(solution)/shard_map/ppermute | solution.py:192
  (22 other events, 258.6 us)
Sparse Core Ops, SparseCore 0:
  26.8 73.9 all-gather.5
  102.8 61.8 all-gather.3
